TPU v7x, 32 devices: a whole 2x2x4 slice. The times are simulated.
32 devices in a mesh: dp: 8 (over y, x, core), shard: 4 (over z).
Axes of the slice: x: 2, y: 2, z: 4, core: 2. Of those that a mesh axis runs over, the one named last changes fastest.
Arguments:
- momentum: float32 [4096, 7168], P('dp', 'shard'), may hold values from -6 to 6
- gradient: bfloat16 [4096, 7168], P('dp', 'shard'), may hold values from -120 to 120
Outputs:
- new_momentum: float32 [4096, 7168], P('dp', 'shard')
- update: float32 [4096, 7168], P('dp', 'shard')
All inputs are finite; a program needn't handle non-finite values.
Results may differ from a plain program's by a relative error of at most 0.0038.
The roundings to bfloat16 on the way count: a program that leaves them out, or rounds other values in their place, can miss the bound.
Values may be sent and summed in bfloat16 or wider, within the bound.
No kernel may reach another device: no remote copies, remote signals or barrier semaphores. Data moves between devices by JAX's collectives and lax.ppermute only.
A program may use at most 64 MiB of HBM per device.

v0:
```python
import math

import jax
import jax.numpy as jnp
from jax import lax
from jax.sharding import PartitionSpec as P

D = 7168
STEPS = 2


momentum_decay = 0.95
linear_term = 3.4445
cubic_term = -4.775
quintic_term = 2.0315


def apply_panel(gram_panel, right_side):
    return jnp.dot(gram_panel, right_side, preferred_element_type=jnp.float32)


def body(momentum, gradient):
    grad_full = gradient.astype(jnp.float32)
    new_momentum = momentum_decay * momentum + grad_full
    current = grad_full + momentum_decay * new_momentum
    for iteration in range(STEPS):
        matrix = current.astype(jnp.bfloat16)
        column_panel = lax.all_gather(matrix, "dp", axis=0, tiled=True)
        summed_part = lax.psum_scatter(
            lax.dot_general(
                matrix, column_panel, (((1,), (1,)), ((), ())), preferred_element_type=jnp.float32
            ),
            "shard",
            scatter_dimension=0,
            tiled=True,
        )
        gram_part = summed_part.astype(jnp.bfloat16)
        gram_panel = lax.all_gather(gram_part, "shard", axis=0, tiled=True)
        square_sum = lax.psum(jnp.sum(jnp.square(gram_part.astype(jnp.float32))), ("dp", "shard"))
        inverse_norm = lax.rsqrt(square_sum)
        root_scale = jnp.sqrt(inverse_norm)
        matrix_full = matrix.astype(jnp.float32)
        first_product = apply_panel(gram_panel, column_panel)
        mixture = (
            cubic_term * root_scale * matrix_full
            + quintic_term * root_scale * inverse_norm * first_product
        ).astype(jnp.bfloat16)
        second_product = apply_panel(gram_panel, lax.all_gather(mixture, "dp", axis=0, tiled=True))
        current = linear_term * root_scale * matrix_full + inverse_norm * second_product
    update = math.sqrt(D) * current
    return (new_momentum, update)


def solution(mesh):
    in_specs = (P("dp", "shard"), P("dp", "shard"))
    out_specs = (P("dp", "shard"), P("dp", "shard"))
    return jax.shard_map(body, mesh=mesh, in_specs=in_specs, out_specs=out_specs, check_vma=False)
```

profile of v0, /device:TPU:0, one launch (start us, length us, event | category | flops | bytes accessed | tf_op | source)
XLA Modules:
  0.0 889.7 jit_solution(13144774973173821033)
XLA Ops:
  7.2 5.7 fusion
  12.9 0.0 reduce-scatter.3.cloned.1.call-start
  13.0 83.7 %all-gather.7.cloned.1.call-done = bf16[4096,1792]{1,0:T(8,128)(2,1)} async-done(((bf16[512,1792]{1,0:T(8,128)(2,1)}), bf16[4096,1792]{1,0:T(8,128)(2,1)}) %all-gather.7.cloned.1.call-update) | async-done | bytes 14680080 | tf_op jit(solution)/shard_map/all_gather | solution.py:28
  96.7 13.5 %fusion.9 = f32[512,4096]{1,0:T(8,128)} fusion(bf16[512,1792]{1,0:T(8,128)(2,1)} %get-tuple-element.6, bf16[4096,1792]{1,0:T(8,128)(2,1)} %all-gather.7.cloned.1.call-done), kind=kOutput, calls=%fused_computation.17 | convolution fusion | flops 7516192768 | bytes 24903680 | tf_op jit(solution)/shard_map/dot_general | solution.py:30
  110.3 144.7 %reduce-scatter.3.cloned.1.call-done = f32[128,4096]{1,0:T(8,128)} async-done(((f32[512,4096]{1,0:T(8,128)}), f32[128,4096]{1,0:T(8,128)}) %reduce-scatter.3.cloned.1.call-update) | async-done | bytes 2097168 | tf_op jit(solution)/shard_map/reduce_scatter | solution.py:29
  255.0 3.7 multiply_reduce_fusion.1
  258.7 0.0 all-gather.11.cloned.1.call-start
  258.7 46.6 %psum.14 = f32[]{:T(128)} all-reduce(f32[]{:T(128)} %get-tuple-element.4), channel_id=1, replica_groups=mesh['dp'=8,'shard'=4] {'dp','shard'}, use_global_device_ids=true, to_apply=%region_2.0 | all-reduce | flops 1 | bytes 8 | tf_op jit(solution)/shard_map/psum | solution.py:39
  306.1 35.1 %all-gather.9.cloned.1.call-done = bf16[512,4096]{1,0:T(8,128)(2,1)} async-done(((bf16[128,4096]{1,0:T(8,128)(2,1)}), bf16[512,4096]{1,0:T(8,128)(2,1)}) %all-gather.9.cloned.1.call-update) | async-done | bytes 4194320 | tf_op jit(solution)/shard_map/all_gather | solution.py:38
  341.2 14.2 %fusion.4 = bf16[512,1792]{1,0:T(8,128)(2,1)} fusion(bf16[512,1792]{1,0:T(8,128)(2,1)S(1)} %copy-done, bf16[512,4096]{1,0:T(8,128)(2,1)} %all-gather.9.cloned.1.call-done, bf16[4096,1792]{1,0:T(8,128)(2,1)} %all-gather.7.cloned.1.call-done, f32[]{:T(128)S(6)} %mul.94, f32[]{:T(128)S(6)} %mul.90), kind=kOutput, calls=%fused_computation.10 | convolution fusion | flops 7520780288 | bytes 22544392 | tf_op jit(solution)/shard_map/dot_general | solution.py:19
  355.4 0.0 all-gather.13.cloned.1.call-start
  355.4 79.4 %all-gather.11.cloned.1.call-done = bf16[4096,1792]{1,0:T(8,128)(2,1)} async-done(((bf16[512,1792]{1,0:T(8,128)(2,1)}), bf16[4096,1792]{1,0:T(8,128)(2,1)}) %all-gather.11.cloned.1.call-update) | async-done | bytes 14680080 | tf_op jit(solution)/shard_map/all_gather | solution.py:48
  434.9 14.2 %fusion.2 = bf16[512,1792]{1,0:T(8,128)(2,1)} fusion(bf16[512,1792]{1,0:T(8,128)(2,1)S(1)} %copy-done, bf16[512,4096]{1,0:T(8,128)(2,1)} %all-gather.9.cloned.1.call-done, bf16[4096,1792]{1,0:T(8,128)(2,1)} %all-gather.11.cloned.1.call-done, f32[]{:T(128)S(6)} %rsqrt.6, f32[]{:T(128)S(6)} %mul.86), kind=kOutput, calls=%fused_computation.8 | convolution fusion | flops 7520780288 | bytes 22544392 | tf_op jit(solution)/shard_map/dot_general | solution.py:19
  449.1 0.2 reduce-scatter.5.cloned.1.call-start
  449.3 80.8 %all-gather.13.cloned.1.call-done = bf16[4096,1792]{1,0:T(8,128)(2,1)} async-done(((bf16[512,1792]{1,0:T(8,128)(2,1)}), bf16[4096,1792]{1,0:T(8,128)(2,1)}) %all-gather.13.cloned.1.call-update) | async-done | bytes 14680080 | tf_op jit(solution)/shard_map/all_gather | solution.py:28
  530.1 13.5 %fusion.10 = f32[512,4096]{1,0:T(8,128)} fusion(bf16[512,1792]{1,0:T(8,128)(2,1)} %fusion.2, bf16[4096,1792]{1,0:T(8,128)(2,1)} %all-gather.13.cloned.1.call-done), kind=kOutput, calls=%fused_computation.18 | convolution fusion | flops 7516192768 | bytes 24903680 | tf_op jit(solution)/shard_map/dot_general | solution.py:30
  543.7 144.7 %reduce-scatter.5.cloned.1.call-done = f32[128,4096]{1,0:T(8,128)} async-done(((f32[512,4096]{1,0:T(8,128)}), f32[128,4096]{1,0:T(8,128)}) %reduce-scatter.5.cloned.1.call-update) | async-done | bytes 2097168 | tf_op jit(solution)/shard_map/reduce_scatter | solution.py:29
  688.5 3.7 multiply_reduce_fusion
  692.1 0.0 all-gather.17.cloned.1.call-start
  692.2 46.6 %psum.15 = f32[]{:T(128)} all-reduce(f32[]{:T(128)} %get-tuple-element.2), channel_id=1, replica_groups=mesh['dp'=8,'shard'=4] {'dp','shard'}, use_global_device_ids=true, to_apply=%region_5.0 | all-reduce | flops 1 | bytes 8 | tf_op jit(solution)/shard_map/psum | solution.py:39
  739.5 35.1 %all-gather.15.cloned.1.call-done = bf16[512,4096]{1,0:T(8,128)(2,1)} async-done(((bf16[128,4096]{1,0:T(8,128)(2,1)}), bf16[512,4096]{1,0:T(8,128)(2,1)}) %all-gather.15.cloned.1.call-update) | async-done | bytes 4194320 | tf_op jit(solution)/shard_map/all_gather | solution.py:38
  774.6 14.2 %fusion.8 = bf16[512,1792]{1,0:T(8,128)(2,1)} fusion(bf16[512,1792]{1,0:T(8,128)(2,1)S(1)} %copy-done.1, bf16[512,4096]{1,0:T(8,128)(2,1)} %all-gather.15.cloned.1.call-done, bf16[4096,1792]{1,0:T(8,128)(2,1)} %all-gather.13.cloned.1.call-done, f32[]{:T(128)S(6)} %mul.106, f32[]{:T(128)S(6)} %mul.102), kind=kOutput, calls=%fused_computation.14 | convolution fusion | flops 7520780288 | bytes 22544392 | tf_op jit(solution)/shard_map/dot_general | solution.py:19
  788.8 79.5 %all-gather.17.cloned.1.call-done = bf16[4096,1792]{1,0:T(8,128)(2,1)} async-done(((bf16[512,1792]{1,0:T(8,128)(2,1)}), bf16[4096,1792]{1,0:T(8,128)(2,1)}) %all-gather.17.cloned.1.call-update) | async-done | bytes 14680080 | tf_op jit(solution)/shard_map/all_gather | solution.py:48
  868.3 14.5 %fusion.6 = f32[512,1792]{1,0:T(8,128)} fusion(bf16[512,1792]{1,0:T(8,128)(2,1)S(1)} %copy-done.1, bf16[512,4096]{1,0:T(8,128)(2,1)} %all-gather.15.cloned.1.call-done, bf16[4096,1792]{1,0:T(8,128)(2,1)} %all-gather.17.cloned.1.call-done, f32[]{:T(128)S(6)} %rsqrt.7, f32[]{:T(128)S(6)} %mul.98), kind=kOutput, calls=%fused_computation.12 | convolution fusion | flops 7520780288 | bytes 24379400 | tf_op jit(solution)/shard_map/dot_general | solution.py:19
  (15 shorter events, 0.3 us)
Async XLA Ops:
  7.2 89.5 %all-gather.7.cloned.1.call-start = ((), (), s32[]{:S(2)}) async-start(), calls=%async_computation.2 | async-start | bytes 16515072 | tf_op jit(solution)/shard_map/all_gather | solution.py:28
  12.9 242.1 %reduce-scatter.3.cloned.1.call-start = ((), (), s32[]{:S(2)}) async-start(), calls=%async_computation.3 | async-start | bytes 10485760 | tf_op jit(solution)/shard_map/reduce_scatter | solution.py:29
  110.2 230.9 %copy-start = (bf16[512,1792]{1,0:T(8,128)(2,1)S(1)}, bf16[512,1792]{1,0:T(8,128)(2,1)}, u32[]{:S(2)}) copy-start(bf16[512,1792]{1,0:T(8,128)(2,1)} %get-tuple-element.6) | copy-start | bytes 5505028
  110.2 230.9 %all-gather.9.cloned.1.call-start = ((), (), s32[]{:S(2)}) async-start(), calls=%async_computation.4 | async-start | bytes 5242880 | tf_op jit(solution)/shard_map/all_gather | solution.py:38
  258.7 176.2 %all-gather.11.cloned.1.call-start = ((), (), s32[]{:S(2)}) async-start(), calls=%async_computation.5 | async-start | bytes 16515072 | tf_op jit(solution)/shard_map/all_gather | solution.py:48
  355.4 174.7 %all-gather.13.cloned.1.call-start = ((), (), s32[]{:S(2)}) async-start(), calls=%async_computation.6 | async-start | bytes 16515072 | tf_op jit(solution)/shard_map/all_gather | solution.py:28
  449.1 239.3 %reduce-scatter.5.cloned.1.call-start = ((), (), s32[]{:S(2)}) async-start(), calls=%async_computation.7 | async-start | bytes 10485760 | tf_op jit(solution)/shard_map/reduce_scatter | solution.py:29
  543.7 230.9 %copy-start.1 = (bf16[512,1792]{1,0:T(8,128)(2,1)S(1)}, bf16[512,1792]{1,0:T(8,128)(2,1)}, u32[]{:S(2)}) copy-start(bf16[512,1792]{1,0:T(8,128)(2,1)} %fusion.2) | copy-start | bytes 5505028
  543.7 230.9 %all-gather.15.cloned.1.call-start = ((), (), s32[]{:S(2)}) async-start(), calls=%async_computation.8 | async-start | bytes 5242880 | tf_op jit(solution)/shard_map/all_gather | solution.py:38
  692.1 176.2 %all-gather.17.cloned.1.call-start = ((), (), s32[]{:S(2)}) async-start(), calls=%async_computation.9 | async-start | bytes 16515072 | tf_op jit(solution)/shard_map/all_gather | solution.py:48
Sparse Core Ops, SparseCore 0:
  13.0 83.5 all-gather.6
  110.3 144.6 reduce-scatter.2
  258.8 82.2 all-gather.8
  355.5 79.3 all-gather.10
  449.2 80.8 all-gather.12
  543.8 144.6 reduce-scatter.4
  692.3 82.2 all-gather.14
  789.0 79.3 all-gather.16
where the time goes:
time: 890 us
  waiting for transfers between devices  683 us (77%)
  blocking collectives  93.2 us (10%)
  matrix products  84.2 us (9%)
  between operations  15.6 us (2%)
  other arithmetic  13 us (1%)
    reduce_scatter x2, waiting for transfers between devices, body(): lax.psum_scatter(lax.dot_general(matrix, column_panel, (((1,), (1,)), (()...  289 us
    all_gather x2, waiting for transfers between devices, body(): column_panel = lax.all_gather(matrix, 'dp', axis=0, tiled=True)  164 us
    all_gather x2, waiting for transfers between devices, body(): lax.all_gather(mixture, 'dp', axis=0, tiled=True)  159 us
    psum x2, blocking collectives, body(): lax.psum(jnp.sum(jnp.square(gram_part.astype(jnp.float32))), ('dp', 'shar...  93.2 us
    all_gather x2, waiting for transfers between devices, body(): gram_panel = lax.all_gather(gram_part, 'shard', axis=0, tiled=True)  70.1 us
    dot_general x4, matrix products, apply_panel(): return jnp.dot(gram_panel, right_side, preferred_element_type=jnp.float32)  57.1 us
    dot_general x2, matrix products, body(): lax.dot_general(matrix, column_panel, (((1,), (1,)), ((), ())), preferred...  27.1 us
  transfers between devices with their start and end apart: 8, of which 8 were waited for; matrix products, arithmetic and copies ran while one was open for 0% of the time, Pallas kernels for 0%

commit v1 on v0

v1 whole, which is shorter than its diff:
```python
import functools
import math

import jax
import jax.numpy as jnp
from jax import lax
from jax.experimental import pallas as pl
from jax.experimental.pallas import tpu as pltpu
from jax.sharding import PartitionSpec as P


STEPS = 2


momentum_decay = 0.95
linear_term = 3.4445
cubic_term = -4.775
quintic_term = 2.0315

f32, bf16 = jnp.float32, jnp.bfloat16


def dot_nn(a, b):
    return lax.dot_general(a, b, (((1,), (0,)), ((), ())), preferred_element_type=f32)


def dot_nt(a, b):
    return lax.dot_general(a, b, (((1,), (1,)), ((), ())), preferred_element_type=f32)


def iterate_general(current):
    matrix = current.astype(bf16)
    column_panel = lax.all_gather(matrix, "dp", axis=0, tiled=True)
    summed_part = lax.psum_scatter(dot_nt(matrix, column_panel), "shard", scatter_dimension=0, tiled=True)
    gram_part = summed_part.astype(bf16)
    gram_panel = lax.all_gather(gram_part, "shard", axis=0, tiled=True)
    square_sum = lax.psum(jnp.sum(jnp.square(gram_part.astype(f32))), ("dp", "shard"))
    inverse_norm = lax.rsqrt(square_sum)
    root_scale = jnp.sqrt(inverse_norm)
    matrix_full = matrix.astype(f32)
    first = dot_nn(gram_panel, column_panel)
    mixture = (
        cubic_term * root_scale * matrix_full + quintic_term * root_scale * inverse_norm * first
    ).astype(bf16)
    second = dot_nn(gram_panel, lax.all_gather(mixture, "dp", axis=0, tiled=True))
    return linear_term * root_scale * matrix_full + inverse_norm * second


def x_bit(i):
    return (i >> 1) & 1


def y_bit(i):
    return (i >> 2) & 1


def x_pick(i):
    return i ^ 2 ^ x_bit(i)


def y_pick(i):
    return i ^ 4 ^ (x_bit(i) ^ y_bit(i))


ROW_DEVICES = 8
VMEM_LIMIT = 20 << 20
CORE = [(i, i ^ 1) for i in range(ROW_DEVICES)]
TAKE_X = [(x_pick(i), i) for i in range(ROW_DEVICES)]
TAKE_Y = [(y_pick(i), i) for i in range(ROW_DEVICES)]
GIVE_X = [(i, x_pick(i)) for i in range(ROW_DEVICES)]
GIVE_Y = [(i, y_pick(i)) for i in range(ROW_DEVICES)]


def over_dp(value, pairs):
    return lax.ppermute(value, "dp", pairs)


def call(kernel, outs, args, specs, out_specs, grid, scratch=(), flops=0, prefetch=0):
    moved = sum(a.size * a.dtype.itemsize for a in args) + sum(o.size * o.dtype.itemsize for o in outs)
    return pl.pallas_call(
        kernel,
        out_shape=outs,
        grid_spec=pltpu.PrefetchScalarGridSpec(
            num_scalar_prefetch=prefetch,
            grid=grid,
            in_specs=specs,
            out_specs=out_specs,
            scratch_shapes=list(scratch),
        ),
        compiler_params=pltpu.CompilerParams(vmem_limit_bytes=VMEM_LIMIT),
        cost_estimate=pl.CostEstimate(flops=flops, bytes_accessed=moved, transcendentals=0),
    )(*args)


def whole_spec(a):
    return pl.BlockSpec(a.shape, lambda *_: (0,) * len(a.shape), pipeline_mode=pl.Buffered(1))


def gram_kernel(pairs, count, size, z_ref, *refs):
    halves, (kept, *pieces), total = refs[:count], refs[count:-1], refs[-1]
    z = z_ref[0]
    rows = kept.shape[1]
    for p, (left, right) in enumerate(pairs):
        value = jnp.concatenate([halves[2 * left][...], halves[2 * left + 1][...]], axis=0)
        half = value.shape[0] // 2
        for h in range(2):
            total[p, :, h * half : (h + 1) * half] = dot_nt(value, halves[2 * right + h][...])
    for by in range(size):
        at = pl.multiple_of(lax.rem(z + by, size) * rows, rows)
        piece = total[:, pl.ds(at, rows), :]
        if by:
            pieces[by - 1][...] = piece.astype(bf16)
        else:
            kept[...] = piece


def gram(z, size, blocks, pairs):
    halves = [half for block in blocks for half in block]
    rows, columns = 2 * halves[0].shape[0], halves[0].shape[1]
    shape = (len(pairs), rows // size, rows)
    outs = [jax.ShapeDtypeStruct(shape, f32)] + [jax.ShapeDtypeStruct(shape, bf16)] * (size - 1)
    return call(
        functools.partial(gram_kernel, pairs, len(halves), size),
        outs,
        [z] + halves,
        [whole_spec(h) for h in halves],
        [pl.BlockSpec(shape, lambda *_: (0, 0, 0), pipeline_mode=pl.Buffered(1))] * size,
        (1,),
        [pltpu.VMEM((len(pairs), rows, rows), f32)],
        2 * len(pairs) * rows * rows * columns,
        1,
    )


def assemble_kernel(takes, size, z_ref, *refs):
    groups, outs = refs[: len(refs) - len(takes)], refs[len(refs) - len(takes) :]
    z = z_ref[0]
    rows = groups[0].shape[1]
    columns = groups[0].shape[2]
    for out, taken in zip(outs, takes):
        for k, (group, index, transposed) in enumerate(taken):
            for by in range(size):
                part = groups[group * size + by][index]
                at = pl.multiple_of(lax.rem(z + size - by, size) * rows, rows)
                if transposed:
                    out[:, pl.ds(pl.multiple_of(k * columns + at, rows), rows)] = part.T
                else:
                    out[pl.ds(at, rows), k * columns : (k + 1) * columns] = part


def assemble(z, size, groups, takes):
    parts = [part for group in groups for part in group]
    columns = parts[0].shape[2]
    outs = [jax.ShapeDtypeStruct((columns, columns * len(taken)), bf16) for taken in takes]
    return call(
        functools.partial(assemble_kernel, takes, size),
        outs,
        [z] + parts,
        [whole_spec(p) for p in parts],
        [pl.BlockSpec(o.shape, lambda *_: (0, 0), pipeline_mode=pl.Buffered(1)) for o in outs],
        (1,),
        prefetch=1,
    )


def product_kernel(n_grams, n_halves, has_sum, finish, *refs):
    refs = list(refs)
    scale_ref = refs.pop(0) if finish else None
    grams, refs = refs[:n_grams], refs[n_grams:]
    halves, refs = refs[:n_halves], refs[n_halves:]
    gram = jnp.concatenate([g[...] for g in grams], axis=1)
    value = dot_nn(gram, jnp.concatenate([h[...] for h in halves], axis=0))
    if has_sum:
        value = value + refs.pop(0)[...]
    if finish:
        own = jnp.concatenate([refs[0][...], refs[1][...]], axis=0)
        value = scale_ref[0] * own.astype(f32) + scale_ref[1] * value
        refs = refs[2:]
    rows = value.shape[0] // len(refs)
    for k, out in enumerate(refs):
        out[...] = value[k * rows : (k + 1) * rows].astype(out.dtype)


def product(grams, blocks, summed=None, finish=None, dtype=f32, parts=1):
    halves = [half for block in blocks for half in block]
    half, columns = halves[0].shape
    tile = 256 if columns % 256 == 0 else columns
    half_spec = pl.BlockSpec((half, tile), lambda t, *_: (0, t))
    row_spec = pl.BlockSpec((2 * half, tile), lambda t, *_: (0, t))
    args = ([finish[0]] if finish else []) + list(grams) + halves
    specs = [whole_spec(g) for g in grams] + [half_spec] * len(halves)
    if summed is not None:
        args, specs = args + [summed], specs + [row_spec]
    if finish:
        args, specs = args + list(finish[1]), specs + [half_spec] * 2
    return call(
        functools.partial(product_kernel, len(grams), len(halves), summed is not None, finish is not None),
        [jax.ShapeDtypeStruct((2 * half // parts, columns), dtype)] * parts,
        args,
        specs,
        [half_spec if parts == 2 else row_spec] * parts,
        (columns // tile,),
        flops=4 * half * half * columns * len(halves),
        prefetch=1 if finish else 0,
    )


def shifted(value, by, size):
    return lax.ppermute(value, "shard", [(z, (z + by) % size) for z in range(size)])


def total_of(value, size):
    value = jnp.broadcast_to(value, (8, 128))
    value = sum([shifted(value, by, size) for by in range(1, size)], value)
    for step in (1, 2, 4):
        value = value + over_dp(value, [(i, i ^ step) for i in range(ROW_DEVICES)])
    return value[0, 0]


def square_of(part):
    return jnp.sum(jnp.square(part.astype(f32)))


def gather(block):
    top, bottom = block
    x_bottom, y_top = over_dp(bottom, TAKE_X), over_dp(top, TAKE_Y)
    x_top, y_bottom = over_dp(top, TAKE_X), over_dp(bottom, TAKE_Y)
    core = over_dp(top, CORE), over_dp(bottom, CORE)
    d_oth_bottom, d_sel_top = over_dp(x_bottom, GIVE_Y), over_dp(y_top, GIVE_X)
    x_oth = over_dp(x_top, CORE), over_dp(x_bottom, CORE)
    y_oth = over_dp(y_top, CORE), over_dp(y_bottom, CORE)
    d_oth_top, d_sel_bottom = over_dp(d_sel_top, CORE), over_dp(d_oth_bottom, CORE)
    near = core, (x_top, x_bottom), (y_top, y_bottom)
    return near, (x_oth, y_oth, (d_sel_top, d_sel_bottom), (d_oth_top, d_oth_bottom))


def reduce_parts(pieces, size):
    kept, *sent = pieces
    total = kept
    for by, piece in enumerate(sent, 1):
        total = total + shifted(piece, by, size).astype(f32)
    return total.astype(bf16)


def spread(part, size):
    return [part] + [shifted(part, by, size) for by in range(1, size)]


def iterate_square(matrix, size, gain, dtype, parts):
    z = lax.axis_index("shard").reshape(1)
    (core, x_sel, y_sel), (x_oth, y_oth, d_sel, d_oth) = gather(matrix)
    own_pieces = gram(z, size, [matrix, core], [(0, 0), (0, 1)])
    own_part = reduce_parts(own_pieces, size)
    own_parts = spread(own_part, size)
    far_pieces = gram(z, size, [matrix, x_sel, y_sel], [(0, 1), (1, 2), (0, 2)])
    far_part = reduce_parts(far_pieces, size)
    square_sum = total_of(square_of(own_part) + 2.0 * square_of(far_part), size)
    far_parts = spread(far_part, size)
    x_parts = [over_dp(p[:2], GIVE_X) for p in far_parts]
    y_parts = [over_dp(p[1:], GIVE_Y) for p in far_parts]
    (own,) = assemble(z, size, [own_parts], [[(0, 0, False), (0, 1, False)]])
    (far,) = assemble(z, size, [far_parts], [[(0, 0, False), (0, 2, False)]])
    side, diagonal = assemble(
        z,
        size,
        [x_parts, y_parts],
        [[(0, 0, True), (1, 1, True)], [(0, 1, False), (1, 0, True)]],
    )
    inverse_norm = lax.rsqrt(square_sum)
    root_scale = jnp.sqrt(inverse_norm)
    (first,) = product([own], [matrix, core])
    (first,) = product([far], [x_sel, y_sel], first)
    scales = jnp.stack([cubic_term * root_scale, quintic_term * root_scale * inverse_norm])
    mixture = product(
        [side, diagonal], [x_oth, y_oth, d_sel, d_oth], first, (scales, matrix), bf16, 2
    )
    (core, x_sel, y_sel), (x_oth, y_oth, d_sel, d_oth) = gather(mixture)
    (second,) = product([own], [mixture, core])
    (second,) = product([far, side], [x_sel, y_sel, x_oth, y_oth], second)
    scales = gain * jnp.stack([linear_term * root_scale, inverse_norm])
    return product([diagonal], [d_sel, d_oth], second, (scales, matrix), dtype, parts)


def current_of(momentum, gradient):
    grad_full = gradient.astype(f32)
    new_momentum = momentum_decay * momentum + grad_full
    return new_momentum, grad_full + momentum_decay * new_momentum


def body_square(size, columns, momentum, gradient):
    half = momentum.shape[0] // 2
    block = [
        current_of(momentum[rows], gradient[rows])[1].astype(bf16)
        for rows in (slice(0, half), slice(half, None))
    ]
    new_momentum, _ = current_of(*lax.optimization_barrier((momentum, gradient)))
    for iteration in range(STEPS):
        last = iteration == STEPS - 1
        block = iterate_square(
            block, size, math.sqrt(columns) if last else 1.0, f32 if last else bf16, 1 if last else 2
        )
    return (new_momentum, block[0])


def body_general(columns, momentum, gradient):
    grad_full = gradient.astype(f32)
    new_momentum = momentum_decay * momentum + grad_full
    current = grad_full + momentum_decay * new_momentum
    for _ in range(STEPS):
        current = iterate_general(current)
    return (new_momentum, math.sqrt(columns) * current)


def solution(mesh):
    row_devices, column_devices = mesh.shape["dp"], mesh.shape["shard"]
    spec = P("dp", "shard")

    def sharded(body):
        return jax.shard_map(body, mesh=mesh, in_specs=(spec, spec), out_specs=(spec, spec), check_vma=False)

    def general(momentum, gradient):
        return sharded(functools.partial(body_general, momentum.shape[1]))(momentum, gradient)

    def square(momentum, gradient):
        return sharded(functools.partial(body_square, column_devices, momentum.shape[1]))(momentum, gradient)

    if row_devices != ROW_DEVICES or column_devices & (column_devices - 1):
        return general
    return square
```

time: 890 us -> 631 us (0.71); the launches traced: 890 us -> 621 us
  waiting for transfers between devices: 683 us -> 310 us
  starting transfers between devices: 0.51 us -> 147 us
  Pallas kernels: 0 us -> 95.2 us
  blocking collectives: 93.2 us -> 0 us
  matrix products: 84.2 us -> 0 us
  local copies, waits for them, and re-layouts: 0.01 us -> 53.5 us
  between operations: 15.6 us -> 5.92 us
    all_gather x6 -> x0, waiting for transfers between devices: 394 us -> none  [the longest x2 164 us: body(): column_panel = lax.all_gather(matrix, 'dp', axis=0, tiled=True)]
    ppermute x0 -> x108, waiting for transfers between devices: none -> 310 us  [the longest x78 207 us: over_dp(): return lax.ppermute(value, 'dp', pairs)]
    reduce_scatter x2 -> x0, waiting for transfers between devices: 289 us -> none  [body(): lax.psum_scatter(lax.dot_general(matrix, column_panel, (((1,), (1,)), (()...]
    ppermute x0 -> x108, starting transfers between devices: none -> 147 us  [the longest x30 101 us: shifted(): lax.ppermute(value, 'shard', [(z, (z + by) % size) for z in range(size)])]
    pallas_call x0 -> x22, Pallas kernels: none -> 95.2 us  [call(): pl.pallas_call(kernel, out_shape=outs, grid_spec=pltpu.PrefetchScalarGrid...]
    psum x2 -> x0, blocking collectives: 93.2 us -> none  [body(): lax.psum(jnp.sum(jnp.square(gram_part.astype(jnp.float32))), ('dp', 'shar...]
    dot_general x6 -> x0, matrix products: 84.2 us -> none  [the longest x4 57.1 us: apply_panel(): return jnp.dot(gram_panel, right_side, preferred_element_type=jnp.float32)]
    unnamed x4 -> x222, local copies, waits for them, and re-layouts: 0.01 us -> 52.2 us
  transfers between devices with their start and end apart: 8 -> 108, of which waited for: 8 -> 39; matrix products, arithmetic and copies ran while one was open for 0% -> 1% of each run, Pallas kernels for 0% -> 10%
where the time goes in v1:
time: 631 us; the launch traced here: 621 us
  waiting for transfers between devices  310 us (49%)
  starting transfers between devices  147 us (23%)
  Pallas kernels  95.2 us (15%)
  local copies, waits for them, and re-layouts  53.5 us (8%)
  other arithmetic  9.16 us (1%)
    ppermute x78, waiting for transfers between devices, over_dp(): return lax.ppermute(value, 'dp', pairs)  207 us
    ppermute x30, waiting for transfers between devices, shifted(): lax.ppermute(value, 'shard', [(z, (z + by) % size) for z in range(size)])  104 us
    ppermute x30, starting transfers between devices, shifted(): lax.ppermute(value, 'shard', [(z, (z + by) % size) for z in range(size)])  101 us
    pallas_call x22, Pallas kernels, call(): pl.pallas_call(kernel, out_shape=outs, grid_spec=pltpu.PrefetchScalarGrid...  95.2 us
    unnamed x222, local copies, waits for them, and re-layouts  52.2 us
    ppermute x78, starting transfers between devices, over_dp(): return lax.ppermute(value, 'dp', pairs)  45.9 us
  transfers between devices with their start and end apart: 108, of which 39 were waited for; matrix products, arithmetic and copies ran while one was open for 1% of the time, Pallas kernels for 10%

profile of v1, /device:TPU:0, one launch (start us, length us, event | category | flops | bytes accessed | tf_op | source)
XLA Modules:
  0.0 621.1 jit_solution(17774002629906080504)
XLA Ops:
  16.4 12.4 %collective-permute-done.6.refs_3_.refs_2_ = bf16[256,1792]{1,0:T(8,128)(2,1)} collective-permute-done((bf16[256,1792]{1,0:T(8,128)(2,1)S(1)}, bf16[256,1792]{1,0:T(8,128)(2,1)}, u32[]{:S(2)}, u32[]{:S(2)}) %collective-permute-start.6) | collective-permute-done | bytes 917536 | tf_op jit(solution)/shard_map/ppermute | solution.py:75
  33.9 13.8 %collective-permute-done.5.refs_2_.refs_1_ = bf16[256,1792]{1,0:T(8,128)(2,1)} collective-permute-done((bf16[256,1792]{1,0:T(8,128)(2,1)S(1)}, bf16[256,1792]{1,0:T(8,128)(2,1)}, u32[]{:S(2)}, u32[]{:S(2)}) %collective-permute-start.5) | collective-permute-done | bytes 917536 | tf_op jit(solution)/shard_map/ppermute | solution.py:75
  60.0 17.0 %collective-permute-done.10 = bf16[3,128,512]{2,1,0:T(8,128)(2,1)S(1)} collective-permute-done((bf16[3,128,512]{2,1,0:T(8,128)(2,1)S(1)}, bf16[3,128,512]{2,1,0:T(8,128)(2,1)S(1)}, u32[]{:S(2)}, u32[]{:S(2)}) %collective-permute-start.10) | collective-permute-done | bytes 393248 | tf_op jit(solution)/shard_map/ppermute | solution.py:209
  115.6 9.9 %collective-permute-done.38.refs_2_ = bf16[2,128,512]{2,1,0:T(8,128)(2,1)S(1)} collective-permute-done((bf16[2,128,512]{2,1,0:T(8,128)(2,1)S(1)}, bf16[2,128,512]{2,1,0:T(8,128)(2,1)S(1)}, u32[]{:S(2)}, u32[]{:S(2)}) %collective-permute-start.38) | collective-permute-done | bytes 262176 | tf_op jit(solution)/shard_map/ppermute | solution.py:209
  128.3 11.3 %collective-permute-start.21 = (bf16[3,128,512]{2,1,0:T(8,128)(2,1)S(1)}, bf16[3,128,512]{2,1,0:T(8,128)(2,1)S(1)}, u32[]{:S(2)}, u32[]{:S(2)}) collective-permute-start(bf16[3,128,512]{2,1,0:T(8,128)(2,1)S(1)} %get-tuple-element.63.refs_0_), channel_id=1, source_target_pairs={{0,2},{1,3},{2,0},{3,1},{4,6},{5,7},{6,4},{7,5},{8,10},{9,11},{10,... | collective-permute-start | bytes 1179656 | tf_op jit(solution)/shard_map/ppermute | solution.py:209
  143.1 14.9 %collective-permute-done.21.refs_2_ = bf16[3,128,512]{2,1,0:T(8,128)(2,1)S(1)} collective-permute-done((bf16[3,128,512]{2,1,0:T(8,128)(2,1)S(1)}, bf16[3,128,512]{2,1,0:T(8,128)(2,1)S(1)}, u32[]{:S(2)}, u32[]{:S(2)}) %collective-permute-start.21) | collective-permute-done | bytes 393248 | tf_op jit(solution)/shard_map/ppermute | solution.py:209
  208.8 8.5 %shard_map.48 = (bf16[256,1792]{1,0:T(8,128)(2,1)S(1)}, bf16[256,1792]{1,0:T(8,128)(2,1)S(1)}) custom-call(f32[2]{0:T(128)S(1)} %pad_maximum_fusion.1.refs_0_, bf16[512,1024]{1,0:T(8,128)(2,1)S(1)} %get-tuple-element.41.refs_1_, bf16[512,1024]{1,0:T(8,128)(2,1)S(1)} %get-tuple-element.40.refs_2_.refs_1_, bf16[256,1792]{1,0:T(8,128)(2,1)} %collective-permute-done.29.refs_3_, ...), custom_call_target="tpu_custom_call" | custom-call | flops 3758096384 | bytes 16777224 | tf_op jit(solution)/shard_map/pallas_call | solution.py:80
  224.3 16.6 %collective-permute-done.46.refs_2_ = bf16[256,1792]{1,0:T(8,128)(2,1)S(1)} collective-permute-done((bf16[256,1792]{1,0:T(8,128)(2,1)S(1)}, bf16[256,1792]{1,0:T(8,128)(2,1)S(1)}, u32[]{:S(2)}, u32[]{:S(2)}) %collective-permute-start.46) | collective-permute-done | bytes 917536 | tf_op jit(solution)/shard_map/ppermute | solution.py:75
  241.8 18.1 %collective-permute-done.42.refs_3_ = bf16[256,1792]{1,0:T(8,128)(2,1)} collective-permute-done((bf16[256,1792]{1,0:T(8,128)(2,1)S(1)}, bf16[256,1792]{1,0:T(8,128)(2,1)}, u32[]{:S(2)}, u32[]{:S(2)}) %collective-permute-start.42) | collective-permute-done | bytes 917536 | tf_op jit(solution)/shard_map/ppermute | solution.py:75
  264.2 18.2 %collective-permute-done.43.refs_5_ = bf16[256,1792]{1,0:T(8,128)(2,1)} collective-permute-done((bf16[256,1792]{1,0:T(8,128)(2,1)}, bf16[256,1792]{1,0:T(8,128)(2,1)}, u32[]{:S(2)}, u32[]{:S(2)}) %collective-permute-start.43) | collective-permute-done | bytes 917536 | tf_op jit(solution)/shard_map/ppermute | solution.py:75
  314.2 9.0 %collective-permute-start.56 = (bf16[2,128,512]{2,1,0:T(8,128)(2,1)S(1)}, bf16[2,128,512]{2,1,0:T(8,128)(2,1)S(1)}, u32[]{:S(2)}, u32[]{:S(2)}) collective-permute-start(bf16[2,128,512]{2,1,0:T(8,128)(2,1)S(1)} %get-tuple-element.47), channel_id=1, source_target_pairs={{0,1},{1,2},{2,3},{3,0},{4,5},{5,6},{6,7},{7,4},{8,9},{9,10},{10,1... | collective-permute-start | bytes 786440 | tf_op jit(solution)/shard_map/ppermute | solution.py:209
  323.3 8.4 %collective-permute-done.59.refs_2_.refs_1_ = bf16[256,1792]{1,0:T(8,128)(2,1)S(1)} collective-permute-done((bf16[256,1792]{1,0:T(8,128)(2,1)S(1)}, bf16[256,1792]{1,0:T(8,128)(2,1)S(1)}, u32[]{:S(2)}, u32[]{:S(2)}) %collective-permute-start.59) | collective-permute-done | bytes 917536 | tf_op jit(solution)/shard_map/ppermute | solution.py:75
  332.3 18.6 %collective-permute-done.60.refs_3_.refs_2_ = bf16[256,1792]{1,0:T(8,128)(2,1)} collective-permute-done((bf16[256,1792]{1,0:T(8,128)(2,1)S(1)}, bf16[256,1792]{1,0:T(8,128)(2,1)}, u32[]{:S(2)}, u32[]{:S(2)}) %collective-permute-start.60) | collective-permute-done | bytes 917536 | tf_op jit(solution)/shard_map/ppermute | solution.py:75
  350.9 11.8 %collective-permute-start.58 = (bf16[2,128,512]{2,1,0:T(8,128)(2,1)S(1)}, bf16[2,128,512]{2,1,0:T(8,128)(2,1)S(1)}, u32[]{:S(2)}, u32[]{:S(2)}) collective-permute-start(bf16[2,128,512]{2,1,0:T(8,128)(2,1)S(1)} %get-tuple-element.49), channel_id=1, source_target_pairs={{0,3},{1,0},{2,1},{3,2},{4,7},{5,4},{6,5},{7,6},{8,11},{9,8},{10,9... | collective-permute-start | bytes 786440 | tf_op jit(solution)/shard_map/ppermute | solution.py:209
  372.5 9.3 %collective-permute-done.63 = bf16[3,128,512]{2,1,0:T(8,128)(2,1)S(1)} collective-permute-done((bf16[3,128,512]{2,1,0:T(8,128)(2,1)S(1)}, bf16[3,128,512]{2,1,0:T(8,128)(2,1)S(1)}, u32[]{:S(2)}, u32[]{:S(2)}) %collective-permute-start.63) | collective-permute-done | bytes 393248 | tf_op jit(solution)/shard_map/ppermute | solution.py:209
  381.7 15.2 %collective-permute-done.64 = bf16[3,128,512]{2,1,0:T(8,128)(2,1)S(1)} collective-permute-done((bf16[3,128,512]{2,1,0:T(8,128)(2,1)S(1)}, bf16[3,128,512]{2,1,0:T(8,128)(2,1)S(1)}, u32[]{:S(2)}, u32[]{:S(2)}) %collective-permute-start.64) | collective-permute-done | bytes 393248 | tf_op jit(solution)/shard_map/ppermute | solution.py:209
  399.3 8.1 %collective-permute-start.66 = (f32[8,128]{1,0:T(8,128)S(1)}, f32[8,128]{1,0:T(8,128)S(1)}, u32[]{:S(2)}, u32[]{:S(2)}) collective-permute-start(f32[8,128]{1,0:T(8,128)S(1)} %broadcast_in_dim.7), channel_id=1, source_target_pairs={{0,1},{1,2},{2,3},{3,0},{4,5},{5,6},{6,7},{7,4},{8,9},{9,10},{10,1... | collective-permute-start | bytes 12296 | tf_op jit(solution)/shard_map/ppermute | solution.py:209
  428.4 9.2 %collective-permute-done.92.refs_2_ = bf16[2,128,512]{2,1,0:T(8,128)(2,1)S(1)} collective-permute-done((bf16[2,128,512]{2,1,0:T(8,128)(2,1)S(1)}, bf16[2,128,512]{2,1,0:T(8,128)(2,1)S(1)}, u32[]{:S(2)}, u32[]{:S(2)}) %collective-permute-start.92) | collective-permute-done | bytes 262176 | tf_op jit(solution)/shard_map/ppermute | solution.py:209
  440.2 10.7 %collective-permute-start.75 = (bf16[3,128,512]{2,1,0:T(8,128)(2,1)S(1)}, bf16[3,128,512]{2,1,0:T(8,128)(2,1)S(1)}, u32[]{:S(2)}, u32[]{:S(2)}) collective-permute-start(bf16[3,128,512]{2,1,0:T(8,128)(2,1)S(1)} %get-tuple-element.59.refs_0_), channel_id=1, source_target_pairs={{0,2},{1,3},{2,0},{3,1},{4,6},{5,7},{6,4},{7,5},{8,10},{9,11},{10,... | collective-permute-start | bytes 1179656 | tf_op jit(solution)/shard_map/ppermute | solution.py:209
  454.4 15.0 %collective-permute-done.75.refs_2_ = bf16[3,128,512]{2,1,0:T(8,128)(2,1)S(1)} collective-permute-done((bf16[3,128,512]{2,1,0:T(8,128)(2,1)S(1)}, bf16[3,128,512]{2,1,0:T(8,128)(2,1)S(1)}, u32[]{:S(2)}, u32[]{:S(2)}) %collective-permute-start.75) | collective-permute-done | bytes 393248 | tf_op jit(solution)/shard_map/ppermute | solution.py:209
  519.1 9.5 %shard_map.59 = (bf16[256,1792]{1,0:T(8,128)(2,1)S(1)}, bf16[256,1792]{1,0:T(8,128)(2,1)S(1)}) custom-call(f32[2]{0:T(128)S(1)} %pad_maximum_fusion.2.refs_0_, bf16[512,1024]{1,0:T(8,128)(2,1)S(1)} %get-tuple-element.55.refs_1_, bf16[512,1024]{1,0:T(8,128)(2,1)S(1)} %get-tuple-element.54.refs_2_.refs_1_, bf16[256,1792]{1,0:T(8,128)(2,1)S(1)} %copy-done.40, ...), custom_call_target="tpu_custom_call" | custom-call | flops 3758096384 | bytes 16777224 | tf_op jit(solution)/shard_map/pallas_call | solution.py:80
  535.6 16.7 %collective-permute-done.100.refs_2_ = bf16[256,1792]{1,0:T(8,128)(2,1)S(1)} collective-permute-done((bf16[256,1792]{1,0:T(8,128)(2,1)S(1)}, bf16[256,1792]{1,0:T(8,128)(2,1)S(1)}, u32[]{:S(2)}, u32[]{:S(2)}) %collective-permute-start.100) | collective-permute-done | bytes 917536 | tf_op jit(solution)/shard_map/ppermute | solution.py:75
  553.1 18.1 %collective-permute-done.96.refs_3_ = bf16[256,1792]{1,0:T(8,128)(2,1)} collective-permute-done((bf16[256,1792]{1,0:T(8,128)(2,1)S(1)}, bf16[256,1792]{1,0:T(8,128)(2,1)}, u32[]{:S(2)}, u32[]{:S(2)}) %collective-permute-start.96) | collective-permute-done | bytes 917536 | tf_op jit(solution)/shard_map/ppermute | solution.py:75
  574.6 19.1 %collective-permute-done.97.refs_5_ = bf16[256,1792]{1,0:T(8,128)(2,1)} collective-permute-done((bf16[256,1792]{1,0:T(8,128)(2,1)}, bf16[256,1792]{1,0:T(8,128)(2,1)}, u32[]{:S(2)}, u32[]{:S(2)}) %collective-permute-start.97) | collective-permute-done | bytes 917536 | tf_op jit(solution)/shard_map/ppermute | solution.py:75
  (466 shorter events, 295.9 us)
Async XLA Ops:
  8.6 39.1 %collective-permute-start.5 = (bf16[256,1792]{1,0:T(8,128)(2,1)S(1)}, bf16[256,1792]{1,0:T(8,128)(2,1)}, u32[]{:S(2)}, u32[]{:S(2)}) collective-permute-start(bf16[256,1792]{1,0:T(8,128)(2,1)S(1)} %get-tuple-element.67.refs_0_.refs_1_.refs_12_.refs_7_), channel_id=1, source_target_pairs={{8,0},{12,4},{4,8},{0,12},{24,16},{28,20},{20,24},{16,28},{9,1},{1... | collective-permute-start | bytes 2752520 | tf_op jit(solution)/shard_map/ppermute | solution.py:75
  9.6 40.0 %collective-permute-start.8 = (bf16[256,1792]{1,0:T(8,128)(2,1)S(1)}, bf16[256,1792]{1,0:T(8,128)(2,1)}, u32[]{:S(2)}, u32[]{:S(2)}) collective-permute-start(bf16[256,1792]{1,0:T(8,128)(2,1)S(1)} %get-tuple-element.66.refs_1_.refs_2_.refs_13_.refs_8_), channel_id=1, source_target_pairs={{16,0},{20,4},{28,8},{24,12},{4,16},{0,20},{8,24},{12,28},{17,1},{... | collective-permute-start | bytes 2752520 | tf_op jit(solution)/shard_map/ppermute | solution.py:75
  14.7 43.9 %collective-permute-start.2 = (bf16[2,128,512]{2,1,0:T(8,128)(2,1)S(1)}, bf16[2,128,512]{2,1,0:T(8,128)(2,1)S(1)}, u32[]{:S(2)}, u32[]{:S(2)}) collective-permute-start(bf16[2,128,512]{2,1,0:T(8,128)(2,1)S(1)} %get-tuple-element.33), channel_id=1, source_target_pairs={{0,1},{1,2},{2,3},{3,0},{4,5},{5,6},{6,7},{7,4},{8,9},{9,10},{10,1... | collective-permute-start | bytes 786440 | tf_op jit(solution)/shard_map/ppermute | solution.py:209
  107.5 32.1 %collective-permute-start.19 = (bf16[3,128,512]{2,1,0:T(8,128)(2,1)S(1)}, bf16[3,128,512]{2,1,0:T(8,128)(2,1)S(1)}, u32[]{:S(2)}, u32[]{:S(2)}) collective-permute-start(bf16[3,128,512]{2,1,0:T(8,128)(2,1)S(1)} %get-tuple-element.63.refs_0_), channel_id=1, source_target_pairs={{0,1},{1,2},{2,3},{3,0},{4,5},{5,6},{6,7},{7,4},{8,9},{9,10},{10,1... | collective-permute-start | bytes 1179656 | tf_op jit(solution)/shard_map/ppermute | solution.py:209
  114.3 53.1 %collective-permute-start.34 = (bf16[256,1792]{1,0:T(8,128)(2,1)}, bf16[256,1792]{1,0:T(8,128)(2,1)}, u32[]{:S(2)}, u32[]{:S(2)}) collective-permute-start(bf16[256,1792]{1,0:T(8,128)(2,1)} %collective-permute-done.6.refs_3_.refs_2_), channel_id=1, source_target_pairs={{0,16},{4,20},{8,28},{12,24},{16,4},{20,0},{24,8},{28,12},{1,17},{... | collective-permute-start | bytes 2752520 | tf_op jit(solution)/shard_map/ppermute | solution.py:75
  126.2 42.7 %collective-permute-start.33 = (bf16[256,1792]{1,0:T(8,128)(2,1)}, bf16[256,1792]{1,0:T(8,128)(2,1)}, u32[]{:S(2)}, u32[]{:S(2)}) collective-permute-start(bf16[256,1792]{1,0:T(8,128)(2,1)} %copy-done.28), channel_id=1, source_target_pairs={{0,8},{4,12},{8,4},{12,0},{16,24},{20,28},{24,20},{28,16},{1,9},{5... | collective-permute-start | bytes 2752520 | tf_op jit(solution)/shard_map/ppermute | solution.py:75
  127.6 42.1 %collective-permute-start.30 = (bf16[256,1792]{1,0:T(8,128)(2,1)}, bf16[256,1792]{1,0:T(8,128)(2,1)S(1)}, u32[]{:S(2)}, u32[]{:S(2)}) collective-permute-start(bf16[256,1792]{1,0:T(8,128)(2,1)} %collective-permute-done.6.refs_3_.refs_2_), channel_id=1, source_target_pairs={{0,4},{4,0},{8,12},{12,8},{16,20},{20,16},{24,28},{28,24},{1,5},{5... | collective-permute-start | bytes 2752520 | tf_op jit(solution)/shard_map/ppermute | solution.py:75
  176.3 32.4 %collective-permute-start.31 = (bf16[256,1792]{1,0:T(8,128)(2,1)}, bf16[256,1792]{1,0:T(8,128)(2,1)}, u32[]{:S(2)}, u32[]{:S(2)}) collective-permute-start(bf16[256,1792]{1,0:T(8,128)(2,1)} %copy-done.28), channel_id=1, source_target_pairs={{0,4},{4,0},{8,12},{12,8},{16,20},{20,16},{24,28},{28,24},{1,5},{5... | collective-permute-start | bytes 2752520 | tf_op jit(solution)/shard_map/ppermute | solution.py:75
  218.4 41.5 %collective-permute-start.42 = (bf16[256,1792]{1,0:T(8,128)(2,1)S(1)}, bf16[256,1792]{1,0:T(8,128)(2,1)}, u32[]{:S(2)}, u32[]{:S(2)}) collective-permute-start(bf16[256,1792]{1,0:T(8,128)(2,1)S(1)} %get-tuple-element.43.refs_2_), channel_id=1, source_target_pairs={{8,0},{12,4},{4,8},{0,12},{24,16},{28,20},{20,24},{16,28},{9,1},{1... | collective-permute-start | bytes 2752520 | tf_op jit(solution)/shard_map/ppermute | solution.py:75
  219.3 41.2 %collective-permute-start.40 = (bf16[256,1792]{1,0:T(8,128)(2,1)S(1)}, bf16[256,1792]{1,0:T(8,128)(2,1)}, u32[]{:S(2)}, u32[]{:S(2)}) collective-permute-start(bf16[256,1792]{1,0:T(8,128)(2,1)S(1)} %get-tuple-element.42.refs_1_), channel_id=1, source_target_pairs={{16,0},{20,4},{28,8},{24,12},{4,16},{0,20},{8,24},{12,28},{17,1},{... | collective-permute-start | bytes 2752520 | tf_op jit(solution)/shard_map/ppermute | solution.py:75
  221.0 40.7 %collective-permute-start.53 = (bf16[256,1792]{1,0:T(8,128)(2,1)S(1)}, bf16[256,1792]{1,0:T(8,128)(2,1)S(1)}, u32[]{:S(2)}, u32[]{:S(2)}) collective-permute-start(bf16[256,1792]{1,0:T(8,128)(2,1)S(1)} %get-tuple-element.43.refs_2_), channel_id=1, source_target_pairs={{0,4},{4,0},{8,12},{12,8},{16,20},{20,16},{24,28},{28,24},{1,5},{5... | collective-permute-start | bytes 2752520 | tf_op jit(solution)/shard_map/ppermute | solution.py:75
  222.0 40.7 %collective-permute-start.47 = (bf16[256,1792]{1,0:T(8,128)(2,1)S(1)}, bf16[256,1792]{1,0:T(8,128)(2,1)}, u32[]{:S(2)}, u32[]{:S(2)}) collective-permute-start(bf16[256,1792]{1,0:T(8,128)(2,1)S(1)} %get-tuple-element.43.refs_2_), channel_id=1, source_target_pairs={{16,0},{20,4},{28,8},{24,12},{4,16},{0,20},{8,24},{12,28},{17,1},{... | collective-permute-start | bytes 2752520 | tf_op jit(solution)/shard_map/ppermute | solution.py:75
  309.3 41.6 %collective-permute-start.60 = (bf16[256,1792]{1,0:T(8,128)(2,1)S(1)}, bf16[256,1792]{1,0:T(8,128)(2,1)}, u32[]{:S(2)}, u32[]{:S(2)}) collective-permute-start(bf16[256,1792]{1,0:T(8,128)(2,1)S(1)} %get-tuple-element.45.refs_1_.refs_2_.refs_13_.refs_8_), channel_id=1, source_target_pairs={{8,0},{12,4},{4,8},{0,12},{24,16},{28,20},{20,24},{16,28},{9,1},{1... | collective-permute-start | bytes 2752520 | tf_op jit(solution)/shard_map/ppermute | solution.py:75
  310.2 52.5 %collective-permute-start.61 = (bf16[256,1792]{1,0:T(8,128)(2,1)S(1)}, bf16[256,1792]{1,0:T(8,128)(2,1)}, u32[]{:S(2)}, u32[]{:S(2)}) collective-permute-start(bf16[256,1792]{1,0:T(8,128)(2,1)S(1)} %get-tuple-element.44.refs_0_.refs_1_.refs_12_.refs_7_), channel_id=1, source_target_pairs={{16,0},{20,4},{28,8},{24,12},{4,16},{0,20},{8,24},{12,28},{17,1},{... | collective-permute-start | bytes 2752520 | tf_op jit(solution)/shard_map/ppermute | solution.py:75
  310.6 52.2 %collective-permute-start.62 = (bf16[256,1792]{1,0:T(8,128)(2,1)S(1)}, bf16[256,1792]{1,0:T(8,128)(2,1)}, u32[]{:S(2)}, u32[]{:S(2)}) collective-permute-start(bf16[256,1792]{1,0:T(8,128)(2,1)S(1)} %get-tuple-element.45.refs_1_.refs_2_.refs_13_.refs_8_), channel_id=1, source_target_pairs={{16,0},{20,4},{28,8},{24,12},{4,16},{0,20},{8,24},{12,28},{17,1},{... | collective-permute-start | bytes 2752520 | tf_op jit(solution)/shard_map/ppermute | solution.py:75
  314.2 55.9 %collective-permute-start.56 = (bf16[2,128,512]{2,1,0:T(8,128)(2,1)S(1)}, bf16[2,128,512]{2,1,0:T(8,128)(2,1)S(1)}, u32[]{:S(2)}, u32[]{:S(2)}) collective-permute-start(bf16[2,128,512]{2,1,0:T(8,128)(2,1)S(1)} %get-tuple-element.47), channel_id=1, source_target_pairs={{0,1},{1,2},{2,3},{3,0},{4,5},{5,6},{6,7},{7,4},{8,9},{9,10},{10,1... | collective-permute-start | bytes 786440 | tf_op jit(solution)/shard_map/ppermute | solution.py:209
  331.7 40.0 %collective-permute-start.57 = (bf16[2,128,512]{2,1,0:T(8,128)(2,1)S(1)}, bf16[2,128,512]{2,1,0:T(8,128)(2,1)S(1)}, u32[]{:S(2)}, u32[]{:S(2)}) collective-permute-start(bf16[2,128,512]{2,1,0:T(8,128)(2,1)S(1)} %get-tuple-element.48), channel_id=1, source_target_pairs={{0,2},{1,3},{2,0},{3,1},{4,6},{5,7},{6,4},{7,5},{8,10},{9,11},{10,... | collective-permute-start | bytes 786440 | tf_op jit(solution)/shard_map/ppermute | solution.py:209
  427.1 51.5 %collective-permute-start.88 = (bf16[256,1792]{1,0:T(8,128)(2,1)}, bf16[256,1792]{1,0:T(8,128)(2,1)}, u32[]{:S(2)}, u32[]{:S(2)}) collective-permute-start(bf16[256,1792]{1,0:T(8,128)(2,1)} %collective-permute-done.60.refs_3_.refs_2_), channel_id=1, source_target_pairs={{0,16},{4,20},{8,28},{12,24},{16,4},{20,0},{24,8},{28,12},{1,17},{... | collective-permute-start | bytes 2752520 | tf_op jit(solution)/shard_map/ppermute | solution.py:75
  438.3 41.9 %collective-permute-start.87 = (bf16[256,1792]{1,0:T(8,128)(2,1)}, bf16[256,1792]{1,0:T(8,128)(2,1)}, u32[]{:S(2)}, u32[]{:S(2)}) collective-permute-start(bf16[256,1792]{1,0:T(8,128)(2,1)} %collective-permute-done.61.refs_4_.refs_3_), channel_id=1, source_target_pairs={{0,8},{4,12},{8,4},{12,0},{16,24},{20,28},{24,20},{28,16},{1,9},{5... | collective-permute-start | bytes 2752520 | tf_op jit(solution)/shard_map/ppermute | solution.py:75
  439.5 40.7 %collective-permute-start.83 = (bf16[256,1792]{1,0:T(8,128)(2,1)}, bf16[256,1792]{1,0:T(8,128)(2,1)S(1)}, u32[]{:S(2)}, u32[]{:S(2)}) collective-permute-start(bf16[256,1792]{1,0:T(8,128)(2,1)} %copy-done.30), channel_id=1, source_target_pairs={{0,4},{4,0},{8,12},{12,8},{16,20},{20,16},{24,28},{28,24},{1,5},{5... | collective-permute-start | bytes 2752520 | tf_op jit(solution)/shard_map/ppermute | solution.py:75
  529.2 42.0 %collective-permute-start.96 = (bf16[256,1792]{1,0:T(8,128)(2,1)S(1)}, bf16[256,1792]{1,0:T(8,128)(2,1)}, u32[]{:S(2)}, u32[]{:S(2)}) collective-permute-start(bf16[256,1792]{1,0:T(8,128)(2,1)S(1)} %get-tuple-element.57.refs_2_), channel_id=1, source_target_pairs={{8,0},{12,4},{4,8},{0,12},{24,16},{28,20},{20,24},{16,28},{9,1},{1... | collective-permute-start | bytes 2752520 | tf_op jit(solution)/shard_map/ppermute | solution.py:75
  530.5 41.5 %collective-permute-start.94 = (bf16[256,1792]{1,0:T(8,128)(2,1)S(1)}, bf16[256,1792]{1,0:T(8,128)(2,1)}, u32[]{:S(2)}, u32[]{:S(2)}) collective-permute-start(bf16[256,1792]{1,0:T(8,128)(2,1)S(1)} %get-tuple-element.56.refs_1_), channel_id=1, source_target_pairs={{16,0},{20,4},{28,8},{24,12},{4,16},{0,20},{8,24},{12,28},{17,1},{... | collective-permute-start | bytes 2752520 | tf_op jit(solution)/shard_map/ppermute | solution.py:75
  532.6 39.6 %collective-permute-start.107 = (bf16[256,1792]{1,0:T(8,128)(2,1)S(1)}, bf16[256,1792]{1,0:T(8,128)(2,1)S(1)}, u32[]{:S(2)}, u32[]{:S(2)}) collective-permute-start(bf16[256,1792]{1,0:T(8,128)(2,1)S(1)} %get-tuple-element.57.refs_2_), channel_id=1, source_target_pairs={{0,4},{4,0},{8,12},{12,8},{16,20},{20,16},{24,28},{28,24},{1,5},{5... | collective-permute-start | bytes 2752520 | tf_op jit(solution)/shard_map/ppermute | solution.py:75
  533.6 39.6 %collective-permute-start.101 = (bf16[256,1792]{1,0:T(8,128)(2,1)S(1)}, bf16[256,1792]{1,0:T(8,128)(2,1)}, u32[]{:S(2)}, u32[]{:S(2)}) collective-permute-start(bf16[256,1792]{1,0:T(8,128)(2,1)S(1)} %get-tuple-element.57.refs_2_), channel_id=1, source_target_pairs={{16,0},{20,4},{28,8},{24,12},{4,16},{0,20},{8,24},{12,28},{17,1},{... | collective-permute-start | bytes 2752520 | tf_op jit(solution)/shard_map/ppermute | solution.py:75
  (195 other events, 2525.3 us)

commit v2 on v1

v2 whole, which is shorter than its diff:
```python
import functools
import math

import jax
import jax.numpy as jnp
from jax import lax
from jax.experimental import pallas as pl
from jax.experimental.pallas import tpu as pltpu
from jax.sharding import PartitionSpec as P


STEPS = 2


momentum_decay = 0.95
linear_term = 3.4445
cubic_term = -4.775
quintic_term = 2.0315

f32, bf16 = jnp.float32, jnp.bfloat16


def dot_nn(a, b):
    return lax.dot_general(a, b, (((1,), (0,)), ((), ())), preferred_element_type=f32)


def dot_nt(a, b):
    return lax.dot_general(a, b, (((1,), (1,)), ((), ())), preferred_element_type=f32)


def iterate_general(current):
    matrix = current.astype(bf16)
    column_panel = lax.all_gather(matrix, "dp", axis=0, tiled=True)
    summed_part = lax.psum_scatter(dot_nt(matrix, column_panel), "shard", scatter_dimension=0, tiled=True)
    gram_part = summed_part.astype(bf16)
    gram_panel = lax.all_gather(gram_part, "shard", axis=0, tiled=True)
    square_sum = lax.psum(jnp.sum(jnp.square(gram_part.astype(f32))), ("dp", "shard"))
    inverse_norm = lax.rsqrt(square_sum)
    root_scale = jnp.sqrt(inverse_norm)
    matrix_full = matrix.astype(f32)
    first = dot_nn(gram_panel, column_panel)
    mixture = (
        cubic_term * root_scale * matrix_full + quintic_term * root_scale * inverse_norm * first
    ).astype(bf16)
    second = dot_nn(gram_panel, lax.all_gather(mixture, "dp", axis=0, tiled=True))
    return linear_term * root_scale * matrix_full + inverse_norm * second


def x_bit(i):
    return (i >> 1) & 1


def y_bit(i):
    return (i >> 2) & 1


def x_pick(i):
    return i ^ 2 ^ x_bit(i)


def y_pick(i):
    return i ^ 4 ^ (x_bit(i) ^ y_bit(i))


ROW_DEVICES = 8
VMEM_LIMIT = 16 << 20
CORE = [(i, i ^ 1) for i in range(ROW_DEVICES)]
TAKE_X = [(x_pick(i), i) for i in range(ROW_DEVICES)]
TAKE_Y = [(y_pick(i), i) for i in range(ROW_DEVICES)]
GIVE_X = [(i, x_pick(i)) for i in range(ROW_DEVICES)]
GIVE_Y = [(i, y_pick(i)) for i in range(ROW_DEVICES)]


def over_dp(value, pairs):
    return lax.ppermute(value, "dp", pairs)


def call(kernel, outs, args, scalars=(), scratch=(), flops=0):
    moved = sum(a.size * a.dtype.itemsize for a in [*args, *outs])
    vmem = pl.BlockSpec(memory_space=pltpu.VMEM)
    return pl.pallas_call(
        kernel,
        out_shape=outs,
        in_specs=[pl.BlockSpec(memory_space=pltpu.SMEM)] * len(scalars) + [vmem] * len(args),
        out_specs=[vmem] * len(outs),
        scratch_shapes=list(scratch),
        compiler_params=pltpu.CompilerParams(vmem_limit_bytes=VMEM_LIMIT),
        cost_estimate=pl.CostEstimate(flops=flops, bytes_accessed=moved, transcendentals=0),
    )(*scalars, *[pltpu.with_memory_space_constraint(a, pltpu.VMEM) for a in args])


def split_rows(total, size, z, kept, pieces):
    rows = kept.shape[1]
    for by in range(size):
        at = pl.multiple_of(lax.rem(z + by, size) * rows, rows)
        piece = total[:, pl.ds(at, rows), :]
        if by:
            pieces[by - 1][...] = piece.astype(bf16)
        else:
            kept[...] = piece


def own_gram_kernel(size, z_ref, core_ref, top, bottom, core_top, core_bottom, kept, *rest):
    pieces, total = rest[:-1], rest[-1]
    for q, (left, right) in enumerate([(top, top), (bottom, bottom), (bottom, top)]):
        total[q] = dot_nt(left[...], right[...])
    for core, (first, second) in enumerate([(core_top, core_bottom), (core_bottom, core_top)]):

        @pl.when(core_ref[0] == core)
        def _():
            total[3] = dot_nt(top[...], first[...])
            total[4] = dot_nt(bottom[...], second[...])

    split_rows(total, size, z_ref[0], kept, pieces)


def far_gram_kernel(size, z_ref, *refs):
    halves, (kept, *pieces), total = refs[:6], refs[6:-1], refs[-1]
    for p, (left, right) in enumerate([(0, 1), (1, 2), (0, 2)]):
        value = jnp.concatenate([halves[2 * left][...], halves[2 * left + 1][...]], axis=0)
        half = value.shape[0] // 2
        for h in range(2):
            total[p, :, h * half : (h + 1) * half] = dot_nt(value, halves[2 * right + h][...])
    split_rows(total, size, z_ref[0], kept, pieces)


def gram(kernel, shape, size, scalars, blocks):
    halves = [half for block in blocks for half in block]
    count, rows, columns = shape
    shape = (count, rows // size, columns)
    outs = [jax.ShapeDtypeStruct(shape, f32)] + [jax.ShapeDtypeStruct(shape, bf16)] * (size - 1)
    return call(
        functools.partial(kernel, size),
        outs,
        halves,
        scalars,
        [pltpu.VMEM((count, rows, columns), f32)],
        2 * count * rows * columns * halves[0].shape[1],
    )


def own_assemble_kernel(size, z_ref, *refs):
    parts, (diagonal, beside) = refs[:-2], refs[-2:]
    z = z_ref[0]
    rows, half = parts[0].shape[1], parts[0].shape[2]
    for by, part in enumerate(parts):
        at = lax.rem(z + size - by, size) * rows
        upper, lower = pl.ds(pl.multiple_of(at, rows), rows), pl.ds(pl.multiple_of(half + at, rows), rows)
        diagonal[upper, :half] = part[0]
        diagonal[lower, half:] = part[1]
        diagonal[lower, :half] = part[2]
        beside[upper, :] = part[3]
        beside[lower, :] = part[4]
    diagonal[:half, half:] = diagonal[half:, :half].T


def own_assemble(z, size, parts):
    half = parts[0].shape[2]
    outs = [jax.ShapeDtypeStruct((2 * half, columns), bf16) for columns in (2 * half, half)]
    return call(functools.partial(own_assemble_kernel, size), outs, parts, [z])


def beside_kernel(core_ref, own, other, out):
    half = own.shape[1]
    for core in range(2):

        @pl.when(core_ref[0] == core)
        def _():
            like, unlike = slice(core * half, (core + 1) * half), slice((1 - core) * half, (2 - core) * half)
            out[:half, like] = own[:half]
            out[half:, unlike] = own[half:]
            out[unlike, :half] = other[:half].T
            out[like, half:] = other[half:].T


def beside_of(core, own, other):
    rows = own.shape[0]
    return call(beside_kernel, [jax.ShapeDtypeStruct((rows, rows), bf16)], [own, other], [core])[0]


def assemble_kernel(takes, size, z_ref, *refs):
    groups, outs = refs[: len(refs) - len(takes)], refs[len(refs) - len(takes) :]
    z = z_ref[0]
    rows = groups[0].shape[1]
    columns = groups[0].shape[2]
    for out, taken in zip(outs, takes):
        for k, (group, index, transposed) in enumerate(taken):
            for by in range(size):
                part = groups[group * size + by][index]
                at = pl.multiple_of(lax.rem(z + size - by, size) * rows, rows)
                if transposed:
                    out[:, pl.ds(pl.multiple_of(k * columns + at, rows), rows)] = part.T
                else:
                    out[pl.ds(at, rows), k * columns : (k + 1) * columns] = part


def assemble(z, size, groups, takes):
    parts = [part for group in groups for part in group]
    columns = parts[0].shape[2]
    outs = [jax.ShapeDtypeStruct((columns, columns * len(taken)), bf16) for taken in takes]
    return call(functools.partial(assemble_kernel, takes, size), outs, parts, [z])


def product_kernel(n_grams, n_halves, has_sum, finish, tile, *refs):
    refs = list(refs)
    if finish:
        inverse_norm = lax.rsqrt(jnp.sum(refs.pop(0)[...], axis=(0, 1), keepdims=True))
        root_scale = jnp.sqrt(inverse_norm)
        scales = finish(root_scale, inverse_norm)
    grams, refs = refs[:n_grams], refs[n_grams:]
    halves, refs = refs[:n_halves], refs[n_halves:]
    summed = refs.pop(0) if has_sum else None
    own, outs = (refs[:2], refs[2:]) if finish else (None, refs)
    columns = halves[0].shape[1]

    def column_tile(t, carry):
        at = pl.ds(pl.multiple_of(t * tile, tile), tile)
        gram = jnp.concatenate([g[...] for g in grams], axis=1)
        value = dot_nn(gram, jnp.concatenate([h[:, at] for h in halves], axis=0))
        if has_sum:
            value = value + summed[:, at]
        if finish:
            block = jnp.concatenate([own[0][:, at], own[1][:, at]], axis=0)
            value = scales[0] * block.astype(f32) + scales[1] * value
        rows = value.shape[0] // len(outs)
        for k, out in enumerate(outs):
            out[:, at] = value[k * rows : (k + 1) * rows].astype(out.dtype)
        return carry

    lax.fori_loop(0, columns // tile, column_tile, 0)


def product(grams, blocks, summed=None, finish=None, dtype=f32, parts=1):
    halves = [half for block in blocks for half in block]
    half, columns = halves[0].shape
    tile = 256 if columns % 256 == 0 else columns
    args = ([finish[1]] if finish else []) + list(grams) + halves
    args += [] if summed is None else [summed]
    args += list(finish[2]) if finish else []
    outs = [jax.ShapeDtypeStruct((2 * half // parts, columns), dtype)] * parts
    return call(
        functools.partial(
            product_kernel, len(grams), len(halves), summed is not None, finish and finish[0], tile
        ),
        outs,
        args,
        flops=4 * half * half * columns * len(halves),
    )


def shifted(value, by, size):
    return lax.ppermute(value, "shard", [(z, (z + by) % size) for z in range(size)])


def total_of(value, size):
    for step in (1, 2, 4):
        value = value + over_dp(value, [(i, i ^ step) for i in range(ROW_DEVICES)])
    return sum([shifted(value, by, size) for by in range(1, size)], value)


def gather(block):
    top, bottom = block
    x_bottom, y_top = over_dp(bottom, TAKE_X), over_dp(top, TAKE_Y)
    x_top, y_bottom = over_dp(top, TAKE_X), over_dp(bottom, TAKE_Y)
    core = over_dp(top, CORE), over_dp(bottom, CORE)
    d_oth_bottom, d_sel_top = over_dp(x_bottom, GIVE_Y), over_dp(y_top, GIVE_X)
    x_oth = over_dp(x_top, CORE), over_dp(x_bottom, CORE)
    y_oth = over_dp(y_top, CORE), over_dp(y_bottom, CORE)
    d_oth_top, d_sel_bottom = over_dp(d_sel_top, CORE), over_dp(d_oth_bottom, CORE)
    near = core, (x_top, x_bottom), (y_top, y_bottom)
    return near, (x_oth, y_oth, (d_sel_top, d_sel_bottom), (d_oth_top, d_oth_bottom))


def fold_kernel(weights, *refs):
    kept, *pieces, before, out, squares = refs
    total = kept[...]
    for piece in pieces:
        total = total + piece[...].astype(f32)
    part = total.astype(bf16)
    out[...] = part
    total = before[...]
    for index, weight in enumerate(weights):
        square = jnp.square(part[index].astype(f32))
        square = sum(square[:, k : k + 128] for k in range(0, square.shape[1], 128))
        total = total + weight * jnp.sum(square.reshape(-1, 8, 128), axis=0)
    squares[...] = total


def reduce_parts(pieces, size, before, weights):
    kept, *sent = pieces
    received = [shifted(piece, by, size) for by, piece in enumerate(sent, 1)]
    outs = [jax.ShapeDtypeStruct(kept.shape, bf16), jax.ShapeDtypeStruct(before.shape, f32)]
    return call(functools.partial(fold_kernel, weights), outs, [kept, *received, before])


def spread(part, size):
    parts = [part]
    for by in range(1, size):
        parts.append(shifted(part, by, size))
    return parts


def iterate_square(matrix, size, gain, dtype, parts):
    z = lax.axis_index("shard").reshape(1)
    side_index = (lax.axis_index("dp") & 1).reshape(1)
    (core, x_sel, y_sel), (x_oth, y_oth, d_sel, d_oth) = gather(matrix)
    half = matrix[0].shape[0]
    own_pieces = gram(own_gram_kernel, (5, half, half), size, [z, side_index], [matrix, core])
    own_part, squares = reduce_parts(
        own_pieces, size, jnp.zeros((8, 128), f32), (1.0, 1.0, 2.0, 2.0, 2.0)
    )
    own_parts = spread(own_part, size)
    far_pieces = gram(far_gram_kernel, (3, 2 * half, 2 * half), size, [z], [matrix, x_sel, y_sel])
    far_part, squares = reduce_parts(far_pieces, size, squares, (2.0, 2.0, 2.0))
    squares = total_of(squares, size)
    far_parts = spread(far_part, size)
    x_parts = [over_dp(p[:2], GIVE_X) for p in far_parts]
    y_parts = [over_dp(p[1:], GIVE_Y) for p in far_parts]
    own, beside = own_assemble(z, size, own_parts)
    beside = beside_of(side_index, beside, over_dp(beside, CORE))
    (far,) = assemble(z, size, [far_parts], [[(0, 0, False), (0, 2, False)]])
    side, diagonal = assemble(
        z,
        size,
        [x_parts, y_parts],
        [[(0, 0, True), (1, 1, True)], [(0, 1, False), (1, 0, True)]],
    )
    (first,) = product([own, beside], [matrix, core])
    (first,) = product([far], [x_sel, y_sel], first)

    def mixing(root_scale, inverse_norm):
        return cubic_term * root_scale, quintic_term * root_scale * inverse_norm

    def ending(root_scale, inverse_norm):
        return gain * linear_term * root_scale, gain * inverse_norm

    mixture = product(
        [side, diagonal], [x_oth, y_oth, d_sel, d_oth], first, (mixing, squares, matrix), bf16, 2
    )
    (core, x_sel, y_sel), (x_oth, y_oth, d_sel, d_oth) = gather(mixture)
    (second,) = product([own, beside], [mixture, core])
    (second,) = product([far, side], [x_sel, y_sel, x_oth, y_oth], second)
    return product([diagonal], [d_sel, d_oth], second, (ending, squares, matrix), dtype, parts)


def current_of(momentum, gradient):
    grad_full = gradient.astype(f32)
    new_momentum = momentum_decay * momentum + grad_full
    return new_momentum, grad_full + momentum_decay * new_momentum


def body_square(size, columns, momentum, gradient):
    half = momentum.shape[0] // 2
    block = [
        current_of(momentum[rows], gradient[rows])[1].astype(bf16)
        for rows in (slice(0, half), slice(half, None))
    ]
    new_momentum, _ = current_of(*lax.optimization_barrier((momentum, gradient)))
    for iteration in range(STEPS):
        last = iteration == STEPS - 1
        block = iterate_square(
            block, size, math.sqrt(columns) if last else 1.0, f32 if last else bf16, 1 if last else 2
        )
    return (new_momentum, block[0])


def body_general(columns, momentum, gradient):
    grad_full = gradient.astype(f32)
    new_momentum = momentum_decay * momentum + grad_full
    current = grad_full + momentum_decay * new_momentum
    for _ in range(STEPS):
        current = iterate_general(current)
    return (new_momentum, math.sqrt(columns) * current)


def solution(mesh):
    row_devices, column_devices = mesh.shape["dp"], mesh.shape["shard"]
    spec = P("dp", "shard")

    def sharded(body):
        return jax.shard_map(body, mesh=mesh, in_specs=(spec, spec), out_specs=(spec, spec), check_vma=False)

    def general(momentum, gradient):
        return sharded(functools.partial(body_general, momentum.shape[1]))(momentum, gradient)

    def square(momentum, gradient):
        return sharded(functools.partial(body_square, column_devices, momentum.shape[1]))(momentum, gradient)

    if row_devices != ROW_DEVICES or column_devices & (column_devices - 1):
        return general
    return square
```

time: 631 us -> 556 us (0.88)
  waiting for transfers between devices: 310 us -> 377 us
  local copies, waits for them, and re-layouts: 53.5 us -> 2.41 us
  starting transfers between devices: 147 us -> 97.8 us
  Pallas kernels: 95.2 us -> 65.8 us
    unnamed x222 -> x10, local copies, waits for them, and re-layouts: 52.2 us -> 2.12 us
    ppermute x30, starting transfers between devices: 101 us -> 51.4 us  [shifted(): lax.ppermute(value, 'shard', [(z, (z + by) % size) for z in range(size)])]
    ppermute x78 -> x80, waiting for transfers between devices: 207 us -> 240 us  [over_dp(): return lax.ppermute(value, 'dp', pairs)]
    ppermute x30, waiting for transfers between devices: 104 us -> 137 us  [shifted(): lax.ppermute(value, 'shard', [(z, (z + by) % size) for z in range(size)])]
    pallas_call x22 -> x28, Pallas kernels: 95.2 us -> 65.8 us  [call(): pl.pallas_call(kernel, out_shape=outs, in_specs=[pl.BlockSpec(memory_spac...]
    ppermute x78 -> x80, starting transfers between devices: 45.9 us -> 46.5 us  [over_dp(): return lax.ppermute(value, 'dp', pairs)]
  transfers between devices with their start and end apart: 108 -> 110, of which waited for: 39 -> 45; matrix products, arithmetic and copies ran while one was open for 1% -> 0% of each run, Pallas kernels for 10% -> 9%
where the time goes in v2:
time: 556 us; the launch traced here: 550 us
  waiting for transfers between devices  377 us (68%)
  starting transfers between devices  97.8 us (18%)
  Pallas kernels  65.8 us (12%)
    ppermute x80, waiting for transfers between devices, over_dp(): return lax.ppermute(value, 'dp', pairs)  240 us
    ppermute x30, waiting for transfers between devices, shifted(): lax.ppermute(value, 'shard', [(z, (z + by) % size) for z in range(size)])  137 us
    pallas_call x28, Pallas kernels, call(): pl.pallas_call(kernel, out_shape=outs, in_specs=[pl.BlockSpec(memory_spac...  65.8 us
    ppermute x30, starting transfers between devices, shifted(): lax.ppermute(value, 'shard', [(z, (z + by) % size) for z in range(size)])  51.4 us
    ppermute x80, starting transfers between devices, over_dp(): return lax.ppermute(value, 'dp', pairs)  46.5 us
  transfers between devices with their start and end apart: 110, of which 45 were waited for; matrix products, arithmetic and copies ran while one was open for 0% of the time, Pallas kernels for 9%

profile of v2, /device:TPU:0, one launch (start us, length us, event | category | flops | bytes accessed | tf_op | source)
XLA Modules:
  0.0 549.8 jit_solution(3259378655199714942)
XLA Ops:
  16.8 11.9 %collective-permute-done.1.refs_3_.refs_2_ = bf16[256,1792]{1,0:T(8,128)(2,1)} collective-permute-done((bf16[256,1792]{1,0:T(8,128)(2,1)S(1)}, bf16[256,1792]{1,0:T(8,128)(2,1)}, u32[]{:S(2)}, u32[]{:S(2)}) %collective-permute-start.1) | collective-permute-done | bytes 917536 | tf_op jit(solution)/shard_map/ppermute | solution.py:75
  32.8 14.9 %collective-permute-done.refs_2_.refs_1_ = bf16[256,1792]{1,0:T(8,128)(2,1)} collective-permute-done((bf16[256,1792]{1,0:T(8,128)(2,1)S(1)}, bf16[256,1792]{1,0:T(8,128)(2,1)}, u32[]{:S(2)}, u32[]{:S(2)}) %collective-permute-start) | collective-permute-done | bytes 917536 | tf_op jit(solution)/shard_map/ppermute | solution.py:75
  61.3 27.6 %collective-permute-done.37.refs_1_ = bf16[5,64,256]{2,1,0:T(8,128)(2,1)S(1)} collective-permute-done((bf16[5,64,256]{2,1,0:T(8,128)(2,1)S(1)}, bf16[5,64,256]{2,1,0:T(8,128)(2,1)S(1)}, u32[]{:S(2)}, u32[]{:S(2)}) %collective-permute-start.37) | collective-permute-done | bytes 163872 | tf_op jit(solution)/shard_map/ppermute | solution.py:252
  89.0 14.1 %collective-permute-done.38.refs_2_ = bf16[5,64,256]{2,1,0:T(8,128)(2,1)S(1)} collective-permute-done((bf16[5,64,256]{2,1,0:T(8,128)(2,1)S(1)}, bf16[5,64,256]{2,1,0:T(8,128)(2,1)S(1)}, u32[]{:S(2)}, u32[]{:S(2)}) %collective-permute-start.38) | collective-permute-done | bytes 163872 | tf_op jit(solution)/shard_map/ppermute | solution.py:252
  112.5 5.7 %collective-permute-done.13 = f32[8,128]{1,0:T(8,128)S(1)} collective-permute-done((f32[8,128]{1,0:T(8,128)S(1)}, f32[8,128]{1,0:T(8,128)S(1)}, u32[]{:S(2)}, u32[]{:S(2)}) %collective-permute-start.13) | collective-permute-done | bytes 4128 | tf_op jit(solution)/shard_map/ppermute | solution.py:75
  134.1 17.9 %collective-permute-done.21.refs_2_ = bf16[3,128,512]{2,1,0:T(8,128)(2,1)S(1)} collective-permute-done((bf16[3,128,512]{2,1,0:T(8,128)(2,1)S(1)}, bf16[3,128,512]{2,1,0:T(8,128)(2,1)S(1)}, u32[]{:S(2)}, u32[]{:S(2)}) %collective-permute-start.21) | collective-permute-done | bytes 393248 | tf_op jit(solution)/shard_map/ppermute | solution.py:252
  153.7 6.7 %collective-permute-done.25.refs_4_ = bf16[2,128,512]{2,1,0:T(8,128)(2,1)S(1)} collective-permute-done((bf16[2,128,512]{2,1,0:T(8,128)(2,1)S(1)}, bf16[2,128,512]{2,1,0:T(8,128)(2,1)S(1)}, u32[]{:S(2)}, u32[]{:S(2)}) %collective-permute-start.25) | collective-permute-done | bytes 262176 | tf_op jit(solution)/shard_map/ppermute | solution.py:75
  176.8 5.3 collective-permute-done.28.refs_7_
  201.5 19.6 %collective-permute-done.47.refs_2_ = bf16[256,1792]{1,0:T(8,128)(2,1)S(1)} collective-permute-done((bf16[256,1792]{1,0:T(8,128)(2,1)S(1)}, bf16[256,1792]{1,0:T(8,128)(2,1)S(1)}, u32[]{:S(2)}, u32[]{:S(2)}) %collective-permute-start.47) | collective-permute-done | bytes 917536 | tf_op jit(solution)/shard_map/ppermute | solution.py:75
  221.1 18.8 %collective-permute-done.43.refs_3_ = bf16[256,1792]{1,0:T(8,128)(2,1)S(1)} collective-permute-done((bf16[256,1792]{1,0:T(8,128)(2,1)S(1)}, bf16[256,1792]{1,0:T(8,128)(2,1)S(1)}, u32[]{:S(2)}, u32[]{:S(2)}) %collective-permute-start.43) | collective-permute-done | bytes 917536 | tf_op jit(solution)/shard_map/ppermute | solution.py:75
  242.4 19.5 %collective-permute-done.44.refs_5_ = bf16[256,1792]{1,0:T(8,128)(2,1)S(1)} collective-permute-done((bf16[256,1792]{1,0:T(8,128)(2,1)S(1)}, bf16[256,1792]{1,0:T(8,128)(2,1)S(1)}, u32[]{:S(2)}, u32[]{:S(2)}) %collective-permute-start.44) | collective-permute-done | bytes 917536 | tf_op jit(solution)/shard_map/ppermute | solution.py:75
  279.8 7.2 %collective-permute-start.64 = (bf16[5,64,256]{2,1,0:T(8,128)(2,1)S(1)}, bf16[5,64,256]{2,1,0:T(8,128)(2,1)S(1)}, u32[]{:S(2)}, u32[]{:S(2)}) collective-permute-start(bf16[5,64,256]{2,1,0:T(8,128)(2,1)S(1)} %get-tuple-element.69), channel_id=1, source_target_pairs={{0,1},{1,2},{2,3},{3,0},{4,5},{5,6},{6,7},{7,4},{8,9},{9,10},{10,1... | collective-permute-start | bytes 491528 | tf_op jit(solution)/shard_map/ppermute | solution.py:252
  287.0 10.8 %collective-permute-done.55.refs_2_.refs_1_ = bf16[256,1792]{1,0:T(8,128)(2,1)S(1)} collective-permute-done((bf16[256,1792]{1,0:T(8,128)(2,1)S(1)}, bf16[256,1792]{1,0:T(8,128)(2,1)S(1)}, u32[]{:S(2)}, u32[]{:S(2)}) %collective-permute-start.55) | collective-permute-done | bytes 917536 | tf_op jit(solution)/shard_map/ppermute | solution.py:75
  298.4 18.6 %collective-permute-done.56.refs_3_.refs_2_ = bf16[256,1792]{1,0:T(8,128)(2,1)S(1)} collective-permute-done((bf16[256,1792]{1,0:T(8,128)(2,1)S(1)}, bf16[256,1792]{1,0:T(8,128)(2,1)S(1)}, u32[]{:S(2)}, u32[]{:S(2)}) %collective-permute-start.56) | collective-permute-done | bytes 917536 | tf_op jit(solution)/shard_map/ppermute | solution.py:75
  317.0 9.9 %collective-permute-start.66 = (bf16[5,64,256]{2,1,0:T(8,128)(2,1)S(1)}, bf16[5,64,256]{2,1,0:T(8,128)(2,1)S(1)}, u32[]{:S(2)}, u32[]{:S(2)}) collective-permute-start(bf16[5,64,256]{2,1,0:T(8,128)(2,1)S(1)} %get-tuple-element.71), channel_id=1, source_target_pairs={{0,3},{1,0},{2,1},{3,2},{4,7},{5,4},{6,5},{7,6},{8,11},{9,8},{10,9... | collective-permute-start | bytes 491528 | tf_op jit(solution)/shard_map/ppermute | solution.py:252
  336.4 28.2 %collective-permute-done.92.refs_1_ = bf16[5,64,256]{2,1,0:T(8,128)(2,1)S(1)} collective-permute-done((bf16[5,64,256]{2,1,0:T(8,128)(2,1)S(1)}, bf16[5,64,256]{2,1,0:T(8,128)(2,1)S(1)}, u32[]{:S(2)}, u32[]{:S(2)}) %collective-permute-start.92) | collective-permute-done | bytes 163872 | tf_op jit(solution)/shard_map/ppermute | solution.py:252
  364.6 12.9 %collective-permute-done.93.refs_2_ = bf16[5,64,256]{2,1,0:T(8,128)(2,1)S(1)} collective-permute-done((bf16[5,64,256]{2,1,0:T(8,128)(2,1)S(1)}, bf16[5,64,256]{2,1,0:T(8,128)(2,1)S(1)}, u32[]{:S(2)}, u32[]{:S(2)}) %collective-permute-start.93) | collective-permute-done | bytes 163872 | tf_op jit(solution)/shard_map/ppermute | solution.py:252
  386.3 5.7 %collective-permute-done.68 = f32[8,128]{1,0:T(8,128)S(1)} collective-permute-done((f32[8,128]{1,0:T(8,128)S(1)}, f32[8,128]{1,0:T(8,128)S(1)}, u32[]{:S(2)}, u32[]{:S(2)}) %collective-permute-start.68) | collective-permute-done | bytes 4128 | tf_op jit(solution)/shard_map/ppermute | solution.py:75
  408.5 18.0 %collective-permute-done.76.refs_2_ = bf16[3,128,512]{2,1,0:T(8,128)(2,1)S(1)} collective-permute-done((bf16[3,128,512]{2,1,0:T(8,128)(2,1)S(1)}, bf16[3,128,512]{2,1,0:T(8,128)(2,1)S(1)}, u32[]{:S(2)}, u32[]{:S(2)}) %collective-permute-start.76) | collective-permute-done | bytes 393248 | tf_op jit(solution)/shard_map/ppermute | solution.py:252
  427.9 7.0 %collective-permute-done.80.refs_4_ = bf16[2,128,512]{2,1,0:T(8,128)(2,1)S(1)} collective-permute-done((bf16[2,128,512]{2,1,0:T(8,128)(2,1)S(1)}, bf16[2,128,512]{2,1,0:T(8,128)(2,1)S(1)}, u32[]{:S(2)}, u32[]{:S(2)}) %collective-permute-start.80) | collective-permute-done | bytes 262176 | tf_op jit(solution)/shard_map/ppermute | solution.py:75
  451.3 5.3 collective-permute-done.83.refs_7_
  473.1 19.6 %collective-permute-done.102.refs_2_ = bf16[256,1792]{1,0:T(8,128)(2,1)S(1)} collective-permute-done((bf16[256,1792]{1,0:T(8,128)(2,1)S(1)}, bf16[256,1792]{1,0:T(8,128)(2,1)S(1)}, u32[]{:S(2)}, u32[]{:S(2)}) %collective-permute-start.102) | collective-permute-done | bytes 917536 | tf_op jit(solution)/shard_map/ppermute | solution.py:75
  492.7 18.8 %collective-permute-done.98.refs_3_ = bf16[256,1792]{1,0:T(8,128)(2,1)S(1)} collective-permute-done((bf16[256,1792]{1,0:T(8,128)(2,1)S(1)}, bf16[256,1792]{1,0:T(8,128)(2,1)S(1)}, u32[]{:S(2)}, u32[]{:S(2)}) %collective-permute-start.98) | collective-permute-done | bytes 917536 | tf_op jit(solution)/shard_map/ppermute | solution.py:75
  514.0 19.6 %collective-permute-done.99.refs_5_ = bf16[256,1792]{1,0:T(8,128)(2,1)S(1)} collective-permute-done((bf16[256,1792]{1,0:T(8,128)(2,1)S(1)}, bf16[256,1792]{1,0:T(8,128)(2,1)S(1)}, u32[]{:S(2)}, u32[]{:S(2)}) %collective-permute-start.99) | collective-permute-done | bytes 917536 | tf_op jit(solution)/shard_map/ppermute | solution.py:75
  (253 shorter events, 204.9 us)
Async XLA Ops:
  8.6 39.1 %collective-permute-start = (bf16[256,1792]{1,0:T(8,128)(2,1)S(1)}, bf16[256,1792]{1,0:T(8,128)(2,1)}, u32[]{:S(2)}, u32[]{:S(2)}) collective-permute-start(bf16[256,1792]{1,0:T(8,128)(2,1)S(1)} %get-tuple-element.83.refs_0_.top.refs_2_.refs_12_.refs_7_), channel_id=1, source_target_pairs={{8,0},{12,4},{4,8},{0,12},{24,16},{28,20},{20,24},{16,28},{9,1},{1... | collective-permute-start | bytes 2752520 | tf_op jit(solution)/shard_map/ppermute | solution.py:75
  9.6 40.0 %collective-permute-start.3 = (bf16[256,1792]{1,0:T(8,128)(2,1)S(1)}, bf16[256,1792]{1,0:T(8,128)(2,1)}, u32[]{:S(2)}, u32[]{:S(2)}) collective-permute-start(bf16[256,1792]{1,0:T(8,128)(2,1)S(1)} %get-tuple-element.82.refs_1_.bottom.refs_3_.refs_13_.refs_8_), channel_id=1, source_target_pairs={{16,0},{20,4},{28,8},{24,12},{4,16},{0,20},{8,24},{12,28},{17,1},{... | collective-permute-start | bytes 2752520 | tf_op jit(solution)/shard_map/ppermute | solution.py:75
  14.1 44.7 %collective-permute-start.10 = (bf16[5,64,256]{2,1,0:T(8,128)(2,1)S(1)}, bf16[5,64,256]{2,1,0:T(8,128)(2,1)S(1)}, u32[]{:S(2)}, u32[]{:S(2)}) collective-permute-start(bf16[5,64,256]{2,1,0:T(8,128)(2,1)S(1)} %get-tuple-element.50), channel_id=1, source_target_pairs={{0,2},{1,3},{2,0},{3,1},{4,6},{5,7},{6,4},{7,5},{8,10},{9,11},{10,... | collective-permute-start | bytes 491528 | tf_op jit(solution)/shard_map/ppermute | solution.py:252
  54.6 52.1 %collective-permute-start.4 = (bf16[3,128,512]{2,1,0:T(8,128)(2,1)S(1)}, bf16[3,128,512]{2,1,0:T(8,128)(2,1)S(1)}, u32[]{:S(2)}, u32[]{:S(2)}) collective-permute-start(bf16[3,128,512]{2,1,0:T(8,128)(2,1)S(1)} %get-tuple-element.45), channel_id=1, source_target_pairs={{0,1},{1,2},{2,3},{3,0},{4,5},{5,6},{6,7},{7,4},{8,9},{9,10},{10,1... | collective-permute-start | bytes 1179656 | tf_op jit(solution)/shard_map/ppermute | solution.py:252
  56.2 50.5 %collective-permute-start.5 = (bf16[3,128,512]{2,1,0:T(8,128)(2,1)S(1)}, bf16[3,128,512]{2,1,0:T(8,128)(2,1)S(1)}, u32[]{:S(2)}, u32[]{:S(2)}) collective-permute-start(bf16[3,128,512]{2,1,0:T(8,128)(2,1)S(1)} %get-tuple-element.46), channel_id=1, source_target_pairs={{0,2},{1,3},{2,0},{3,1},{4,6},{5,7},{6,4},{7,5},{8,10},{9,11},{10,... | collective-permute-start | bytes 1179656 | tf_op jit(solution)/shard_map/ppermute | solution.py:252
  58.8 47.9 %collective-permute-start.6 = (bf16[3,128,512]{2,1,0:T(8,128)(2,1)S(1)}, bf16[3,128,512]{2,1,0:T(8,128)(2,1)S(1)}, u32[]{:S(2)}, u32[]{:S(2)}) collective-permute-start(bf16[3,128,512]{2,1,0:T(8,128)(2,1)S(1)} %get-tuple-element.47), channel_id=1, source_target_pairs={{0,3},{1,0},{2,1},{3,2},{4,7},{5,4},{6,5},{7,6},{8,11},{9,8},{10,9... | collective-permute-start | bytes 1179656 | tf_op jit(solution)/shard_map/ppermute | solution.py:252
  61.0 42.0 %collective-permute-start.38 = (bf16[5,64,256]{2,1,0:T(8,128)(2,1)S(1)}, bf16[5,64,256]{2,1,0:T(8,128)(2,1)S(1)}, u32[]{:S(2)}, u32[]{:S(2)}) collective-permute-start(bf16[5,64,256]{2,1,0:T(8,128)(2,1)S(1)} %get-tuple-element.57.refs_0_), channel_id=1, source_target_pairs={{0,2},{1,3},{2,0},{3,1},{4,6},{5,7},{6,4},{7,5},{8,10},{9,11},{10,... | collective-permute-start | bytes 491528 | tf_op jit(solution)/shard_map/ppermute | solution.py:252
  198.2 41.7 %collective-permute-start.43 = (bf16[256,1792]{1,0:T(8,128)(2,1)S(1)}, bf16[256,1792]{1,0:T(8,128)(2,1)S(1)}, u32[]{:S(2)}, u32[]{:S(2)}) collective-permute-start(bf16[256,1792]{1,0:T(8,128)(2,1)S(1)} %get-tuple-element.61.refs_3_), channel_id=1, source_target_pairs={{8,0},{12,4},{4,8},{0,12},{24,16},{28,20},{20,24},{16,28},{9,1},{1... | collective-permute-start | bytes 2752520 | tf_op jit(solution)/shard_map/ppermute | solution.py:75
  199.3 41.0 %collective-permute-start.41 = (bf16[256,1792]{1,0:T(8,128)(2,1)S(1)}, bf16[256,1792]{1,0:T(8,128)(2,1)S(1)}, u32[]{:S(2)}, u32[]{:S(2)}) collective-permute-start(bf16[256,1792]{1,0:T(8,128)(2,1)S(1)} %get-tuple-element.60.refs_2_), channel_id=1, source_target_pairs={{16,0},{20,4},{28,8},{24,12},{4,16},{0,20},{8,24},{12,28},{17,1},{... | collective-permute-start | bytes 2752520 | tf_op jit(solution)/shard_map/ppermute | solution.py:75
  200.1 41.1 %collective-permute-start.54 = (bf16[256,1792]{1,0:T(8,128)(2,1)S(1)}, bf16[256,1792]{1,0:T(8,128)(2,1)S(1)}, u32[]{:S(2)}, u32[]{:S(2)}) collective-permute-start(bf16[256,1792]{1,0:T(8,128)(2,1)S(1)} %get-tuple-element.61.refs_3_), channel_id=1, source_target_pairs={{0,4},{4,0},{8,12},{12,8},{16,20},{20,16},{24,28},{28,24},{1,5},{5... | collective-permute-start | bytes 2752520 | tf_op jit(solution)/shard_map/ppermute | solution.py:75
  200.1 41.9 %collective-permute-start.48 = (bf16[256,1792]{1,0:T(8,128)(2,1)S(1)}, bf16[256,1792]{1,0:T(8,128)(2,1)S(1)}, u32[]{:S(2)}, u32[]{:S(2)}) collective-permute-start(bf16[256,1792]{1,0:T(8,128)(2,1)S(1)} %get-tuple-element.61.refs_3_), channel_id=1, source_target_pairs={{16,0},{20,4},{28,8},{24,12},{4,16},{0,20},{8,24},{12,28},{17,1},{... | collective-permute-start | bytes 2752520 | tf_op jit(solution)/shard_map/ppermute | solution.py:75
  275.5 41.5 %collective-permute-start.56 = (bf16[256,1792]{1,0:T(8,128)(2,1)S(1)}, bf16[256,1792]{1,0:T(8,128)(2,1)S(1)}, u32[]{:S(2)}, u32[]{:S(2)}) collective-permute-start(bf16[256,1792]{1,0:T(8,128)(2,1)S(1)} %get-tuple-element.63.refs_1_.bottom.refs_3_.refs_13_.refs_8_), channel_id=1, source_target_pairs={{8,0},{12,4},{4,8},{0,12},{24,16},{28,20},{20,24},{16,28},{9,1},{1... | collective-permute-start | bytes 2752520 | tf_op jit(solution)/shard_map/ppermute | solution.py:75
  276.4 50.5 %collective-permute-start.57 = (bf16[256,1792]{1,0:T(8,128)(2,1)S(1)}, bf16[256,1792]{1,0:T(8,128)(2,1)S(1)}, u32[]{:S(2)}, u32[]{:S(2)}) collective-permute-start(bf16[256,1792]{1,0:T(8,128)(2,1)S(1)} %get-tuple-element.62.refs_0_.top.refs_2_.refs_12_.refs_7_), channel_id=1, source_target_pairs={{16,0},{20,4},{28,8},{24,12},{4,16},{0,20},{8,24},{12,28},{17,1},{... | collective-permute-start | bytes 2752520 | tf_op jit(solution)/shard_map/ppermute | solution.py:75
  277.2 49.8 %collective-permute-start.58 = (bf16[256,1792]{1,0:T(8,128)(2,1)S(1)}, bf16[256,1792]{1,0:T(8,128)(2,1)S(1)}, u32[]{:S(2)}, u32[]{:S(2)}) collective-permute-start(bf16[256,1792]{1,0:T(8,128)(2,1)S(1)} %get-tuple-element.63.refs_1_.bottom.refs_3_.refs_13_.refs_8_), channel_id=1, source_target_pairs={{16,0},{20,4},{28,8},{24,12},{4,16},{0,20},{8,24},{12,28},{17,1},{... | collective-permute-start | bytes 2752520 | tf_op jit(solution)/shard_map/ppermute | solution.py:75
  279.8 52.8 %collective-permute-start.64 = (bf16[5,64,256]{2,1,0:T(8,128)(2,1)S(1)}, bf16[5,64,256]{2,1,0:T(8,128)(2,1)S(1)}, u32[]{:S(2)}, u32[]{:S(2)}) collective-permute-start(bf16[5,64,256]{2,1,0:T(8,128)(2,1)S(1)} %get-tuple-element.69), channel_id=1, source_target_pairs={{0,1},{1,2},{2,3},{3,0},{4,5},{5,6},{6,7},{7,4},{8,9},{9,10},{10,1... | collective-permute-start | bytes 491528 | tf_op jit(solution)/shard_map/ppermute | solution.py:252
  297.9 36.2 %collective-permute-start.65 = (bf16[5,64,256]{2,1,0:T(8,128)(2,1)S(1)}, bf16[5,64,256]{2,1,0:T(8,128)(2,1)S(1)}, u32[]{:S(2)}, u32[]{:S(2)}) collective-permute-start(bf16[5,64,256]{2,1,0:T(8,128)(2,1)S(1)} %get-tuple-element.70), channel_id=1, source_target_pairs={{0,2},{1,3},{2,0},{3,1},{4,6},{5,7},{6,4},{7,5},{8,10},{9,11},{10,... | collective-permute-start | bytes 491528 | tf_op jit(solution)/shard_map/ppermute | solution.py:252
  330.2 50.9 %collective-permute-start.59 = (bf16[3,128,512]{2,1,0:T(8,128)(2,1)S(1)}, bf16[3,128,512]{2,1,0:T(8,128)(2,1)S(1)}, u32[]{:S(2)}, u32[]{:S(2)}) collective-permute-start(bf16[3,128,512]{2,1,0:T(8,128)(2,1)S(1)} %get-tuple-element.65), channel_id=1, source_target_pairs={{0,1},{1,2},{2,3},{3,0},{4,5},{5,6},{6,7},{7,4},{8,9},{9,10},{10,1... | collective-permute-start | bytes 1179656 | tf_op jit(solution)/shard_map/ppermute | solution.py:252
  330.3 50.9 %collective-permute-start.60 = (bf16[3,128,512]{2,1,0:T(8,128)(2,1)S(1)}, bf16[3,128,512]{2,1,0:T(8,128)(2,1)S(1)}, u32[]{:S(2)}, u32[]{:S(2)}) collective-permute-start(bf16[3,128,512]{2,1,0:T(8,128)(2,1)S(1)} %get-tuple-element.66), channel_id=1, source_target_pairs={{0,2},{1,3},{2,0},{3,1},{4,6},{5,7},{6,4},{7,5},{8,10},{9,11},{10,... | collective-permute-start | bytes 1179656 | tf_op jit(solution)/shard_map/ppermute | solution.py:252
  332.6 48.6 %collective-permute-start.61 = (bf16[3,128,512]{2,1,0:T(8,128)(2,1)S(1)}, bf16[3,128,512]{2,1,0:T(8,128)(2,1)S(1)}, u32[]{:S(2)}, u32[]{:S(2)}) collective-permute-start(bf16[3,128,512]{2,1,0:T(8,128)(2,1)S(1)} %get-tuple-element.67), channel_id=1, source_target_pairs={{0,3},{1,0},{2,1},{3,2},{4,7},{5,4},{6,5},{7,6},{8,11},{9,8},{10,9... | collective-permute-start | bytes 1179656 | tf_op jit(solution)/shard_map/ppermute | solution.py:252
  334.9 42.6 %collective-permute-start.93 = (bf16[5,64,256]{2,1,0:T(8,128)(2,1)S(1)}, bf16[5,64,256]{2,1,0:T(8,128)(2,1)S(1)}, u32[]{:S(2)}, u32[]{:S(2)}) collective-permute-start(bf16[5,64,256]{2,1,0:T(8,128)(2,1)S(1)} %get-tuple-element.77.refs_0_), channel_id=1, source_target_pairs={{0,2},{1,3},{2,0},{3,1},{4,6},{5,7},{6,4},{7,5},{8,10},{9,11},{10,... | collective-permute-start | bytes 491528 | tf_op jit(solution)/shard_map/ppermute | solution.py:252
  469.5 42.0 %collective-permute-start.98 = (bf16[256,1792]{1,0:T(8,128)(2,1)S(1)}, bf16[256,1792]{1,0:T(8,128)(2,1)S(1)}, u32[]{:S(2)}, u32[]{:S(2)}) collective-permute-start(bf16[256,1792]{1,0:T(8,128)(2,1)S(1)} %get-tuple-element.81.refs_3_), channel_id=1, source_target_pairs={{8,0},{12,4},{4,8},{0,12},{24,16},{28,20},{20,24},{16,28},{9,1},{1... | collective-permute-start | bytes 2752520 | tf_op jit(solution)/shard_map/ppermute | solution.py:75
  470.9 41.2 %collective-permute-start.96 = (bf16[256,1792]{1,0:T(8,128)(2,1)S(1)}, bf16[256,1792]{1,0:T(8,128)(2,1)S(1)}, u32[]{:S(2)}, u32[]{:S(2)}) collective-permute-start(bf16[256,1792]{1,0:T(8,128)(2,1)S(1)} %get-tuple-element.80.refs_2_), channel_id=1, source_target_pairs={{16,0},{20,4},{28,8},{24,12},{4,16},{0,20},{8,24},{12,28},{17,1},{... | collective-permute-start | bytes 2752520 | tf_op jit(solution)/shard_map/ppermute | solution.py:75
  471.8 40.3 %collective-permute-start.109 = (bf16[256,1792]{1,0:T(8,128)(2,1)S(1)}, bf16[256,1792]{1,0:T(8,128)(2,1)S(1)}, u32[]{:S(2)}, u32[]{:S(2)}) collective-permute-start(bf16[256,1792]{1,0:T(8,128)(2,1)S(1)} %get-tuple-element.81.refs_3_), channel_id=1, source_target_pairs={{0,4},{4,0},{8,12},{12,8},{16,20},{20,16},{24,28},{28,24},{1,5},{5... | collective-permute-start | bytes 2752520 | tf_op jit(solution)/shard_map/ppermute | solution.py:75
  471.8 41.7 %collective-permute-start.103 = (bf16[256,1792]{1,0:T(8,128)(2,1)S(1)}, bf16[256,1792]{1,0:T(8,128)(2,1)S(1)}, u32[]{:S(2)}, u32[]{:S(2)}) collective-permute-start(bf16[256,1792]{1,0:T(8,128)(2,1)S(1)} %get-tuple-element.81.refs_3_), channel_id=1, source_target_pairs={{16,0},{20,4},{28,8},{24,12},{4,16},{0,20},{8,24},{12,28},{17,1},{... | collective-permute-start | bytes 2752520 | tf_op jit(solution)/shard_map/ppermute | solution.py:75
  (91 other events, 1643.5 us)

commit v3 on v2

--- a/solution.py
+++ b/solution.py
@@ -114,18 +114,35 @@
     split_rows(total, size, z_ref[0], kept, pieces)
 
 
-def far_gram_kernel(size, z_ref, *refs):
-    halves, (kept, *pieces), total = refs[:6], refs[6:-1], refs[-1]
-    for p, (left, right) in enumerate([(0, 1), (1, 2), (0, 2)]):
-        value = jnp.concatenate([halves[2 * left][...], halves[2 * left + 1][...]], axis=0)
-        half = value.shape[0] // 2
-        for h in range(2):
-            total[p, :, h * half : (h + 1) * half] = dot_nt(value, halves[2 * right + h][...])
+def stacked(top, bottom):
+    return jnp.concatenate([top[...], bottom[...]], axis=0)
+
+
+def early_gram_kernel(size, z_ref, top, bottom, x_bottom, y_top, kept, *rest):
+    pieces, total = rest[:-1], rest[-1]
+    half = top.shape[0]
+    own = stacked(top, bottom)
+    for q, right in ((0, x_bottom), (3, y_top)):
+        value = dot_nt(own, right[...])
+        total[q], total[q + 1] = value[:half], value[half:]
+    total[2] = dot_nt(x_bottom[...], y_top[...])
     split_rows(total, size, z_ref[0], kept, pieces)
 
 
-def gram(kernel, shape, size, scalars, blocks):
-    halves = [half for block in blocks for half in block]
+def late_gram_kernel(size, z_ref, top, bottom, x_top, x_bottom, y_top, y_bottom, kept, *rest):
+    pieces, total = rest[:-1], rest[-1]
+    half = top.shape[0]
+    own = stacked(top, bottom)
+    for q, right in ((0, x_top), (5, y_bottom)):
+        value = dot_nt(own, right[...])
+        total[q], total[q + 1] = value[:half], value[half:]
+    total[2] = dot_nt(x_top[...], y_top[...])
+    value = dot_nt(stacked(x_top, x_bottom), y_bottom[...])
+    total[3], total[4] = value[:half], value[half:]
+    split_rows(total, size, z_ref[0], kept, pieces)
+
+
+def gram(kernel, shape, size, scalars, halves):
     count, rows, columns = shape
     shape = (count, rows // size, columns)
     outs = [jax.ShapeDtypeStruct(shape, f32)] + [jax.ShapeDtypeStruct(shape, bf16)] * (size - 1)
@@ -178,27 +195,68 @@
     return call(beside_kernel, [jax.ShapeDtypeStruct((rows, rows), bf16)], [own, other], [core])[0]
 
 
-def assemble_kernel(takes, size, z_ref, *refs):
-    groups, outs = refs[: len(refs) - len(takes)], refs[len(refs) - len(takes) :]
-    z = z_ref[0]
-    rows = groups[0].shape[1]
-    columns = groups[0].shape[2]
-    for out, taken in zip(outs, takes):
-        for k, (group, index, transposed) in enumerate(taken):
-            for by in range(size):
-                part = groups[group * size + by][index]
-                at = pl.multiple_of(lax.rem(z + size - by, size) * rows, rows)
-                if transposed:
-                    out[:, pl.ds(pl.multiple_of(k * columns + at, rows), rows)] = part.T
-                else:
-                    out[pl.ds(at, rows), k * columns : (k + 1) * columns] = part
-
-
-def assemble(z, size, groups, takes):
-    parts = [part for group in groups for part in group]
-    columns = parts[0].shape[2]
-    outs = [jax.ShapeDtypeStruct((columns, columns * len(taken)), bf16) for taken in takes]
-    return call(functools.partial(assemble_kernel, takes, size), outs, parts, [z])
+def rows_at(z, by, size, rows):
+    return pl.multiple_of(lax.rem(z + size - by, size) * rows, rows)
+
+
+def near_assemble_kernel(size, z_ref, *refs):
+    parts, near, wholes = refs[:size], refs[size], refs[size + 1 :]
+    count, rows, half = parts[0].shape
+    for by, part in enumerate(parts):
+        at = rows_at(z_ref[0], by, size, rows)
+        lower = pl.multiple_of(half + at, rows)
+        near[pl.ds(at, rows), :half] = part[0]
+        near[pl.ds(lower, rows), :half] = part[1]
+        near[pl.ds(at, rows), half:] = part[count - 2]
+        near[pl.ds(lower, rows), half:] = part[count - 1]
+        for k, whole in enumerate(wholes):
+            whole[:, pl.ds(at, rows), :] = part[2 * k : count - 2 + 2 * k]
+
+
+def near_assemble(z, size, parts, with_wholes):
+    count, _, half = parts[0].shape
+    outs = [jax.ShapeDtypeStruct((2 * half, 2 * half), bf16)]
+    if with_wholes:
+        outs += [jax.ShapeDtypeStruct((count - 2, half, half), bf16)] * 2
+    return call(functools.partial(near_assemble_kernel, size), outs, parts, [z])
+
+
+def mirror_assemble_kernel(size, z_ref, *refs):
+    (x_early, y_early), refs = refs[:2], refs[2:]
+    x_parts, y_parts, refs = refs[:size], refs[size : 2 * size], refs[2 * size :]
+    side, linked, crossed, x_late, y_late = refs
+    rows, half = x_parts[0].shape[1:]
+    for by in range(size):
+        at = pl.ds(rows_at(z_ref[0], by, size, rows), rows)
+        x_late[:, at, :] = x_parts[by][...]
+        y_late[:, at, :] = y_parts[by][...]
+    columns = [slice(k * half, (k + 1) * half) for k in range(4)]
+    top, bottom = columns[0], columns[1]
+    for k in range(2):
+        side[top, columns[k]] = x_late[k].T
+        side[bottom, columns[k]] = x_early[k].T
+        side[top, columns[2 + k]] = y_early[1 + k].T
+        side[bottom, columns[2 + k]] = y_late[3 + k].T
+    linked[top, top] = x_late[2]
+    linked[bottom, top] = x_early[2]
+    linked[top, bottom] = y_early[0].T
+    linked[bottom, bottom] = y_late[2].T
+    crossed[top, top] = x_late[3]
+    crossed[bottom, top] = x_late[4]
+    crossed[top, bottom] = y_late[0].T
+    crossed[bottom, bottom] = y_late[1].T
+
+
+def mirror_assemble(z, size, early, x_parts, y_parts):
+    count, _, half = x_parts[0].shape
+    outs = [jax.ShapeDtypeStruct((2 * half, width * half), bf16) for width in (4, 2, 2)]
+    return call(
+        functools.partial(mirror_assemble_kernel, size),
+        outs,
+        [*early, *x_parts, *y_parts],
+        [z],
+        [pltpu.VMEM((count, half, half), bf16)] * 2,
+    )
 
 
 def product_kernel(n_grams, n_halves, has_sum, finish, tile, *refs):
@@ -230,11 +288,10 @@
     lax.fori_loop(0, columns // tile, column_tile, 0)
 
 
-def product(grams, blocks, summed=None, finish=None, dtype=f32, parts=1):
-    halves = [half for block in blocks for half in block]
+def product(grams, halves, summed=None, finish=None, dtype=f32, parts=1):
     half, columns = halves[0].shape
     tile = 256 if columns % 256 == 0 else columns
-    args = ([finish[1]] if finish else []) + list(grams) + halves
+    args = ([finish[1]] if finish else []) + list(grams) + list(halves)
     args += [] if summed is None else [summed]
     args += list(finish[2]) if finish else []
     outs = [jax.ShapeDtypeStruct((2 * half // parts, columns), dtype)] * parts
@@ -264,11 +321,9 @@
     x_top, y_bottom = over_dp(top, TAKE_X), over_dp(bottom, TAKE_Y)
     core = over_dp(top, CORE), over_dp(bottom, CORE)
     d_oth_bottom, d_sel_top = over_dp(x_bottom, GIVE_Y), over_dp(y_top, GIVE_X)
-    x_oth = over_dp(x_top, CORE), over_dp(x_bottom, CORE)
-    y_oth = over_dp(y_top, CORE), over_dp(y_bottom, CORE)
-    d_oth_top, d_sel_bottom = over_dp(d_sel_top, CORE), over_dp(d_oth_bottom, CORE)
-    near = core, (x_top, x_bottom), (y_top, y_bottom)
-    return near, (x_oth, y_oth, (d_sel_top, d_sel_bottom), (d_oth_top, d_oth_bottom))
+    side = [over_dp(half, CORE) for half in (x_top, x_bottom, y_top, y_bottom)]
+    crossed = over_dp(d_oth_bottom, CORE), over_dp(d_sel_top, CORE)
+    return core, (x_bottom, y_top), (x_top, y_bottom), side, (d_sel_top, d_oth_bottom), crossed
 
 
 def fold_kernel(weights, *refs):
@@ -303,30 +358,31 @@
 def iterate_square(matrix, size, gain, dtype, parts):
     z = lax.axis_index("shard").reshape(1)
     side_index = (lax.axis_index("dp") & 1).reshape(1)
-    (core, x_sel, y_sel), (x_oth, y_oth, d_sel, d_oth) = gather(matrix)
+    core, one, two, side, linked, crossed = gather(matrix)
+    (x_bottom, y_top), (x_top, y_bottom) = one, two
     half = matrix[0].shape[0]
-    own_pieces = gram(own_gram_kernel, (5, half, half), size, [z, side_index], [matrix, core])
+    own_pieces = gram(own_gram_kernel, (5, half, half), size, [z, side_index], [*matrix, *core])
     own_part, squares = reduce_parts(
         own_pieces, size, jnp.zeros((8, 128), f32), (1.0, 1.0, 2.0, 2.0, 2.0)
     )
     own_parts = spread(own_part, size)
-    far_pieces = gram(far_gram_kernel, (3, 2 * half, 2 * half), size, [z], [matrix, x_sel, y_sel])
-    far_part, squares = reduce_parts(far_pieces, size, squares, (2.0, 2.0, 2.0))
+    early_pieces = gram(early_gram_kernel, (5, half, half), size, [z], [*matrix, x_bottom, y_top])
+    early_part, squares = reduce_parts(early_pieces, size, squares, (2.0,) * 5)
+    late_pieces = gram(
+        late_gram_kernel, (7, half, half), size, [z], [*matrix, x_top, x_bottom, y_top, y_bottom]
+    )
+    late_part, squares = reduce_parts(late_pieces, size, squares, (2.0,) * 7)
     squares = total_of(squares, size)
-    far_parts = spread(far_part, size)
-    x_parts = [over_dp(p[:2], GIVE_X) for p in far_parts]
-    y_parts = [over_dp(p[1:], GIVE_Y) for p in far_parts]
+    early_parts = spread(early_part, size)
+    late_parts = spread(late_part, size)
+    near_one, x_whole, y_whole = near_assemble(z, size, early_parts, True)
+    early = over_dp(x_whole, GIVE_X), over_dp(y_whole, GIVE_Y)
+    x_parts = [over_dp(p[:-2], GIVE_X) for p in late_parts]
+    y_parts = [over_dp(p[2:], GIVE_Y) for p in late_parts]
     own, beside = own_assemble(z, size, own_parts)
     beside = beside_of(side_index, beside, over_dp(beside, CORE))
-    (far,) = assemble(z, size, [far_parts], [[(0, 0, False), (0, 2, False)]])
-    side, diagonal = assemble(
-        z,
-        size,
-        [x_parts, y_parts],
-        [[(0, 0, True), (1, 1, True)], [(0, 1, False), (1, 0, True)]],
-    )
-    (first,) = product([own, beside], [matrix, core])
-    (first,) = product([far], [x_sel, y_sel], first)
+    (near_two,) = near_assemble(z, size, late_parts, False)
+    side_gram, linked_gram, crossed_gram = mirror_assemble(z, size, early, x_parts, y_parts)
 
     def mixing(root_scale, inverse_norm):
         return cubic_term * root_scale, quintic_term * root_scale * inverse_norm
@@ -334,13 +390,21 @@
     def ending(root_scale, inverse_norm):
         return gain * linear_term * root_scale, gain * inverse_norm
 
+    (first,) = product([own, beside], [*matrix, *core])
+    (first,) = product([near_one, near_two], [*one, *two], first)
     mixture = product(
-        [side, diagonal], [x_oth, y_oth, d_sel, d_oth], first, (mixing, squares, matrix), bf16, 2
-    )
-    (core, x_sel, y_sel), (x_oth, y_oth, d_sel, d_oth) = gather(mixture)
-    (second,) = product([own, beside], [mixture, core])
-    (second,) = product([far, side], [x_sel, y_sel, x_oth, y_oth], second)
-    return product([diagonal], [d_sel, d_oth], second, (ending, squares, matrix), dtype, parts)
+        [side_gram, linked_gram, crossed_gram],
+        [*side, *linked, *crossed],
+        first,
+        (mixing, squares, matrix),
+        bf16,
+        2,
+    )
+    core, one, two, side, linked, crossed = gather(mixture)
+    (second,) = product([own, beside], [*mixture, *core])
+    (second,) = product([near_one, near_two, side_gram], [*one, *two, *side], second)
+    (second,) = product([linked_gram], linked, second)
+    return product([crossed_gram], crossed, second, (ending, squares, matrix), dtype, parts)
 
 
 def current_of(momentum, gradient):

time: 556 us -> 576 us (1.036)
  starting transfers between devices: 97.8 us -> 198 us
  waiting for transfers between devices: 377 us -> 297 us
    ppermute x30 -> x42, waiting for transfers between devices: 137 us -> 53 us  [shifted(): lax.ppermute(value, 'shard', [(z, (z + by) % size) for z in range(size)])]
    ppermute x30 -> x42, starting transfers between devices: 51.4 us -> 123 us  [shifted(): lax.ppermute(value, 'shard', [(z, (z + by) % size) for z in range(size)])]
    ppermute x80 -> x84, starting transfers between devices: 46.5 us -> 74.9 us  [over_dp(): return lax.ppermute(value, 'dp', pairs)]
    pallas_call x28 -> x36, Pallas kernels: 65.8 us -> 69.9 us  [call(): pl.pallas_call(kernel, out_shape=outs, in_specs=[pl.BlockSpec(memory_spac...]
    ppermute x80 -> x84, waiting for transfers between devices: 240 us -> 244 us  [over_dp(): return lax.ppermute(value, 'dp', pairs)]
  transfers between devices with their start and end apart: 110 -> 126, of which waited for: 45 -> 48; matrix products, arithmetic and copies ran while one was open for 0% -> 0% of each run, Pallas kernels for 9% -> 9%
where the time goes in v3:
time: 576 us; the launch traced here: 574 us
  waiting for transfers between devices  297 us (52%)
  starting transfers between devices  198 us (34%)
  Pallas kernels  69.9 us (12%)
    ppermute x84, waiting for transfers between devices, over_dp(): return lax.ppermute(value, 'dp', pairs)  244 us
    ppermute x42, starting transfers between devices, shifted(): lax.ppermute(value, 'shard', [(z, (z + by) % size) for z in range(size)])  123 us
    ppermute x84, starting transfers between devices, over_dp(): return lax.ppermute(value, 'dp', pairs)  74.9 us
    pallas_call x36, Pallas kernels, call(): pl.pallas_call(kernel, out_shape=outs, in_specs=[pl.BlockSpec(memory_spac...  69.9 us
    ppermute x42, waiting for transfers between devices, shifted(): lax.ppermute(value, 'shard', [(z, (z + by) % size) for z in range(size)])  53 us
  transfers between devices with their start and end apart: 126, of which 48 were waited for; matrix products, arithmetic and copies ran while one was open for 0% of the time, Pallas kernels for 9%

profile of v3, /device:TPU:0, one launch (start us, length us, event | category | flops | bytes accessed | tf_op | source)
XLA Modules:
  0.0 573.5 jit_solution(2622744522963973485)
XLA Ops:
  15.8 12.9 %collective-permute-done.1.x_bottom.refs_2_ = bf16[256,1792]{1,0:T(8,128)(2,1)} collective-permute-done((bf16[256,1792]{1,0:T(8,128)(2,1)S(1)}, bf16[256,1792]{1,0:T(8,128)(2,1)}, u32[]{:S(2)}, u32[]{:S(2)}) %collective-permute-start.1) | collective-permute-done | bytes 917536 | tf_op jit(solution)/shard_map/ppermute | solution.py:75
  36.6 11.1 %collective-permute-done.x_top.refs_4_ = bf16[256,1792]{1,0:T(8,128)(2,1)} collective-permute-done((bf16[256,1792]{1,0:T(8,128)(2,1)S(1)}, bf16[256,1792]{1,0:T(8,128)(2,1)}, u32[]{:S(2)}, u32[]{:S(2)}) %collective-permute-start) | collective-permute-done | bytes 917536 | tf_op jit(solution)/shard_map/ppermute | solution.py:75
  62.1 10.2 %collective-permute-done.8.refs_2_ = bf16[5,64,256]{2,1,0:T(8,128)(2,1)S(1)} collective-permute-done((bf16[5,64,256]{2,1,0:T(8,128)(2,1)S(1)}, bf16[5,64,256]{2,1,0:T(8,128)(2,1)S(1)}, u32[]{:S(2)}, u32[]{:S(2)}) %collective-permute-start.8) | collective-permute-done | bytes 163872 | tf_op jit(solution)/shard_map/ppermute | solution.py:309
  72.3 11.7 %collective-permute-done.9.refs_3_ = bf16[5,64,256]{2,1,0:T(8,128)(2,1)S(1)} collective-permute-done((bf16[5,64,256]{2,1,0:T(8,128)(2,1)S(1)}, bf16[5,64,256]{2,1,0:T(8,128)(2,1)S(1)}, u32[]{:S(2)}, u32[]{:S(2)}) %collective-permute-start.9) | collective-permute-done | bytes 163872 | tf_op jit(solution)/shard_map/ppermute | solution.py:309
  107.2 11.8 %collective-permute-start.22 = (bf16[5,64,256]{2,1,0:T(8,128)(2,1)S(1)}, bf16[5,64,256]{2,1,0:T(8,128)(2,1)S(1)}, u32[]{:S(2)}, u32[]{:S(2)}) collective-permute-start(bf16[5,64,256]{2,1,0:T(8,128)(2,1)S(1)} %get-tuple-element.79.refs_0_), channel_id=1, source_target_pairs={{0,2},{1,3},{2,0},{3,1},{4,6},{5,7},{6,4},{7,5},{8,10},{9,11},{10,... | collective-permute-start | bytes 491528 | tf_op jit(solution)/shard_map/ppermute | solution.py:309
  143.3 21.1 %collective-permute-done.28.refs_3_ = bf16[5,64,256]{2,1,0:T(8,128)(2,1)S(1)} collective-permute-done((bf16[5,64,256]{2,1,0:T(8,128)(2,1)S(1)}, bf16[5,64,256]{2,1,0:T(8,128)(2,1)S(1)}, u32[]{:S(2)}, u32[]{:S(2)}) %collective-permute-start.28) | collective-permute-done | bytes 163872 | tf_op jit(solution)/shard_map/ppermute | solution.py:75
  182.4 5.4 collective-permute-done.24.refs_0_
  202.4 5.2 shard_map.54
  212.2 19.1 %collective-permute-done.55.refs_5_ = bf16[256,1792]{1,0:T(8,128)(2,1)S(1)} collective-permute-done((bf16[256,1792]{1,0:T(8,128)(2,1)S(1)}, bf16[256,1792]{1,0:T(8,128)(2,1)S(1)}, u32[]{:S(2)}, u32[]{:S(2)}) %collective-permute-start.55) | collective-permute-done | bytes 917536 | tf_op jit(solution)/shard_map/ppermute | solution.py:75
  231.4 18.8 %collective-permute-done.49.refs_3_ = bf16[256,1792]{1,0:T(8,128)(2,1)S(1)} collective-permute-done((bf16[256,1792]{1,0:T(8,128)(2,1)S(1)}, bf16[256,1792]{1,0:T(8,128)(2,1)S(1)}, u32[]{:S(2)}, u32[]{:S(2)}) %collective-permute-start.49) | collective-permute-done | bytes 917536 | tf_op jit(solution)/shard_map/ppermute | solution.py:75
  253.5 18.4 %collective-permute-done.50.refs_2_ = bf16[256,1792]{1,0:T(8,128)(2,1)S(1)} collective-permute-done((bf16[256,1792]{1,0:T(8,128)(2,1)S(1)}, bf16[256,1792]{1,0:T(8,128)(2,1)S(1)}, u32[]{:S(2)}, u32[]{:S(2)}) %collective-permute-start.50) | collective-permute-done | bytes 917536 | tf_op jit(solution)/shard_map/ppermute | solution.py:75
  297.3 13.7 %collective-permute-done.64.x_bottom.refs_2_ = bf16[256,1792]{1,0:T(8,128)(2,1)S(1)} collective-permute-done((bf16[256,1792]{1,0:T(8,128)(2,1)S(1)}, bf16[256,1792]{1,0:T(8,128)(2,1)S(1)}, u32[]{:S(2)}, u32[]{:S(2)}) %collective-permute-start.64) | collective-permute-done | bytes 917536 | tf_op jit(solution)/shard_map/ppermute | solution.py:75
  312.1 7.0 %collective-permute-start.77 = (bf16[5,64,256]{2,1,0:T(8,128)(2,1)S(1)}, bf16[5,64,256]{2,1,0:T(8,128)(2,1)S(1)}, u32[]{:S(2)}, u32[]{:S(2)}) collective-permute-start(bf16[5,64,256]{2,1,0:T(8,128)(2,1)S(1)} %get-tuple-element.105), channel_id=1, source_target_pairs={{0,3},{1,0},{2,1},{3,2},{4,7},{5,4},{6,5},{7,6},{8,11},{9,8},{10,9... | collective-permute-start | bytes 491528 | tf_op jit(solution)/shard_map/ppermute | solution.py:309
  320.6 9.6 %collective-permute-done.63.x_top.refs_4_ = bf16[256,1792]{1,0:T(8,128)(2,1)S(1)} collective-permute-done((bf16[256,1792]{1,0:T(8,128)(2,1)S(1)}, bf16[256,1792]{1,0:T(8,128)(2,1)S(1)}, u32[]{:S(2)}, u32[]{:S(2)}) %collective-permute-start.63) | collective-permute-done | bytes 917536 | tf_op jit(solution)/shard_map/ppermute | solution.py:75
  346.7 11.6 %collective-permute-done.71.refs_2_ = bf16[5,64,256]{2,1,0:T(8,128)(2,1)S(1)} collective-permute-done((bf16[5,64,256]{2,1,0:T(8,128)(2,1)S(1)}, bf16[5,64,256]{2,1,0:T(8,128)(2,1)S(1)}, u32[]{:S(2)}, u32[]{:S(2)}) %collective-permute-start.71) | collective-permute-done | bytes 163872 | tf_op jit(solution)/shard_map/ppermute | solution.py:309
  358.3 10.5 %collective-permute-done.72.refs_3_ = bf16[5,64,256]{2,1,0:T(8,128)(2,1)S(1)} collective-permute-done((bf16[5,64,256]{2,1,0:T(8,128)(2,1)S(1)}, bf16[5,64,256]{2,1,0:T(8,128)(2,1)S(1)}, u32[]{:S(2)}, u32[]{:S(2)}) %collective-permute-start.72) | collective-permute-done | bytes 163872 | tf_op jit(solution)/shard_map/ppermute | solution.py:309
  374.7 5.7 collective-permute-start.109
  391.6 12.0 %collective-permute-start.85 = (bf16[5,64,256]{2,1,0:T(8,128)(2,1)S(1)}, bf16[5,64,256]{2,1,0:T(8,128)(2,1)S(1)}, u32[]{:S(2)}, u32[]{:S(2)}) collective-permute-start(bf16[5,64,256]{2,1,0:T(8,128)(2,1)S(1)} %get-tuple-element.109.refs_0_), channel_id=1, source_target_pairs={{0,2},{1,3},{2,0},{3,1},{4,6},{5,7},{6,4},{7,5},{8,10},{9,11},{10,... | collective-permute-start | bytes 491528 | tf_op jit(solution)/shard_map/ppermute | solution.py:309
  427.5 21.3 %collective-permute-done.91.refs_3_ = bf16[5,64,256]{2,1,0:T(8,128)(2,1)S(1)} collective-permute-done((bf16[5,64,256]{2,1,0:T(8,128)(2,1)S(1)}, bf16[5,64,256]{2,1,0:T(8,128)(2,1)S(1)}, u32[]{:S(2)}, u32[]{:S(2)}) %collective-permute-start.91) | collective-permute-done | bytes 163872 | tf_op jit(solution)/shard_map/ppermute | solution.py:75
  484.9 5.2 shard_map.72
  494.5 19.4 %collective-permute-done.118.refs_5_ = bf16[256,1792]{1,0:T(8,128)(2,1)S(1)} collective-permute-done((bf16[256,1792]{1,0:T(8,128)(2,1)S(1)}, bf16[256,1792]{1,0:T(8,128)(2,1)S(1)}, u32[]{:S(2)}, u32[]{:S(2)}) %collective-permute-start.118) | collective-permute-done | bytes 917536 | tf_op jit(solution)/shard_map/ppermute | solution.py:75
  513.9 18.8 %collective-permute-done.112.refs_3_ = bf16[256,1792]{1,0:T(8,128)(2,1)S(1)} collective-permute-done((bf16[256,1792]{1,0:T(8,128)(2,1)S(1)}, bf16[256,1792]{1,0:T(8,128)(2,1)S(1)}, u32[]{:S(2)}, u32[]{:S(2)}) %collective-permute-start.112) | collective-permute-done | bytes 917536 | tf_op jit(solution)/shard_map/ppermute | solution.py:75
  535.4 19.3 %collective-permute-done.113.refs_2_ = bf16[256,1792]{1,0:T(8,128)(2,1)S(1)} collective-permute-done((bf16[256,1792]{1,0:T(8,128)(2,1)S(1)}, bf16[256,1792]{1,0:T(8,128)(2,1)S(1)}, u32[]{:S(2)}, u32[]{:S(2)}) %collective-permute-start.113) | collective-permute-done | bytes 917536 | tf_op jit(solution)/shard_map/ppermute | solution.py:75
  562.3 5.0 shard_map.74.refs_3_
  (293 shorter events, 267.3 us)
Async XLA Ops:
  8.6 39.1 %collective-permute-start = (bf16[256,1792]{1,0:T(8,128)(2,1)S(1)}, bf16[256,1792]{1,0:T(8,128)(2,1)}, u32[]{:S(2)}, u32[]{:S(2)}) collective-permute-start(bf16[256,1792]{1,0:T(8,128)(2,1)S(1)} %get-tuple-element.123.top.refs_2_.refs_13_.refs_5_), channel_id=1, source_target_pairs={{8,0},{12,4},{4,8},{0,12},{24,16},{28,20},{20,24},{16,28},{9,1},{1... | collective-permute-start | bytes 2752520 | tf_op jit(solution)/shard_map/ppermute | solution.py:75
  9.6 40.0 %collective-permute-start.3 = (bf16[256,1792]{1,0:T(8,128)(2,1)S(1)}, bf16[256,1792]{1,0:T(8,128)(2,1)}, u32[]{:S(2)}, u32[]{:S(2)}) collective-permute-start(bf16[256,1792]{1,0:T(8,128)(2,1)S(1)} %get-tuple-element.122.bottom.refs_3_.refs_14_.refs_6_), channel_id=1, source_target_pairs={{16,0},{20,4},{28,8},{24,12},{4,16},{0,20},{8,24},{12,28},{17,1},{... | collective-permute-start | bytes 2752520 | tf_op jit(solution)/shard_map/ppermute | solution.py:75
  14.1 41.8 %collective-permute-start.12 = (bf16[5,64,256]{2,1,0:T(8,128)(2,1)S(1)}, bf16[5,64,256]{2,1,0:T(8,128)(2,1)S(1)}, u32[]{:S(2)}, u32[]{:S(2)}) collective-permute-start(bf16[5,64,256]{2,1,0:T(8,128)(2,1)S(1)} %get-tuple-element.73), channel_id=1, source_target_pairs={{0,1},{1,2},{2,3},{3,0},{4,5},{5,6},{6,7},{7,4},{8,9},{9,10},{10,1... | collective-permute-start | bytes 491528 | tf_op jit(solution)/shard_map/ppermute | solution.py:309
  28.7 28.9 %collective-permute-start.13 = (bf16[5,64,256]{2,1,0:T(8,128)(2,1)S(1)}, bf16[5,64,256]{2,1,0:T(8,128)(2,1)S(1)}, u32[]{:S(2)}, u32[]{:S(2)}) collective-permute-start(bf16[5,64,256]{2,1,0:T(8,128)(2,1)S(1)} %get-tuple-element.74), channel_id=1, source_target_pairs={{0,2},{1,3},{2,0},{3,1},{4,6},{5,7},{6,4},{7,5},{8,10},{9,11},{10,... | collective-permute-start | bytes 491528 | tf_op jit(solution)/shard_map/ppermute | solution.py:309
  137.5 54.2 %collective-permute-start.42 = (bf16[256,1792]{1,0:T(8,128)(2,1)}, bf16[256,1792]{1,0:T(8,128)(2,1)S(1)}, u32[]{:S(2)}, u32[]{:S(2)}) collective-permute-start(bf16[256,1792]{1,0:T(8,128)(2,1)} %collective-permute-done.1.x_bottom.refs_2_), channel_id=1, source_target_pairs={{0,16},{4,20},{8,28},{12,24},{16,4},{20,0},{24,8},{28,12},{1,17},{... | collective-permute-start | bytes 2752520 | tf_op jit(solution)/shard_map/ppermute | solution.py:75
  138.9 52.8 %collective-permute-start.41 = (bf16[256,1792]{1,0:T(8,128)(2,1)S(1)}, bf16[256,1792]{1,0:T(8,128)(2,1)S(1)}, u32[]{:S(2)}, u32[]{:S(2)}) collective-permute-start(bf16[256,1792]{1,0:T(8,128)(2,1)S(1)} %collective-permute-done.2.y_top.refs_3_), channel_id=1, source_target_pairs={{0,8},{4,12},{8,4},{12,0},{16,24},{20,28},{24,20},{28,16},{1,9},{5... | collective-permute-start | bytes 2752520 | tf_op jit(solution)/shard_map/ppermute | solution.py:75
  141.1 51.1 %collective-permute-start.38 = (bf16[256,1792]{1,0:T(8,128)(2,1)}, bf16[256,1792]{1,0:T(8,128)(2,1)S(1)}, u32[]{:S(2)}, u32[]{:S(2)}) collective-permute-start(bf16[256,1792]{1,0:T(8,128)(2,1)} %collective-permute-done.1.x_bottom.refs_2_), channel_id=1, source_target_pairs={{0,4},{4,0},{8,12},{12,8},{16,20},{20,16},{24,28},{28,24},{1,5},{5... | collective-permute-start | bytes 2752520 | tf_op jit(solution)/shard_map/ppermute | solution.py:75
  209.4 40.8 %collective-permute-start.49 = (bf16[256,1792]{1,0:T(8,128)(2,1)S(1)}, bf16[256,1792]{1,0:T(8,128)(2,1)S(1)}, u32[]{:S(2)}, u32[]{:S(2)}) collective-permute-start(bf16[256,1792]{1,0:T(8,128)(2,1)S(1)} %get-tuple-element.90.refs_3_), channel_id=1, source_target_pairs={{8,0},{12,4},{4,8},{0,12},{24,16},{28,20},{20,24},{16,28},{9,1},{1... | collective-permute-start | bytes 2752520 | tf_op jit(solution)/shard_map/ppermute | solution.py:75
  209.6 42.9 %collective-permute-start.52 = (bf16[256,1792]{1,0:T(8,128)(2,1)S(1)}, bf16[256,1792]{1,0:T(8,128)(2,1)S(1)}, u32[]{:S(2)}, u32[]{:S(2)}) collective-permute-start(bf16[256,1792]{1,0:T(8,128)(2,1)S(1)} %get-tuple-element.91.refs_2_), channel_id=1, source_target_pairs={{16,0},{20,4},{28,8},{24,12},{4,16},{0,20},{8,24},{12,28},{17,1},{... | collective-permute-start | bytes 2752520 | tf_op jit(solution)/shard_map/ppermute | solution.py:75
  211.8 41.1 %collective-permute-start.62 = (bf16[256,1792]{1,0:T(8,128)(2,1)S(1)}, bf16[256,1792]{1,0:T(8,128)(2,1)S(1)}, u32[]{:S(2)}, u32[]{:S(2)}) collective-permute-start(bf16[256,1792]{1,0:T(8,128)(2,1)S(1)} %get-tuple-element.90.refs_3_), channel_id=1, source_target_pairs={{0,4},{4,0},{8,12},{12,8},{16,20},{20,16},{24,28},{28,24},{1,5},{5... | collective-permute-start | bytes 2752520 | tf_op jit(solution)/shard_map/ppermute | solution.py:75
  212.0 41.0 %collective-permute-start.56 = (bf16[256,1792]{1,0:T(8,128)(2,1)S(1)}, bf16[256,1792]{1,0:T(8,128)(2,1)S(1)}, u32[]{:S(2)}, u32[]{:S(2)}) collective-permute-start(bf16[256,1792]{1,0:T(8,128)(2,1)S(1)} %get-tuple-element.90.refs_3_), channel_id=1, source_target_pairs={{16,0},{20,4},{28,8},{24,12},{4,16},{0,20},{8,24},{12,28},{17,1},{... | collective-permute-start | bytes 2752520 | tf_op jit(solution)/shard_map/ppermute | solution.py:75
  288.7 41.4 %collective-permute-start.63 = (bf16[256,1792]{1,0:T(8,128)(2,1)S(1)}, bf16[256,1792]{1,0:T(8,128)(2,1)S(1)}, u32[]{:S(2)}, u32[]{:S(2)}) collective-permute-start(bf16[256,1792]{1,0:T(8,128)(2,1)S(1)} %get-tuple-element.92.top.refs_2_.refs_13_.refs_5_), channel_id=1, source_target_pairs={{8,0},{12,4},{4,8},{0,12},{24,16},{28,20},{20,24},{16,28},{9,1},{1... | collective-permute-start | bytes 2752520 | tf_op jit(solution)/shard_map/ppermute | solution.py:75
  289.8 44.6 %collective-permute-start.66 = (bf16[256,1792]{1,0:T(8,128)(2,1)S(1)}, bf16[256,1792]{1,0:T(8,128)(2,1)S(1)}, u32[]{:S(2)}, u32[]{:S(2)}) collective-permute-start(bf16[256,1792]{1,0:T(8,128)(2,1)S(1)} %get-tuple-element.93.bottom.refs_3_.refs_14_.refs_6_), channel_id=1, source_target_pairs={{16,0},{20,4},{28,8},{24,12},{4,16},{0,20},{8,24},{12,28},{17,1},{... | collective-permute-start | bytes 2752520 | tf_op jit(solution)/shard_map/ppermute | solution.py:75
  293.0 46.9 %collective-permute-start.75 = (bf16[5,64,256]{2,1,0:T(8,128)(2,1)S(1)}, bf16[5,64,256]{2,1,0:T(8,128)(2,1)S(1)}, u32[]{:S(2)}, u32[]{:S(2)}) collective-permute-start(bf16[5,64,256]{2,1,0:T(8,128)(2,1)S(1)} %get-tuple-element.103), channel_id=1, source_target_pairs={{0,1},{1,2},{2,3},{3,0},{4,5},{5,6},{6,7},{7,4},{8,9},{9,10},{10,1... | collective-permute-start | bytes 491528 | tf_op jit(solution)/shard_map/ppermute | solution.py:309
  311.0 29.5 %collective-permute-start.76 = (bf16[5,64,256]{2,1,0:T(8,128)(2,1)S(1)}, bf16[5,64,256]{2,1,0:T(8,128)(2,1)S(1)}, u32[]{:S(2)}, u32[]{:S(2)}) collective-permute-start(bf16[5,64,256]{2,1,0:T(8,128)(2,1)S(1)} %get-tuple-element.104), channel_id=1, source_target_pairs={{0,2},{1,3},{2,0},{3,1},{4,6},{5,7},{6,4},{7,5},{8,10},{9,11},{10,... | collective-permute-start | bytes 491528 | tf_op jit(solution)/shard_map/ppermute | solution.py:309
  339.9 29.1 %collective-permute-start.67 = (bf16[7,64,256]{2,1,0:T(8,128)(2,1)S(1)}, bf16[7,64,256]{2,1,0:T(8,128)(2,1)S(1)}, u32[]{:S(2)}, u32[]{:S(2)}) collective-permute-start(bf16[7,64,256]{2,1,0:T(8,128)(2,1)S(1)} %get-tuple-element.95), channel_id=1, source_target_pairs={{0,1},{1,2},{2,3},{3,0},{4,5},{5,6},{6,7},{7,4},{8,9},{9,10},{10,1... | collective-permute-start | bytes 688136 | tf_op jit(solution)/shard_map/ppermute | solution.py:309
  340.5 28.4 %collective-permute-start.69 = (bf16[7,64,256]{2,1,0:T(8,128)(2,1)S(1)}, bf16[7,64,256]{2,1,0:T(8,128)(2,1)S(1)}, u32[]{:S(2)}, u32[]{:S(2)}) collective-permute-start(bf16[7,64,256]{2,1,0:T(8,128)(2,1)S(1)} %get-tuple-element.97), channel_id=1, source_target_pairs={{0,3},{1,0},{2,1},{3,2},{4,7},{5,4},{6,5},{7,6},{8,11},{9,8},{10,9... | collective-permute-start | bytes 688136 | tf_op jit(solution)/shard_map/ppermute | solution.py:309
  422.0 55.3 %collective-permute-start.105 = (bf16[256,1792]{1,0:T(8,128)(2,1)S(1)}, bf16[256,1792]{1,0:T(8,128)(2,1)S(1)}, u32[]{:S(2)}, u32[]{:S(2)}) collective-permute-start(bf16[256,1792]{1,0:T(8,128)(2,1)S(1)} %collective-permute-done.64.x_bottom.refs_2_), channel_id=1, source_target_pairs={{0,16},{4,20},{8,28},{12,24},{16,4},{20,0},{24,8},{28,12},{1,17},{... | collective-permute-start | bytes 2752520 | tf_op jit(solution)/shard_map/ppermute | solution.py:75
  423.4 53.9 %collective-permute-start.104 = (bf16[256,1792]{1,0:T(8,128)(2,1)S(1)}, bf16[256,1792]{1,0:T(8,128)(2,1)S(1)}, u32[]{:S(2)}, u32[]{:S(2)}) collective-permute-start(bf16[256,1792]{1,0:T(8,128)(2,1)S(1)} %collective-permute-done.65.y_top.refs_3_), channel_id=1, source_target_pairs={{0,8},{4,12},{8,4},{12,0},{16,24},{20,28},{24,20},{28,16},{1,9},{5... | collective-permute-start | bytes 2752520 | tf_op jit(solution)/shard_map/ppermute | solution.py:75
  425.4 52.4 %collective-permute-start.100 = (bf16[256,1792]{1,0:T(8,128)(2,1)S(1)}, bf16[256,1792]{1,0:T(8,128)(2,1)S(1)}, u32[]{:S(2)}, u32[]{:S(2)}) collective-permute-start(bf16[256,1792]{1,0:T(8,128)(2,1)S(1)} %collective-permute-done.63.x_top.refs_4_), channel_id=1, source_target_pairs={{0,4},{4,0},{8,12},{12,8},{16,20},{20,16},{24,28},{28,24},{1,5},{5... | collective-permute-start | bytes 2752520 | tf_op jit(solution)/shard_map/ppermute | solution.py:75
  491.1 41.6 %collective-permute-start.112 = (bf16[256,1792]{1,0:T(8,128)(2,1)S(1)}, bf16[256,1792]{1,0:T(8,128)(2,1)S(1)}, u32[]{:S(2)}, u32[]{:S(2)}) collective-permute-start(bf16[256,1792]{1,0:T(8,128)(2,1)S(1)} %get-tuple-element.120.refs_3_), channel_id=1, source_target_pairs={{8,0},{12,4},{4,8},{0,12},{24,16},{28,20},{20,24},{16,28},{9,1},{1... | collective-permute-start | bytes 2752520 | tf_op jit(solution)/shard_map/ppermute | solution.py:75
  492.1 42.6 %collective-permute-start.115 = (bf16[256,1792]{1,0:T(8,128)(2,1)S(1)}, bf16[256,1792]{1,0:T(8,128)(2,1)S(1)}, u32[]{:S(2)}, u32[]{:S(2)}) collective-permute-start(bf16[256,1792]{1,0:T(8,128)(2,1)S(1)} %get-tuple-element.121.refs_2_), channel_id=1, source_target_pairs={{16,0},{20,4},{28,8},{24,12},{4,16},{0,20},{8,24},{12,28},{17,1},{... | collective-permute-start | bytes 2752520 | tf_op jit(solution)/shard_map/ppermute | solution.py:75
  494.1 40.8 %collective-permute-start.125 = (bf16[256,1792]{1,0:T(8,128)(2,1)S(1)}, bf16[256,1792]{1,0:T(8,128)(2,1)S(1)}, u32[]{:S(2)}, u32[]{:S(2)}) collective-permute-start(bf16[256,1792]{1,0:T(8,128)(2,1)S(1)} %get-tuple-element.120.refs_3_), channel_id=1, source_target_pairs={{0,4},{4,0},{8,12},{12,8},{16,20},{20,16},{24,28},{28,24},{1,5},{5... | collective-permute-start | bytes 2752520 | tf_op jit(solution)/shard_map/ppermute | solution.py:75
  494.3 40.6 %collective-permute-start.119 = (bf16[256,1792]{1,0:T(8,128)(2,1)S(1)}, bf16[256,1792]{1,0:T(8,128)(2,1)S(1)}, u32[]{:S(2)}, u32[]{:S(2)}) collective-permute-start(bf16[256,1792]{1,0:T(8,128)(2,1)S(1)} %get-tuple-element.120.refs_3_), channel_id=1, source_target_pairs={{16,0},{20,4},{28,8},{24,12},{4,16},{0,20},{8,24},{12,28},{17,1},{... | collective-permute-start | bytes 2752520 | tf_op jit(solution)/shard_map/ppermute | solution.py:75
  (107 other events, 1852.1 us)

commit v4 on v3

--- a/solution.py
+++ b/solution.py
@@ -75,14 +75,14 @@
     return lax.ppermute(value, "dp", pairs)
 
 
-def call(kernel, outs, args, scalars=(), scratch=(), flops=0):
+def call(kernel, outs, args, scalars=(), scratch=(), flops=0, streamed=False):
     moved = sum(a.size * a.dtype.itemsize for a in [*args, *outs])
     vmem = pl.BlockSpec(memory_space=pltpu.VMEM)
     return pl.pallas_call(
         kernel,
         out_shape=outs,
         in_specs=[pl.BlockSpec(memory_space=pltpu.SMEM)] * len(scalars) + [vmem] * len(args),
-        out_specs=[vmem] * len(outs),
+        out_specs=[pl.BlockSpec(memory_space=pl.ANY) if streamed else vmem] * len(outs),
         scratch_shapes=list(scratch),
         compiler_params=pltpu.CompilerParams(vmem_limit_bytes=VMEM_LIMIT),
         cost_estimate=pl.CostEstimate(flops=flops, bytes_accessed=moved, transcendentals=0),
@@ -221,15 +221,19 @@
     return call(functools.partial(near_assemble_kernel, size), outs, parts, [z])
 
 
+def shifts_of(size):
+    return [by for by in range(1, size) if by * 2 != size], size // 2
+
+
 def mirror_assemble_kernel(size, z_ref, *refs):
-    (x_early, y_early), refs = refs[:2], refs[2:]
-    x_parts, y_parts, refs = refs[:size], refs[size : 2 * size], refs[2 * size :]
-    side, linked, crossed, x_late, y_late = refs
-    rows, half = x_parts[0].shape[1:]
-    for by in range(size):
-        at = pl.ds(rows_at(z_ref[0], by, size, rows), rows)
-        x_late[:, at, :] = x_parts[by][...]
-        y_late[:, at, :] = y_parts[by][...]
+    x_early, y_early, *late, side, linked, crossed, x_late, y_late = refs
+    rows, half = late[0].shape[1:]
+    packed, last = shifts_of(size)
+    for shifts, x_part, y_part in zip(([0], packed, [last]), late[::2], late[1::2]):
+        for k, by in enumerate(shifts):
+            at = pl.ds(rows_at(z_ref[0], by, size, rows), rows)
+            x_late[:, at, :] = x_part[:, k * rows : (k + 1) * rows]
+            y_late[:, at, :] = y_part[:, k * rows : (k + 1) * rows]
     columns = [slice(k * half, (k + 1) * half) for k in range(4)]
     top, bottom = columns[0], columns[1]
     for k in range(2):
@@ -247,20 +251,28 @@
     crossed[bottom, bottom] = y_late[1].T
 
 
-def mirror_assemble(z, size, early, x_parts, y_parts):
-    count, _, half = x_parts[0].shape
+def mirror_assemble(z, size, mirrored):
+    count, half = mirrored[-1].shape[0], mirrored[-1].shape[2]
     outs = [jax.ShapeDtypeStruct((2 * half, width * half), bf16) for width in (4, 2, 2)]
     return call(
         functools.partial(mirror_assemble_kernel, size),
         outs,
-        [*early, *x_parts, *y_parts],
+        mirrored,
         [z],
         [pltpu.VMEM((count, half, half), bf16)] * 2,
     )
 
 
-def product_kernel(n_grams, n_halves, has_sum, finish, tile, *refs):
+def product_kernel(n_grams, n_halves, has_sum, finish, tile, stream, *refs):
     refs = list(refs)
+    if stream:
+        streamed, held, arrived = refs[-3:]
+        refs = refs[:-3] + [held]
+
+        def column_copy(t):
+            at = pl.ds(pl.multiple_of(t * tile, tile), tile)
+            return pltpu.make_async_copy(held.at[:, at], streamed.at[:, at], arrived.at[t])
+
     if finish:
         inverse_norm = lax.rsqrt(jnp.sum(refs.pop(0)[...], axis=(0, 1), keepdims=True))
         root_scale = jnp.sqrt(inverse_norm)
@@ -283,9 +295,18 @@
         rows = value.shape[0] // len(outs)
         for k, out in enumerate(outs):
             out[:, at] = value[k * rows : (k + 1) * rows].astype(out.dtype)
+        if stream:
+            column_copy(t).start()
         return carry
 
     lax.fori_loop(0, columns // tile, column_tile, 0)
+    if stream:
+
+        def wait(t, carry):
+            column_copy(t).wait()
+            return carry
+
+        lax.fori_loop(0, columns // tile, wait, 0)
 
 
 def product(grams, halves, summed=None, finish=None, dtype=f32, parts=1):
@@ -295,12 +316,15 @@
     args += [] if summed is None else [summed]
     args += list(finish[2]) if finish else []
     outs = [jax.ShapeDtypeStruct((2 * half // parts, columns), dtype)] * parts
+    stream = bool(finish) and parts == 1
     return call(
         functools.partial(
-            product_kernel, len(grams), len(halves), summed is not None, finish and finish[0], tile
+            product_kernel, len(grams), len(halves), summed is not None, finish and finish[0], tile, stream
         ),
         outs,
         args,
+        scratch=[pltpu.VMEM(outs[0].shape, dtype), pltpu.SemaphoreType.DMA((columns // tile,))] if stream else (),
+        streamed=stream,
         flops=4 * half * half * columns * len(halves),
     )
 
@@ -310,9 +334,10 @@
 
 
 def total_of(value, size):
+    value = sum([shifted(value, by, size) for by in range(1, size)], value)
     for step in (1, 2, 4):
         value = value + over_dp(value, [(i, i ^ step) for i in range(ROW_DEVICES)])
-    return sum([shifted(value, by, size) for by in range(1, size)], value)
+    return value
 
 
 def gather(block):
@@ -321,7 +346,9 @@
     x_top, y_bottom = over_dp(top, TAKE_X), over_dp(bottom, TAKE_Y)
     core = over_dp(top, CORE), over_dp(bottom, CORE)
     d_oth_bottom, d_sel_top = over_dp(x_bottom, GIVE_Y), over_dp(y_top, GIVE_X)
-    side = [over_dp(half, CORE) for half in (x_top, x_bottom, y_top, y_bottom)]
+    x_oth_bottom, y_oth_top = over_dp(x_bottom, CORE), over_dp(y_top, CORE)
+    x_oth_top, y_oth_bottom = over_dp(x_top, CORE), over_dp(y_bottom, CORE)
+    side = x_oth_top, x_oth_bottom, y_oth_top, y_oth_bottom
     crossed = over_dp(d_oth_bottom, CORE), over_dp(d_sel_top, CORE)
     return core, (x_bottom, y_top), (x_top, y_bottom), side, (d_sel_top, d_oth_bottom), crossed
 
@@ -377,12 +404,18 @@
     late_parts = spread(late_part, size)
     near_one, x_whole, y_whole = near_assemble(z, size, early_parts, True)
     early = over_dp(x_whole, GIVE_X), over_dp(y_whole, GIVE_Y)
-    x_parts = [over_dp(p[:-2], GIVE_X) for p in late_parts]
-    y_parts = [over_dp(p[2:], GIVE_Y) for p in late_parts]
+    packed, last = shifts_of(size)
+    late_own = over_dp(late_part[:-2], GIVE_X), over_dp(late_part[2:], GIVE_Y)
+    x_pack = jnp.concatenate([late_parts[by][:-2] for by in packed], axis=1)
+    y_pack = jnp.concatenate([late_parts[by][2:] for by in packed], axis=1)
+    late_packed = over_dp(x_pack, GIVE_X), over_dp(y_pack, GIVE_Y)
+    late_last = over_dp(late_parts[last][:-2], GIVE_X), over_dp(late_parts[last][2:], GIVE_Y)
     own, beside = own_assemble(z, size, own_parts)
     beside = beside_of(side_index, beside, over_dp(beside, CORE))
     (near_two,) = near_assemble(z, size, late_parts, False)
-    side_gram, linked_gram, crossed_gram = mirror_assemble(z, size, early, x_parts, y_parts)
+    side_gram, linked_gram, crossed_gram = mirror_assemble(
+        z, size, [*early, *late_own, *late_packed, *late_last]
+    )
 
     def mixing(root_scale, inverse_norm):
         return cubic_term * root_scale, quintic_term * root_scale * inverse_norm
@@ -402,7 +435,8 @@
     )
     core, one, two, side, linked, crossed = gather(mixture)
     (second,) = product([own, beside], [*mixture, *core])
-    (second,) = product([near_one, near_two, side_gram], [*one, *two, *side], second)
+    (second,) = product([near_one], one, second)
+    (second,) = product([near_two, side_gram], [*two, *side], second)
     (second,) = product([linked_gram], linked, second)
     return product([crossed_gram], crossed, second, (ending, squares, matrix), dtype, parts)
 
@@ -450,6 +484,6 @@
     def square(momentum, gradient):
         return sharded(functools.partial(body_square, column_devices, momentum.shape[1]))(momentum, gradient)
 
-    if row_devices != ROW_DEVICES or column_devices & (column_devices - 1):
+    if row_devices != ROW_DEVICES or column_devices % 4 or column_devices & (column_devices - 1):
         return general
     return square

time: 576 us -> 569 us (0.988)
  starting transfers between devices: 198 us -> 122 us
  waiting for transfers between devices: 297 us -> 366 us
    ppermute x42, starting transfers between devices: 123 us -> 66.6 us  [shifted(): lax.ppermute(value, 'shard', [(z, (z + by) % size) for z in range(size)])]
    ppermute x42, waiting for transfers between devices: 53 us -> 91.8 us  [shifted(): lax.ppermute(value, 'shard', [(z, (z + by) % size) for z in range(size)])]
    ppermute x84 -> x80, waiting for transfers between devices: 244 us -> 274 us  [over_dp(): return lax.ppermute(value, 'dp', pairs)]
    ppermute x84 -> x80, starting transfers between devices: 74.9 us -> 55.3 us  [over_dp(): return lax.ppermute(value, 'dp', pairs)]
    pallas_call x36 -> x38, Pallas kernels: 69.9 us -> 71.2 us  [call(): pl.pallas_call(kernel, out_shape=outs, in_specs=[pl.BlockSpec(memory_spac...]
  transfers between devices with their start and end apart: 126 -> 122, of which waited for: 48 -> 40; matrix products, arithmetic and copies ran while one was open for 0% -> 0% of each run, Pallas kernels for 9% -> 10%
where the time goes in v4:
time: 569 us
  waiting for transfers between devices  366 us (64%)
  starting transfers between devices  122 us (21%)
  Pallas kernels  71.2 us (13%)
    ppermute x80, waiting for transfers between devices, over_dp(): return lax.ppermute(value, 'dp', pairs)  274 us
    ppermute x42, waiting for transfers between devices, shifted(): lax.ppermute(value, 'shard', [(z, (z + by) % size) for z in range(size)])  91.8 us
    pallas_call x38, Pallas kernels, call(): pl.pallas_call(kernel, out_shape=outs, in_specs=[pl.BlockSpec(memory_spac...  71.2 us
    ppermute x42, starting transfers between devices, shifted(): lax.ppermute(value, 'shard', [(z, (z + by) % size) for z in range(size)])  66.6 us
    ppermute x80, starting transfers between devices, over_dp(): return lax.ppermute(value, 'dp', pairs)  55.3 us
  transfers between devices with their start and end apart: 122, of which 40 were waited for; matrix products, arithmetic and copies ran while one was open for 0% of the time, Pallas kernels for 10%

profile of v4, /device:TPU:0, one launch (start us, length us, event | category | flops | bytes accessed | tf_op | source)
XLA Modules:
  0.0 569.0 jit_solution(10173700055265232525)
XLA Ops:
  15.8 12.9 %collective-permute-done.1.x_bottom.refs_2_ = bf16[256,1792]{1,0:T(8,128)(2,1)} collective-permute-done((bf16[256,1792]{1,0:T(8,128)(2,1)S(1)}, bf16[256,1792]{1,0:T(8,128)(2,1)}, u32[]{:S(2)}, u32[]{:S(2)}) %collective-permute-start.1) | collective-permute-done | bytes 917536 | tf_op jit(solution)/shard_map/ppermute | solution.py:75
  36.6 11.1 %collective-permute-done.x_top.refs_4_ = bf16[256,1792]{1,0:T(8,128)(2,1)} collective-permute-done((bf16[256,1792]{1,0:T(8,128)(2,1)S(1)}, bf16[256,1792]{1,0:T(8,128)(2,1)}, u32[]{:S(2)}, u32[]{:S(2)}) %collective-permute-start) | collective-permute-done | bytes 917536 | tf_op jit(solution)/shard_map/ppermute | solution.py:75
  62.1 22.2 %collective-permute-done.8.refs_2_ = bf16[5,64,256]{2,1,0:T(8,128)(2,1)S(1)} collective-permute-done((bf16[5,64,256]{2,1,0:T(8,128)(2,1)S(1)}, bf16[5,64,256]{2,1,0:T(8,128)(2,1)S(1)}, u32[]{:S(2)}, u32[]{:S(2)}) %collective-permute-start.8) | collective-permute-done | bytes 163872 | tf_op jit(solution)/shard_map/ppermute | solution.py:333
  110.6 11.4 %collective-permute-done.22.refs_2_ = bf16[5,64,256]{2,1,0:T(8,128)(2,1)S(1)} collective-permute-done((bf16[5,64,256]{2,1,0:T(8,128)(2,1)S(1)}, bf16[5,64,256]{2,1,0:T(8,128)(2,1)S(1)}, u32[]{:S(2)}, u32[]{:S(2)}) %collective-permute-start.22) | collective-permute-done | bytes 163872 | tf_op jit(solution)/shard_map/ppermute | solution.py:333
  130.8 7.1 %collective-permute-done.32.refs_2_ = bf16[7,64,256]{2,1,0:T(8,128)(2,1)S(1)} collective-permute-done((bf16[7,64,256]{2,1,0:T(8,128)(2,1)S(1)}, bf16[7,64,256]{2,1,0:T(8,128)(2,1)S(1)}, u32[]{:S(2)}, u32[]{:S(2)}) %collective-permute-start.32) | collective-permute-done | bytes 229408 | tf_op jit(solution)/shard_map/ppermute | solution.py:333
  148.9 20.7 %collective-permute-done.33.refs_6_ = bf16[5,64,256]{2,1,0:T(8,128)(2,1)S(1)} collective-permute-done((bf16[5,64,256]{2,1,0:T(8,128)(2,1)S(1)}, bf16[5,64,256]{2,1,0:T(8,128)(2,1)S(1)}, u32[]{:S(2)}, u32[]{:S(2)}) %collective-permute-start.33) | collective-permute-done | bytes 163872 | tf_op jit(solution)/shard_map/ppermute | solution.py:75
  172.7 7.6 %collective-permute-done.24.refs_0_ = bf16[3,256,256]{2,1,0:T(8,128)(2,1)S(1)} collective-permute-done((bf16[3,256,256]{2,1,0:T(8,128)(2,1)S(1)}, bf16[3,256,256]{2,1,0:T(8,128)(2,1)S(1)}, u32[]{:S(2)}, u32[]{:S(2)}) %collective-permute-start.24) | collective-permute-done | bytes 393248 | tf_op jit(solution)/shard_map/ppermute | solution.py:75
  184.0 7.3 %collective-permute-done.31.refs_5_ = bf16[5,128,256]{2,1,0:T(8,128)(2,1)S(1)} collective-permute-done((bf16[5,128,256]{2,1,0:T(8,128)(2,1)S(1)}, bf16[5,128,256]{2,1,0:T(8,128)(2,1)S(1)}, u32[]{:S(2)}, u32[]{:S(2)}) %collective-permute-start.31) | collective-permute-done | bytes 327712 | tf_op jit(solution)/shard_map/ppermute | solution.py:75
  205.1 5.3 shard_map.54
  214.5 19.3 %collective-permute-done.53.refs_2_ = bf16[256,1792]{1,0:T(8,128)(2,1)S(1)} collective-permute-done((bf16[256,1792]{1,0:T(8,128)(2,1)S(1)}, bf16[256,1792]{1,0:T(8,128)(2,1)S(1)}, u32[]{:S(2)}, u32[]{:S(2)}) %collective-permute-start.53) | collective-permute-done | bytes 917536 | tf_op jit(solution)/shard_map/ppermute | solution.py:75
  233.8 19.1 %collective-permute-done.47.refs_1_ = bf16[256,1792]{1,0:T(8,128)(2,1)S(1)} collective-permute-done((bf16[256,1792]{1,0:T(8,128)(2,1)S(1)}, bf16[256,1792]{1,0:T(8,128)(2,1)S(1)}, u32[]{:S(2)}, u32[]{:S(2)}) %collective-permute-start.47) | collective-permute-done | bytes 917536 | tf_op jit(solution)/shard_map/ppermute | solution.py:75
  255.2 20.1 %collective-permute-done.48.refs_2_ = bf16[256,1792]{1,0:T(8,128)(2,1)S(1)} collective-permute-done((bf16[256,1792]{1,0:T(8,128)(2,1)S(1)}, bf16[256,1792]{1,0:T(8,128)(2,1)S(1)}, u32[]{:S(2)}, u32[]{:S(2)}) %collective-permute-start.48) | collective-permute-done | bytes 917536 | tf_op jit(solution)/shard_map/ppermute | solution.py:75
  295.1 18.2 %collective-permute-done.62.x_bottom.refs_2_ = bf16[256,1792]{1,0:T(8,128)(2,1)S(1)} collective-permute-done((bf16[256,1792]{1,0:T(8,128)(2,1)S(1)}, bf16[256,1792]{1,0:T(8,128)(2,1)S(1)}, u32[]{:S(2)}, u32[]{:S(2)}) %collective-permute-start.62) | collective-permute-done | bytes 917536 | tf_op jit(solution)/shard_map/ppermute | solution.py:75
  314.9 17.2 %collective-permute-done.61.x_top.refs_4_ = bf16[256,1792]{1,0:T(8,128)(2,1)S(1)} collective-permute-done((bf16[256,1792]{1,0:T(8,128)(2,1)S(1)}, bf16[256,1792]{1,0:T(8,128)(2,1)S(1)}, u32[]{:S(2)}, u32[]{:S(2)}) %collective-permute-start.61) | collective-permute-done | bytes 917536 | tf_op jit(solution)/shard_map/ppermute | solution.py:75
  343.1 23.0 %collective-permute-done.69.refs_2_ = bf16[5,64,256]{2,1,0:T(8,128)(2,1)S(1)} collective-permute-done((bf16[5,64,256]{2,1,0:T(8,128)(2,1)S(1)}, bf16[5,64,256]{2,1,0:T(8,128)(2,1)S(1)}, u32[]{:S(2)}, u32[]{:S(2)}) %collective-permute-start.69) | collective-permute-done | bytes 163872 | tf_op jit(solution)/shard_map/ppermute | solution.py:333
  392.5 13.8 %collective-permute-done.83.refs_2_ = bf16[5,64,256]{2,1,0:T(8,128)(2,1)S(1)} collective-permute-done((bf16[5,64,256]{2,1,0:T(8,128)(2,1)S(1)}, bf16[5,64,256]{2,1,0:T(8,128)(2,1)S(1)}, u32[]{:S(2)}, u32[]{:S(2)}) %collective-permute-start.83) | collective-permute-done | bytes 163872 | tf_op jit(solution)/shard_map/ppermute | solution.py:333
  411.8 7.9 %collective-permute-done.93.refs_2_ = bf16[7,64,256]{2,1,0:T(8,128)(2,1)S(1)} collective-permute-done((bf16[7,64,256]{2,1,0:T(8,128)(2,1)S(1)}, bf16[7,64,256]{2,1,0:T(8,128)(2,1)S(1)}, u32[]{:S(2)}, u32[]{:S(2)}) %collective-permute-start.93) | collective-permute-done | bytes 229408 | tf_op jit(solution)/shard_map/ppermute | solution.py:333
  419.8 6.4 %collective-permute-done.88.refs_3_ = bf16[5,64,256]{2,1,0:T(8,128)(2,1)S(1)} collective-permute-done((bf16[5,64,256]{2,1,0:T(8,128)(2,1)S(1)}, bf16[5,64,256]{2,1,0:T(8,128)(2,1)S(1)}, u32[]{:S(2)}, u32[]{:S(2)}) %collective-permute-start.88) | collective-permute-done | bytes 163872 | tf_op jit(solution)/shard_map/ppermute | solution.py:75
  429.5 22.1 %collective-permute-done.94.refs_6_ = bf16[5,64,256]{2,1,0:T(8,128)(2,1)S(1)} collective-permute-done((bf16[5,64,256]{2,1,0:T(8,128)(2,1)S(1)}, bf16[5,64,256]{2,1,0:T(8,128)(2,1)S(1)}, u32[]{:S(2)}, u32[]{:S(2)}) %collective-permute-start.94) | collective-permute-done | bytes 163872 | tf_op jit(solution)/shard_map/ppermute | solution.py:75
  452.9 9.9 %collective-permute-done.85.refs_0_ = bf16[3,256,256]{2,1,0:T(8,128)(2,1)S(1)} collective-permute-done((bf16[3,256,256]{2,1,0:T(8,128)(2,1)S(1)}, bf16[3,256,256]{2,1,0:T(8,128)(2,1)S(1)}, u32[]{:S(2)}, u32[]{:S(2)}) %collective-permute-start.85) | collective-permute-done | bytes 393248 | tf_op jit(solution)/shard_map/ppermute | solution.py:75
  464.7 8.0 %collective-permute-done.92.refs_5_ = bf16[5,128,256]{2,1,0:T(8,128)(2,1)S(1)} collective-permute-done((bf16[5,128,256]{2,1,0:T(8,128)(2,1)S(1)}, bf16[5,128,256]{2,1,0:T(8,128)(2,1)S(1)}, u32[]{:S(2)}, u32[]{:S(2)}) %collective-permute-start.92) | collective-permute-done | bytes 327712 | tf_op jit(solution)/shard_map/ppermute | solution.py:75
  490.7 19.3 %collective-permute-done.114.refs_2_ = bf16[256,1792]{1,0:T(8,128)(2,1)S(1)} collective-permute-done((bf16[256,1792]{1,0:T(8,128)(2,1)S(1)}, bf16[256,1792]{1,0:T(8,128)(2,1)S(1)}, u32[]{:S(2)}, u32[]{:S(2)}) %collective-permute-start.114) | collective-permute-done | bytes 917536 | tf_op jit(solution)/shard_map/ppermute | solution.py:75
  510.0 19.1 %collective-permute-done.108.refs_1_ = bf16[256,1792]{1,0:T(8,128)(2,1)S(1)} collective-permute-done((bf16[256,1792]{1,0:T(8,128)(2,1)S(1)}, bf16[256,1792]{1,0:T(8,128)(2,1)S(1)}, u32[]{:S(2)}, u32[]{:S(2)}) %collective-permute-start.108) | collective-permute-done | bytes 917536 | tf_op jit(solution)/shard_map/ppermute | solution.py:75
  531.3 20.2 %collective-permute-done.109.refs_2_ = bf16[256,1792]{1,0:T(8,128)(2,1)S(1)} collective-permute-done((bf16[256,1792]{1,0:T(8,128)(2,1)S(1)}, bf16[256,1792]{1,0:T(8,128)(2,1)S(1)}, u32[]{:S(2)}, u32[]{:S(2)}) %collective-permute-start.109) | collective-permute-done | bytes 917536 | tf_op jit(solution)/shard_map/ppermute | solution.py:75
  (291 shorter events, 218.1 us)
Async XLA Ops:
  8.6 39.1 %collective-permute-start = (bf16[256,1792]{1,0:T(8,128)(2,1)S(1)}, bf16[256,1792]{1,0:T(8,128)(2,1)}, u32[]{:S(2)}, u32[]{:S(2)}) collective-permute-start(bf16[256,1792]{1,0:T(8,128)(2,1)S(1)} %get-tuple-element.123.top.refs_2_.refs_13_.refs_5_), channel_id=1, source_target_pairs={{8,0},{12,4},{4,8},{0,12},{24,16},{28,20},{20,24},{16,28},{9,1},{1... | collective-permute-start | bytes 2752520 | tf_op jit(solution)/shard_map/ppermute | solution.py:75
  9.6 40.0 %collective-permute-start.3 = (bf16[256,1792]{1,0:T(8,128)(2,1)S(1)}, bf16[256,1792]{1,0:T(8,128)(2,1)}, u32[]{:S(2)}, u32[]{:S(2)}) collective-permute-start(bf16[256,1792]{1,0:T(8,128)(2,1)S(1)} %get-tuple-element.122.bottom.refs_3_.refs_14_.refs_6_), channel_id=1, source_target_pairs={{16,0},{20,4},{28,8},{24,12},{4,16},{0,20},{8,24},{12,28},{17,1},{... | collective-permute-start | bytes 2752520 | tf_op jit(solution)/shard_map/ppermute | solution.py:75
  14.1 40.9 %collective-permute-start.12 = (bf16[5,64,256]{2,1,0:T(8,128)(2,1)S(1)}, bf16[5,64,256]{2,1,0:T(8,128)(2,1)S(1)}, u32[]{:S(2)}, u32[]{:S(2)}) collective-permute-start(bf16[5,64,256]{2,1,0:T(8,128)(2,1)S(1)} %get-tuple-element.73), channel_id=1, source_target_pairs={{0,1},{1,2},{2,3},{3,0},{4,5},{5,6},{6,7},{7,4},{8,9},{9,10},{10,1... | collective-permute-start | bytes 491528 | tf_op jit(solution)/shard_map/ppermute | solution.py:333
  110.6 35.9 %collective-permute-start.46 = (bf16[512,256]{1,0:T(8,128)(2,1)S(1)}, bf16[512,256]{1,0:T(8,128)(2,1)S(1)}, u32[]{:S(2)}, u32[]{:S(2)}) collective-permute-start(bf16[512,256]{1,0:T(8,128)(2,1)S(1)} %get-tuple-element.89.own), channel_id=1, source_target_pairs={{0,4},{4,0},{8,12},{12,8},{16,20},{20,16},{24,28},{28,24},{1,5},{5... | collective-permute-start | bytes 786440 | tf_op jit(solution)/shard_map/ppermute | solution.py:75
  139.7 54.4 %collective-permute-start.40 = (bf16[256,1792]{1,0:T(8,128)(2,1)}, bf16[256,1792]{1,0:T(8,128)(2,1)S(1)}, u32[]{:S(2)}, u32[]{:S(2)}) collective-permute-start(bf16[256,1792]{1,0:T(8,128)(2,1)} %collective-permute-done.1.x_bottom.refs_2_), channel_id=1, source_target_pairs={{0,16},{4,20},{8,28},{12,24},{16,4},{20,0},{24,8},{28,12},{1,17},{... | collective-permute-start | bytes 2752520 | tf_op jit(solution)/shard_map/ppermute | solution.py:75
  144.2 50.3 %collective-permute-start.39 = (bf16[256,1792]{1,0:T(8,128)(2,1)S(1)}, bf16[256,1792]{1,0:T(8,128)(2,1)S(1)}, u32[]{:S(2)}, u32[]{:S(2)}) collective-permute-start(bf16[256,1792]{1,0:T(8,128)(2,1)S(1)} %collective-permute-done.2.y_top.refs_3_), channel_id=1, source_target_pairs={{0,8},{4,12},{8,4},{12,0},{16,24},{20,28},{24,20},{28,16},{1,9},{5... | collective-permute-start | bytes 2752520 | tf_op jit(solution)/shard_map/ppermute | solution.py:75
  146.1 48.5 %collective-permute-start.36 = (bf16[256,1792]{1,0:T(8,128)(2,1)}, bf16[256,1792]{1,0:T(8,128)(2,1)S(1)}, u32[]{:S(2)}, u32[]{:S(2)}) collective-permute-start(bf16[256,1792]{1,0:T(8,128)(2,1)} %collective-permute-done.1.x_bottom.refs_2_), channel_id=1, source_target_pairs={{0,4},{4,0},{8,12},{12,8},{16,20},{20,16},{24,28},{28,24},{1,5},{5... | collective-permute-start | bytes 2752520 | tf_op jit(solution)/shard_map/ppermute | solution.py:75
  210.6 42.3 %collective-permute-start.47 = (bf16[256,1792]{1,0:T(8,128)(2,1)S(1)}, bf16[256,1792]{1,0:T(8,128)(2,1)S(1)}, u32[]{:S(2)}, u32[]{:S(2)}) collective-permute-start(bf16[256,1792]{1,0:T(8,128)(2,1)S(1)} %get-tuple-element.90.refs_3_), channel_id=1, source_target_pairs={{8,0},{12,4},{4,8},{0,12},{24,16},{28,20},{20,24},{16,28},{9,1},{1... | collective-permute-start | bytes 2752520 | tf_op jit(solution)/shard_map/ppermute | solution.py:75
  212.4 40.6 %collective-permute-start.50 = (bf16[256,1792]{1,0:T(8,128)(2,1)S(1)}, bf16[256,1792]{1,0:T(8,128)(2,1)S(1)}, u32[]{:S(2)}, u32[]{:S(2)}) collective-permute-start(bf16[256,1792]{1,0:T(8,128)(2,1)S(1)} %get-tuple-element.91.refs_2_), channel_id=1, source_target_pairs={{16,0},{20,4},{28,8},{24,12},{4,16},{0,20},{8,24},{12,28},{17,1},{... | collective-permute-start | bytes 2752520 | tf_op jit(solution)/shard_map/ppermute | solution.py:75
  212.5 41.1 %collective-permute-start.60 = (bf16[256,1792]{1,0:T(8,128)(2,1)S(1)}, bf16[256,1792]{1,0:T(8,128)(2,1)S(1)}, u32[]{:S(2)}, u32[]{:S(2)}) collective-permute-start(bf16[256,1792]{1,0:T(8,128)(2,1)S(1)} %get-tuple-element.90.refs_3_), channel_id=1, source_target_pairs={{0,4},{4,0},{8,12},{12,8},{16,20},{20,16},{24,28},{28,24},{1,5},{5... | collective-permute-start | bytes 2752520 | tf_op jit(solution)/shard_map/ppermute | solution.py:75
  213.0 41.7 %collective-permute-start.54 = (bf16[256,1792]{1,0:T(8,128)(2,1)S(1)}, bf16[256,1792]{1,0:T(8,128)(2,1)S(1)}, u32[]{:S(2)}, u32[]{:S(2)}) collective-permute-start(bf16[256,1792]{1,0:T(8,128)(2,1)S(1)} %get-tuple-element.90.refs_3_), channel_id=1, source_target_pairs={{16,0},{20,4},{28,8},{24,12},{4,16},{0,20},{8,24},{12,28},{17,1},{... | collective-permute-start | bytes 2752520 | tf_op jit(solution)/shard_map/ppermute | solution.py:75
  291.7 40.4 %collective-permute-start.61 = (bf16[256,1792]{1,0:T(8,128)(2,1)S(1)}, bf16[256,1792]{1,0:T(8,128)(2,1)S(1)}, u32[]{:S(2)}, u32[]{:S(2)}) collective-permute-start(bf16[256,1792]{1,0:T(8,128)(2,1)S(1)} %get-tuple-element.92.top.refs_2_.refs_13_.refs_5_), channel_id=1, source_target_pairs={{8,0},{12,4},{4,8},{0,12},{24,16},{28,20},{20,24},{16,28},{9,1},{1... | collective-permute-start | bytes 2752520 | tf_op jit(solution)/shard_map/ppermute | solution.py:75
  292.0 40.4 %collective-permute-start.64 = (bf16[256,1792]{1,0:T(8,128)(2,1)S(1)}, bf16[256,1792]{1,0:T(8,128)(2,1)S(1)}, u32[]{:S(2)}, u32[]{:S(2)}) collective-permute-start(bf16[256,1792]{1,0:T(8,128)(2,1)S(1)} %get-tuple-element.93.bottom.refs_3_.refs_14_.refs_6_), channel_id=1, source_target_pairs={{16,0},{20,4},{28,8},{24,12},{4,16},{0,20},{8,24},{12,28},{17,1},{... | collective-permute-start | bytes 2752520 | tf_op jit(solution)/shard_map/ppermute | solution.py:75
  295.0 39.5 %collective-permute-start.73 = (bf16[5,64,256]{2,1,0:T(8,128)(2,1)S(1)}, bf16[5,64,256]{2,1,0:T(8,128)(2,1)S(1)}, u32[]{:S(2)}, u32[]{:S(2)}) collective-permute-start(bf16[5,64,256]{2,1,0:T(8,128)(2,1)S(1)} %get-tuple-element.103), channel_id=1, source_target_pairs={{0,1},{1,2},{2,3},{3,0},{4,5},{5,6},{6,7},{7,4},{8,9},{9,10},{10,1... | collective-permute-start | bytes 491528 | tf_op jit(solution)/shard_map/ppermute | solution.py:333
  334.5 31.7 %collective-permute-start.65 = (bf16[7,64,256]{2,1,0:T(8,128)(2,1)S(1)}, bf16[7,64,256]{2,1,0:T(8,128)(2,1)S(1)}, u32[]{:S(2)}, u32[]{:S(2)}) collective-permute-start(bf16[7,64,256]{2,1,0:T(8,128)(2,1)S(1)} %get-tuple-element.95), channel_id=1, source_target_pairs={{0,1},{1,2},{2,3},{3,0},{4,5},{5,6},{6,7},{7,4},{8,9},{9,10},{10,1... | collective-permute-start | bytes 688136 | tf_op jit(solution)/shard_map/ppermute | solution.py:333
  334.5 31.7 %collective-permute-start.66 = (bf16[7,64,256]{2,1,0:T(8,128)(2,1)S(1)}, bf16[7,64,256]{2,1,0:T(8,128)(2,1)S(1)}, u32[]{:S(2)}, u32[]{:S(2)}) collective-permute-start(bf16[7,64,256]{2,1,0:T(8,128)(2,1)S(1)} %get-tuple-element.96), channel_id=1, source_target_pairs={{0,2},{1,3},{2,0},{3,1},{4,6},{5,7},{6,4},{7,5},{8,10},{9,11},{10,... | collective-permute-start | bytes 688136 | tf_op jit(solution)/shard_map/ppermute | solution.py:333
  392.4 35.9 %collective-permute-start.107 = (bf16[512,256]{1,0:T(8,128)(2,1)S(1)}, bf16[512,256]{1,0:T(8,128)(2,1)S(1)}, u32[]{:S(2)}, u32[]{:S(2)}) collective-permute-start(bf16[512,256]{1,0:T(8,128)(2,1)S(1)} %get-tuple-element.119.own), channel_id=1, source_target_pairs={{0,4},{4,0},{8,12},{12,8},{16,20},{20,16},{24,28},{28,24},{1,5},{5... | collective-permute-start | bytes 786440 | tf_op jit(solution)/shard_map/ppermute | solution.py:75
  419.8 53.6 %collective-permute-start.101 = (bf16[256,1792]{1,0:T(8,128)(2,1)S(1)}, bf16[256,1792]{1,0:T(8,128)(2,1)S(1)}, u32[]{:S(2)}, u32[]{:S(2)}) collective-permute-start(bf16[256,1792]{1,0:T(8,128)(2,1)S(1)} %collective-permute-done.62.x_bottom.refs_2_), channel_id=1, source_target_pairs={{0,16},{4,20},{8,28},{12,24},{16,4},{20,0},{24,8},{28,12},{1,17},{... | collective-permute-start | bytes 2752520 | tf_op jit(solution)/shard_map/ppermute | solution.py:75
  426.2 47.6 %collective-permute-start.100 = (bf16[256,1792]{1,0:T(8,128)(2,1)S(1)}, bf16[256,1792]{1,0:T(8,128)(2,1)S(1)}, u32[]{:S(2)}, u32[]{:S(2)}) collective-permute-start(bf16[256,1792]{1,0:T(8,128)(2,1)S(1)} %collective-permute-done.63.y_top.refs_3_), channel_id=1, source_target_pairs={{0,8},{4,12},{8,4},{12,0},{16,24},{20,28},{24,20},{28,16},{1,9},{5... | collective-permute-start | bytes 2752520 | tf_op jit(solution)/shard_map/ppermute | solution.py:75
  426.9 47.0 %collective-permute-start.96 = (bf16[256,1792]{1,0:T(8,128)(2,1)S(1)}, bf16[256,1792]{1,0:T(8,128)(2,1)S(1)}, u32[]{:S(2)}, u32[]{:S(2)}) collective-permute-start(bf16[256,1792]{1,0:T(8,128)(2,1)S(1)} %collective-permute-done.61.x_top.refs_4_), channel_id=1, source_target_pairs={{0,4},{4,0},{8,12},{12,8},{16,20},{20,16},{24,28},{28,24},{1,5},{5... | collective-permute-start | bytes 2752520 | tf_op jit(solution)/shard_map/ppermute | solution.py:75
  488.0 41.1 %collective-permute-start.108 = (bf16[256,1792]{1,0:T(8,128)(2,1)S(1)}, bf16[256,1792]{1,0:T(8,128)(2,1)S(1)}, u32[]{:S(2)}, u32[]{:S(2)}) collective-permute-start(bf16[256,1792]{1,0:T(8,128)(2,1)S(1)} %get-tuple-element.120.refs_3_), channel_id=1, source_target_pairs={{8,0},{12,4},{4,8},{0,12},{24,16},{28,20},{20,24},{16,28},{9,1},{1... | collective-permute-start | bytes 2752520 | tf_op jit(solution)/shard_map/ppermute | solution.py:75
  488.5 40.8 %collective-permute-start.111 = (bf16[256,1792]{1,0:T(8,128)(2,1)S(1)}, bf16[256,1792]{1,0:T(8,128)(2,1)S(1)}, u32[]{:S(2)}, u32[]{:S(2)}) collective-permute-start(bf16[256,1792]{1,0:T(8,128)(2,1)S(1)} %get-tuple-element.121.refs_2_), channel_id=1, source_target_pairs={{16,0},{20,4},{28,8},{24,12},{4,16},{0,20},{8,24},{12,28},{17,1},{... | collective-permute-start | bytes 2752520 | tf_op jit(solution)/shard_map/ppermute | solution.py:75
  489.1 41.1 %collective-permute-start.121 = (bf16[256,1792]{1,0:T(8,128)(2,1)S(1)}, bf16[256,1792]{1,0:T(8,128)(2,1)S(1)}, u32[]{:S(2)}, u32[]{:S(2)}) collective-permute-start(bf16[256,1792]{1,0:T(8,128)(2,1)S(1)} %get-tuple-element.120.refs_3_), channel_id=1, source_target_pairs={{0,4},{4,0},{8,12},{12,8},{16,20},{20,16},{24,28},{28,24},{1,5},{5... | collective-permute-start | bytes 2752520 | tf_op jit(solution)/shard_map/ppermute | solution.py:75
  489.2 41.7 %collective-permute-start.115 = (bf16[256,1792]{1,0:T(8,128)(2,1)S(1)}, bf16[256,1792]{1,0:T(8,128)(2,1)S(1)}, u32[]{:S(2)}, u32[]{:S(2)}) collective-permute-start(bf16[256,1792]{1,0:T(8,128)(2,1)S(1)} %get-tuple-element.120.refs_3_), channel_id=1, source_target_pairs={{16,0},{20,4},{28,8},{24,12},{4,16},{0,20},{8,24},{12,28},{17,1},{... | collective-permute-start | bytes 2752520 | tf_op jit(solution)/shard_map/ppermute | solution.py:75
  (103 other events, 1847.6 us)

commit v5 on v4

--- a/solution.py
+++ b/solution.py
@@ -63,6 +63,7 @@
 
 
 ROW_DEVICES = 8
+COLUMN_DEVICES = 4
 VMEM_LIMIT = 16 << 20
 CORE = [(i, i ^ 1) for i in range(ROW_DEVICES)]
 TAKE_X = [(x_pick(i), i) for i in range(ROW_DEVICES)]
@@ -89,19 +90,18 @@
     )(*scalars, *[pltpu.with_memory_space_constraint(a, pltpu.VMEM) for a in args])
 
 
-def split_rows(total, size, z, kept, pieces):
-    rows = kept.shape[1]
-    for by in range(size):
-        at = pl.multiple_of(lax.rem(z + by, size) * rows, rows)
-        piece = total[:, pl.ds(at, rows), :]
-        if by:
-            pieces[by - 1][...] = piece.astype(bf16)
-        else:
-            kept[...] = piece
-
-
-def own_gram_kernel(size, z_ref, core_ref, top, bottom, core_top, core_bottom, kept, *rest):
-    pieces, total = rest[:-1], rest[-1]
+def rows_at(z, k, rows):
+    return pl.ds(pl.multiple_of((z ^ k) * rows, rows), rows)
+
+
+def split_rows(total, z, outs):
+    rows = outs[0].shape[1]
+    for k, out in enumerate(outs):
+        out[...] = total[:, rows_at(z, k, rows), :].astype(out.dtype)
+
+
+def own_gram_kernel(z_ref, core_ref, top, bottom, core_top, core_bottom, *rest):
+    outs, total = rest[:-1], rest[-1]
     for q, (left, right) in enumerate([(top, top), (bottom, bottom), (bottom, top)]):
         total[q] = dot_nt(left[...], right[...])
     for core, (first, second) in enumerate([(core_top, core_bottom), (core_bottom, core_top)]):
@@ -111,26 +111,26 @@
             total[3] = dot_nt(top[...], first[...])
             total[4] = dot_nt(bottom[...], second[...])
 
-    split_rows(total, size, z_ref[0], kept, pieces)
+    split_rows(total, z_ref[0], outs)
 
 
 def stacked(top, bottom):
     return jnp.concatenate([top[...], bottom[...]], axis=0)
 
 
-def early_gram_kernel(size, z_ref, top, bottom, x_bottom, y_top, kept, *rest):
-    pieces, total = rest[:-1], rest[-1]
+def early_gram_kernel(z_ref, top, bottom, x_bottom, y_top, *rest):
+    outs, total = rest[:-1], rest[-1]
     half = top.shape[0]
     own = stacked(top, bottom)
     for q, right in ((0, x_bottom), (3, y_top)):
         value = dot_nt(own, right[...])
         total[q], total[q + 1] = value[:half], value[half:]
     total[2] = dot_nt(x_bottom[...], y_top[...])
-    split_rows(total, size, z_ref[0], kept, pieces)
-
-
-def late_gram_kernel(size, z_ref, top, bottom, x_top, x_bottom, y_top, y_bottom, kept, *rest):
-    pieces, total = rest[:-1], rest[-1]
+    split_rows(total, z_ref[0], outs)
+
+
+def late_gram_kernel(z_ref, top, bottom, x_top, x_bottom, y_top, y_bottom, *rest):
+    outs, total = rest[:-1], rest[-1]
     half = top.shape[0]
     own = stacked(top, bottom)
     for q, right in ((0, x_top), (5, y_bottom)):
@@ -139,16 +139,15 @@
     total[2] = dot_nt(x_top[...], y_top[...])
     value = dot_nt(stacked(x_top, x_bottom), y_bottom[...])
     total[3], total[4] = value[:half], value[half:]
-    split_rows(total, size, z_ref[0], kept, pieces)
-
-
-def gram(kernel, shape, size, scalars, halves):
+    split_rows(total, z_ref[0], outs)
+
+
+def gram(kernel, shape, scalars, halves):
     count, rows, columns = shape
-    shape = (count, rows // size, columns)
-    outs = [jax.ShapeDtypeStruct(shape, f32)] + [jax.ShapeDtypeStruct(shape, bf16)] * (size - 1)
+    shape = (count, rows // COLUMN_DEVICES, columns)
     return call(
-        functools.partial(kernel, size),
-        outs,
+        kernel,
+        [jax.ShapeDtypeStruct(shape, kind) for kind in (f32, bf16, f32, bf16)],
         halves,
         scalars,
         [pltpu.VMEM((count, rows, columns), f32)],
@@ -156,25 +155,24 @@
     )
 
 
-def own_assemble_kernel(size, z_ref, *refs):
+def own_assemble_kernel(z_ref, *refs):
     parts, (diagonal, beside) = refs[:-2], refs[-2:]
-    z = z_ref[0]
-    rows, half = parts[0].shape[1], parts[0].shape[2]
-    for by, part in enumerate(parts):
-        at = lax.rem(z + size - by, size) * rows
-        upper, lower = pl.ds(pl.multiple_of(at, rows), rows), pl.ds(pl.multiple_of(half + at, rows), rows)
-        diagonal[upper, :half] = part[0]
+    rows, half = parts[0].shape[1:]
+    for k, part in enumerate(parts):
+        at = rows_at(z_ref[0], k, rows)
+        lower = pl.ds(pl.multiple_of(half + at.start, rows), rows)
+        diagonal[at, :half] = part[0]
         diagonal[lower, half:] = part[1]
         diagonal[lower, :half] = part[2]
-        beside[upper, :] = part[3]
+        beside[at, :] = part[3]
         beside[lower, :] = part[4]
     diagonal[:half, half:] = diagonal[half:, :half].T
 
 
-def own_assemble(z, size, parts):
+def own_assemble(z, parts):
     half = parts[0].shape[2]
     outs = [jax.ShapeDtypeStruct((2 * half, columns), bf16) for columns in (2 * half, half)]
-    return call(functools.partial(own_assemble_kernel, size), outs, parts, [z])
+    return call(own_assemble_kernel, outs, parts, [z])
 
 
 def beside_kernel(core_ref, own, other, out):
@@ -195,43 +193,34 @@
     return call(beside_kernel, [jax.ShapeDtypeStruct((rows, rows), bf16)], [own, other], [core])[0]
 
 
-def rows_at(z, by, size, rows):
-    return pl.multiple_of(lax.rem(z + size - by, size) * rows, rows)
-
-
-def near_assemble_kernel(size, z_ref, *refs):
-    parts, near, wholes = refs[:size], refs[size], refs[size + 1 :]
+def near_assemble_kernel(z_ref, *refs):
+    parts, near, wholes = refs[:COLUMN_DEVICES], refs[COLUMN_DEVICES], refs[COLUMN_DEVICES + 1 :]
     count, rows, half = parts[0].shape
-    for by, part in enumerate(parts):
-        at = rows_at(z_ref[0], by, size, rows)
-        lower = pl.multiple_of(half + at, rows)
-        near[pl.ds(at, rows), :half] = part[0]
-        near[pl.ds(lower, rows), :half] = part[1]
-        near[pl.ds(at, rows), half:] = part[count - 2]
-        near[pl.ds(lower, rows), half:] = part[count - 1]
-        for k, whole in enumerate(wholes):
-            whole[:, pl.ds(at, rows), :] = part[2 * k : count - 2 + 2 * k]
-
-
-def near_assemble(z, size, parts, with_wholes):
+    for k, part in enumerate(parts):
+        at = rows_at(z_ref[0], k, rows)
+        lower = pl.ds(pl.multiple_of(half + at.start, rows), rows)
+        near[at, :half] = part[0]
+        near[lower, :half] = part[1]
+        near[at, half:] = part[count - 2]
+        near[lower, half:] = part[count - 1]
+        for w, whole in enumerate(wholes):
+            whole[:, at, :] = part[2 * w : count - 2 + 2 * w]
+
+
+def near_assemble(z, parts, with_wholes):
     count, _, half = parts[0].shape
     outs = [jax.ShapeDtypeStruct((2 * half, 2 * half), bf16)]
     if with_wholes:
         outs += [jax.ShapeDtypeStruct((count - 2, half, half), bf16)] * 2
-    return call(functools.partial(near_assemble_kernel, size), outs, parts, [z])
-
-
-def shifts_of(size):
-    return [by for by in range(1, size) if by * 2 != size], size // 2
-
-
-def mirror_assemble_kernel(size, z_ref, *refs):
+    return call(near_assemble_kernel, outs, parts, [z])
+
+
+def mirror_assemble_kernel(z_ref, *refs):
     x_early, y_early, *late, side, linked, crossed, x_late, y_late = refs
     rows, half = late[0].shape[1:]
-    packed, last = shifts_of(size)
-    for shifts, x_part, y_part in zip(([0], packed, [last]), late[::2], late[1::2]):
-        for k, by in enumerate(shifts):
-            at = pl.ds(rows_at(z_ref[0], by, size, rows), rows)
+    for shifts, x_part, y_part in zip(((0,), (1, 2), (3,)), late[::2], late[1::2]):
+        for k, shift in enumerate(shifts):
+            at = rows_at(z_ref[0], shift, rows)
             x_late[:, at, :] = x_part[:, k * rows : (k + 1) * rows]
             y_late[:, at, :] = y_part[:, k * rows : (k + 1) * rows]
     columns = [slice(k * half, (k + 1) * half) for k in range(4)]
@@ -251,16 +240,10 @@
     crossed[bottom, bottom] = y_late[1].T
 
 
-def mirror_assemble(z, size, mirrored):
-    count, half = mirrored[-1].shape[0], mirrored[-1].shape[2]
+def mirror_assemble(z, mirrored):
+    count, _, half = mirrored[-1].shape
     outs = [jax.ShapeDtypeStruct((2 * half, width * half), bf16) for width in (4, 2, 2)]
-    return call(
-        functools.partial(mirror_assemble_kernel, size),
-        outs,
-        mirrored,
-        [z],
-        [pltpu.VMEM((count, half, half), bf16)] * 2,
-    )
+    return call(mirror_assemble_kernel, outs, mirrored, [z], [pltpu.VMEM((count, half, half), bf16)] * 2)
 
 
 def product_kernel(n_grams, n_halves, has_sum, finish, tile, stream, *refs):
@@ -329,12 +312,12 @@
     )
 
 
-def shifted(value, by, size):
-    return lax.ppermute(value, "shard", [(z, (z + by) % size) for z in range(size)])
-
-
-def total_of(value, size):
-    value = sum([shifted(value, by, size) for by in range(1, size)], value)
+def exchanged(value, distance):
+    return lax.ppermute(value, "shard", [(z, z ^ distance) for z in range(COLUMN_DEVICES)])
+
+
+def total_of(value):
+    value = value + exchanged(value, 1) + (exchanged(value, 2) + exchanged(value, 3))
     for step in (1, 2, 4):
         value = value + over_dp(value, [(i, i ^ step) for i in range(ROW_DEVICES)])
     return value
@@ -351,6 +334,10 @@
     side = x_oth_top, x_oth_bottom, y_oth_top, y_oth_bottom
     crossed = over_dp(d_oth_bottom, CORE), over_dp(d_sel_top, CORE)
     return core, (x_bottom, y_top), (x_top, y_bottom), side, (d_sel_top, d_oth_bottom), crossed
+
+
+def add_kernel(kept, piece, out):
+    out[...] = (kept[...] + piece[...].astype(f32)).astype(out.dtype)
 
 
 def fold_kernel(weights, *refs):
@@ -368,54 +355,53 @@
     squares[...] = total
 
 
-def reduce_parts(pieces, size, before, weights):
-    kept, *sent = pieces
-    received = [shifted(piece, by, size) for by, piece in enumerate(sent, 1)]
-    outs = [jax.ShapeDtypeStruct(kept.shape, bf16), jax.ShapeDtypeStruct(before.shape, f32)]
-    return call(functools.partial(fold_kernel, weights), outs, [kept, *received, before])
-
-
-def spread(part, size):
-    parts = [part]
-    for by in range(1, size):
-        parts.append(shifted(part, by, size))
-    return parts
-
-
-def iterate_square(matrix, size, gain, dtype, parts):
+def reduce_parts(pieces, before, weights):
+    kept, one, passed, three = pieces
+    three, one = exchanged(three, 1), exchanged(one, 1)
+    out = jax.ShapeDtypeStruct(kept.shape, bf16)
+    (two,) = call(add_kernel, [out], [passed, three])
+    two = exchanged(two, 2)
+    outs = [out, jax.ShapeDtypeStruct(before.shape, f32)]
+    return call(functools.partial(fold_kernel, weights), outs, [kept, one, two, before])
+
+
+def spread(part):
+    two, one = exchanged(part, 2), exchanged(part, 1)
+    three = exchanged(two, 1)
+    return [part, one, two, three]
+
+
+def iterate_square(matrix, gain, dtype, parts):
     z = lax.axis_index("shard").reshape(1)
     side_index = (lax.axis_index("dp") & 1).reshape(1)
     core, one, two, side, linked, crossed = gather(matrix)
     (x_bottom, y_top), (x_top, y_bottom) = one, two
     half = matrix[0].shape[0]
-    own_pieces = gram(own_gram_kernel, (5, half, half), size, [z, side_index], [*matrix, *core])
-    own_part, squares = reduce_parts(
-        own_pieces, size, jnp.zeros((8, 128), f32), (1.0, 1.0, 2.0, 2.0, 2.0)
+    own_pieces = gram(own_gram_kernel, (5, half, half), [z, side_index], [*matrix, *core])
+    own_part, squares = reduce_parts(own_pieces, jnp.zeros((8, 128), f32), (1.0, 1.0, 2.0, 2.0, 2.0))
+    own_parts = spread(own_part)
+    early_pieces = gram(early_gram_kernel, (5, half, half), [z], [*matrix, x_bottom, y_top])
+    early_part, squares = reduce_parts(early_pieces, squares, (2.0,) * 5)
+    late_pieces = gram(
+        late_gram_kernel, (7, half, half), [z], [*matrix, x_top, x_bottom, y_top, y_bottom]
     )
-    own_parts = spread(own_part, size)
-    early_pieces = gram(early_gram_kernel, (5, half, half), size, [z], [*matrix, x_bottom, y_top])
-    early_part, squares = reduce_parts(early_pieces, size, squares, (2.0,) * 5)
-    late_pieces = gram(
-        late_gram_kernel, (7, half, half), size, [z], [*matrix, x_top, x_bottom, y_top, y_bottom]
-    )
-    late_part, squares = reduce_parts(late_pieces, size, squares, (2.0,) * 7)
-    squares = total_of(squares, size)
-    early_parts = spread(early_part, size)
-    late_parts = spread(late_part, size)
-    near_one, x_whole, y_whole = near_assemble(z, size, early_parts, True)
+    late_part, squares = reduce_parts(late_pieces, squares, (2.0,) * 7)
+    squares = total_of(squares)
+    early_parts = spread(early_part)
+    late_parts = spread(late_part)
+    near_one, x_whole, y_whole = near_assemble(z, early_parts, True)
     early = over_dp(x_whole, GIVE_X), over_dp(y_whole, GIVE_Y)
-    packed, last = shifts_of(size)
-    late_own = over_dp(late_part[:-2], GIVE_X), over_dp(late_part[2:], GIVE_Y)
-    x_pack = jnp.concatenate([late_parts[by][:-2] for by in packed], axis=1)
-    y_pack = jnp.concatenate([late_parts[by][2:] for by in packed], axis=1)
-    late_packed = over_dp(x_pack, GIVE_X), over_dp(y_pack, GIVE_Y)
-    late_last = over_dp(late_parts[last][:-2], GIVE_X), over_dp(late_parts[last][2:], GIVE_Y)
-    own, beside = own_assemble(z, size, own_parts)
+    late = []
+    for shifts in ((0,), (1, 2), (3,)):
+        x_part, y_part = late_parts[shifts[0]][:-2], late_parts[shifts[0]][2:]
+        if len(shifts) > 1:
+            x_part = jnp.concatenate([late_parts[k][:-2] for k in shifts], axis=1)
+            y_part = jnp.concatenate([late_parts[k][2:] for k in shifts], axis=1)
+        late += [over_dp(x_part, GIVE_X), over_dp(y_part, GIVE_Y)]
+    own, beside = own_assemble(z, own_parts)
     beside = beside_of(side_index, beside, over_dp(beside, CORE))
-    (near_two,) = near_assemble(z, size, late_parts, False)
-    side_gram, linked_gram, crossed_gram = mirror_assemble(
-        z, size, [*early, *late_own, *late_packed, *late_last]
-    )
+    (near_two,) = near_assemble(z, late_parts, False)
+    side_gram, linked_gram, crossed_gram = mirror_assemble(z, [*early, *late])
 
     def mixing(root_scale, inverse_norm):
         return cubic_term * root_scale, quintic_term * root_scale * inverse_norm
@@ -447,7 +433,7 @@
     return new_momentum, grad_full + momentum_decay * new_momentum
 
 
-def body_square(size, columns, momentum, gradient):
+def body_square(columns, momentum, gradient):
     half = momentum.shape[0] // 2
     block = [
         current_of(momentum[rows], gradient[rows])[1].astype(bf16)
@@ -457,7 +443,7 @@
     for iteration in range(STEPS):
         last = iteration == STEPS - 1
         block = iterate_square(
-            block, size, math.sqrt(columns) if last else 1.0, f32 if last else bf16, 1 if last else 2
+            block, math.sqrt(columns) if last else 1.0, f32 if last else bf16, 1 if last else 2
         )
     return (new_momentum, block[0])
 
@@ -482,8 +468,8 @@
         return sharded(functools.partial(body_general, momentum.shape[1]))(momentum, gradient)
 
     def square(momentum, gradient):
-        return sharded(functools.partial(body_square, column_devices, momentum.shape[1]))(momentum, gradient)
-
-    if row_devices != ROW_DEVICES or column_devices % 4 or column_devices & (column_devices - 1):
+        return sharded(functools.partial(body_square, momentum.shape[1]))(momentum, gradient)
+
+    if (row_devices, column_devices) != (ROW_DEVICES, COLUMN_DEVICES):
         return general
     return square

time: 569 us -> 528 us (0.928)
  starting transfers between devices: 122 us -> 99.2 us
  waiting for transfers between devices: 366 us -> 348 us
    ppermute x80, starting transfers between devices: 55.3 us -> 42.1 us  [over_dp(): return lax.ppermute(value, 'dp', pairs)]
    ppermute x80, waiting for transfers between devices: 274 us -> 264 us  [over_dp(): return lax.ppermute(value, 'dp', pairs)]
    ppermute x42, starting transfers between devices: 66.6 us -> 57.1 us  [exchanged(): lax.ppermute(value, 'shard', [(z, z ^ distance) for z in range(COLUMN_DEV...]
    ppermute x42, waiting for transfers between devices: 91.8 us -> 84.2 us  [exchanged(): lax.ppermute(value, 'shard', [(z, z ^ distance) for z in range(COLUMN_DEV...]
    pallas_call x38 -> x44, Pallas kernels: 71.2 us -> 71.2 us  [call(): pl.pallas_call(kernel, out_shape=outs, in_specs=[pl.BlockSpec(memory_spac...]
  transfers between devices with their start and end apart: 122 -> 122, of which waited for: 40 -> 50; matrix products, arithmetic and copies ran while one was open for 0% -> 0% of each run, Pallas kernels for 10% -> 10%
where the time goes in v5:
time: 528 us
  waiting for transfers between devices  348 us (66%)
  starting transfers between devices  99.2 us (19%)
  Pallas kernels  71.2 us (13%)
  other arithmetic  5.65 us (1%)
    ppermute x80, waiting for transfers between devices, over_dp(): return lax.ppermute(value, 'dp', pairs)  264 us
    ppermute x42, waiting for transfers between devices, exchanged(): lax.ppermute(value, 'shard', [(z, z ^ distance) for z in range(COLUMN_DEV...  84.2 us
    pallas_call x44, Pallas kernels, call(): pl.pallas_call(kernel, out_shape=outs, in_specs=[pl.BlockSpec(memory_spac...  71.2 us
    ppermute x42, starting transfers between devices, exchanged(): lax.ppermute(value, 'shard', [(z, z ^ distance) for z in range(COLUMN_DEV...  57.1 us
    ppermute x80, starting transfers between devices, over_dp(): return lax.ppermute(value, 'dp', pairs)  42.1 us
  transfers between devices with their start and end apart: 122, of which 50 were waited for; matrix products, arithmetic and copies ran while one was open for 0% of the time, Pallas kernels for 10%

profile of v5, /device:TPU:0, one launch (start us, length us, event | category | flops | bytes accessed | tf_op | source)
XLA Modules:
  0.0 527.7 jit_solution(7460124297894759563)
XLA Ops:
  15.8 12.9 %collective-permute-done.1.x_bottom.refs_2_ = bf16[256,1792]{1,0:T(8,128)(2,1)} collective-permute-done((bf16[256,1792]{1,0:T(8,128)(2,1)S(1)}, bf16[256,1792]{1,0:T(8,128)(2,1)}, u32[]{:S(2)}, u32[]{:S(2)}) %collective-permute-start.1) | collective-permute-done | bytes 917536 | tf_op jit(solution)/shard_map/ppermute | solution.py:76
  30.3 17.4 %collective-permute-done.x_top.refs_4_ = bf16[256,1792]{1,0:T(8,128)(2,1)} collective-permute-done((bf16[256,1792]{1,0:T(8,128)(2,1)S(1)}, bf16[256,1792]{1,0:T(8,128)(2,1)}, u32[]{:S(2)}, u32[]{:S(2)}) %collective-permute-start) | collective-permute-done | bytes 917536 | tf_op jit(solution)/shard_map/ppermute | solution.py:76
  62.8 5.9 %collective-permute-start.6 = (bf16[7,64,256]{2,1,0:T(8,128)(2,1)S(1)}, bf16[7,64,256]{2,1,0:T(8,128)(2,1)S(1)}, u32[]{:S(2)}, u32[]{:S(2)}) collective-permute-start(bf16[7,64,256]{2,1,0:T(8,128)(2,1)S(1)} %shard_map.42), channel_id=1, source_target_pairs={{0,2},{1,3},{2,0},{3,1},{4,6},{5,7},{6,4},{7,5},{8,10},{9,11},{10,... | collective-permute-start | bytes 688136 | tf_op jit(solution)/shard_map/ppermute | solution.py:316
  71.8 5.5 %collective-permute-done.12.refs_1_ = bf16[5,64,256]{2,1,0:T(8,128)(2,1)S(1)} collective-permute-done((bf16[5,64,256]{2,1,0:T(8,128)(2,1)S(1)}, bf16[5,64,256]{2,1,0:T(8,128)(2,1)S(1)}, u32[]{:S(2)}, u32[]{:S(2)}) %collective-permute-start.12) | collective-permute-done | bytes 163872 | tf_op jit(solution)/shard_map/ppermute | solution.py:316
  80.4 8.8 %collective-permute-done.7.refs_1_ = bf16[5,64,256]{2,1,0:T(8,128)(2,1)S(1)} collective-permute-done((bf16[5,64,256]{2,1,0:T(8,128)(2,1)S(1)}, bf16[5,64,256]{2,1,0:T(8,128)(2,1)S(1)}, u32[]{:S(2)}, u32[]{:S(2)}) %collective-permute-start.7) | collective-permute-done | bytes 163872 | tf_op jit(solution)/shard_map/ppermute | solution.py:316
  113.1 7.6 %collective-permute-done.23.refs_3_ = bf16[5,64,256]{2,1,0:T(8,128)(2,1)S(1)} collective-permute-done((bf16[5,64,256]{2,1,0:T(8,128)(2,1)S(1)}, bf16[5,64,256]{2,1,0:T(8,128)(2,1)S(1)}, u32[]{:S(2)}, u32[]{:S(2)}) %collective-permute-start.23) | collective-permute-done | bytes 163872 | tf_op jit(solution)/shard_map/ppermute | solution.py:316
  120.8 9.4 %collective-permute-done.20 = f32[8,128]{1,0:T(8,128)S(1)} collective-permute-done((f32[8,128]{1,0:T(8,128)S(1)}, f32[8,128]{1,0:T(8,128)S(1)}, u32[]{:S(2)}, u32[]{:S(2)}) %collective-permute-start.20) | collective-permute-done | bytes 4128 | tf_op jit(solution)/shard_map/ppermute | solution.py:76
  137.3 6.2 %collective-permute-done.29.refs_2_ = bf16[7,64,256]{2,1,0:T(8,128)(2,1)S(1)} collective-permute-done((bf16[7,64,256]{2,1,0:T(8,128)(2,1)S(1)}, bf16[7,64,256]{2,1,0:T(8,128)(2,1)S(1)}, u32[]{:S(2)}, u32[]{:S(2)}) %collective-permute-start.29) | collective-permute-done | bytes 229408 | tf_op jit(solution)/shard_map/ppermute | solution.py:316
  145.0 6.6 %collective-permute-done.32.refs_3_ = bf16[7,64,256]{2,1,0:T(8,128)(2,1)S(1)} collective-permute-done((bf16[7,64,256]{2,1,0:T(8,128)(2,1)S(1)}, bf16[7,64,256]{2,1,0:T(8,128)(2,1)S(1)}, u32[]{:S(2)}, u32[]{:S(2)}) %collective-permute-start.32) | collective-permute-done | bytes 229408 | tf_op jit(solution)/shard_map/ppermute | solution.py:316
  155.5 14.6 %collective-permute-done.30.refs_4_ = bf16[5,128,256]{2,1,0:T(8,128)(2,1)S(1)} collective-permute-done((bf16[5,128,256]{2,1,0:T(8,128)(2,1)S(1)}, bf16[5,128,256]{2,1,0:T(8,128)(2,1)S(1)}, u32[]{:S(2)}, u32[]{:S(2)}) %collective-permute-start.30) | collective-permute-done | bytes 327712 | tf_op jit(solution)/shard_map/ppermute | solution.py:76
  193.1 19.3 %collective-permute-done.53.refs_2_ = bf16[256,1792]{1,0:T(8,128)(2,1)S(1)} collective-permute-done((bf16[256,1792]{1,0:T(8,128)(2,1)S(1)}, bf16[256,1792]{1,0:T(8,128)(2,1)S(1)}, u32[]{:S(2)}, u32[]{:S(2)}) %collective-permute-start.53) | collective-permute-done | bytes 917536 | tf_op jit(solution)/shard_map/ppermute | solution.py:76
  212.4 19.1 %collective-permute-done.47.refs_1_ = bf16[256,1792]{1,0:T(8,128)(2,1)S(1)} collective-permute-done((bf16[256,1792]{1,0:T(8,128)(2,1)S(1)}, bf16[256,1792]{1,0:T(8,128)(2,1)S(1)}, u32[]{:S(2)}, u32[]{:S(2)}) %collective-permute-start.47) | collective-permute-done | bytes 917536 | tf_op jit(solution)/shard_map/ppermute | solution.py:76
  233.8 20.2 %collective-permute-done.48.refs_2_ = bf16[256,1792]{1,0:T(8,128)(2,1)S(1)} collective-permute-done((bf16[256,1792]{1,0:T(8,128)(2,1)S(1)}, bf16[256,1792]{1,0:T(8,128)(2,1)S(1)}, u32[]{:S(2)}, u32[]{:S(2)}) %collective-permute-start.48) | collective-permute-done | bytes 917536 | tf_op jit(solution)/shard_map/ppermute | solution.py:76
  274.0 18.1 %collective-permute-done.62.x_bottom.refs_2_ = bf16[256,1792]{1,0:T(8,128)(2,1)S(1)} collective-permute-done((bf16[256,1792]{1,0:T(8,128)(2,1)S(1)}, bf16[256,1792]{1,0:T(8,128)(2,1)S(1)}, u32[]{:S(2)}, u32[]{:S(2)}) %collective-permute-start.62) | collective-permute-done | bytes 917536 | tf_op jit(solution)/shard_map/ppermute | solution.py:76
  292.3 18.6 %collective-permute-done.61.x_top.refs_4_ = bf16[256,1792]{1,0:T(8,128)(2,1)S(1)} collective-permute-done((bf16[256,1792]{1,0:T(8,128)(2,1)S(1)}, bf16[256,1792]{1,0:T(8,128)(2,1)S(1)}, u32[]{:S(2)}, u32[]{:S(2)}) %collective-permute-start.61) | collective-permute-done | bytes 917536 | tf_op jit(solution)/shard_map/ppermute | solution.py:76
  320.2 7.4 %collective-permute-done.66.piece = bf16[7,64,256]{2,1,0:T(8,128)(2,1)S(1)} collective-permute-done((bf16[7,64,256]{2,1,0:T(8,128)(2,1)S(1)}, bf16[7,64,256]{2,1,0:T(8,128)(2,1)S(1)}, u32[]{:S(2)}, u32[]{:S(2)}) %collective-permute-start.66) | collective-permute-done | bytes 229408 | tf_op jit(solution)/shard_map/ppermute | solution.py:316
  331.2 7.3 %collective-permute-done.73.refs_1_ = bf16[5,64,256]{2,1,0:T(8,128)(2,1)S(1)} collective-permute-done((bf16[5,64,256]{2,1,0:T(8,128)(2,1)S(1)}, bf16[5,64,256]{2,1,0:T(8,128)(2,1)S(1)}, u32[]{:S(2)}, u32[]{:S(2)}) %collective-permute-start.73) | collective-permute-done | bytes 163872 | tf_op jit(solution)/shard_map/ppermute | solution.py:316
  341.6 7.3 %collective-permute-done.68.refs_1_ = bf16[5,64,256]{2,1,0:T(8,128)(2,1)S(1)} collective-permute-done((bf16[5,64,256]{2,1,0:T(8,128)(2,1)S(1)}, bf16[5,64,256]{2,1,0:T(8,128)(2,1)S(1)}, u32[]{:S(2)}, u32[]{:S(2)}) %collective-permute-start.68) | collective-permute-done | bytes 163872 | tf_op jit(solution)/shard_map/ppermute | solution.py:316
  371.4 8.2 %collective-permute-done.84.refs_3_ = bf16[5,64,256]{2,1,0:T(8,128)(2,1)S(1)} collective-permute-done((bf16[5,64,256]{2,1,0:T(8,128)(2,1)S(1)}, bf16[5,64,256]{2,1,0:T(8,128)(2,1)S(1)}, u32[]{:S(2)}, u32[]{:S(2)}) %collective-permute-start.84) | collective-permute-done | bytes 163872 | tf_op jit(solution)/shard_map/ppermute | solution.py:316
  379.7 7.9 %collective-permute-done.81 = f32[8,128]{1,0:T(8,128)S(1)} collective-permute-done((f32[8,128]{1,0:T(8,128)S(1)}, f32[8,128]{1,0:T(8,128)S(1)}, u32[]{:S(2)}, u32[]{:S(2)}) %collective-permute-start.81) | collective-permute-done | bytes 4128 | tf_op jit(solution)/shard_map/ppermute | solution.py:76
  414.9 14.2 %collective-permute-done.91.refs_4_ = bf16[5,128,256]{2,1,0:T(8,128)(2,1)S(1)} collective-permute-done((bf16[5,128,256]{2,1,0:T(8,128)(2,1)S(1)}, bf16[5,128,256]{2,1,0:T(8,128)(2,1)S(1)}, u32[]{:S(2)}, u32[]{:S(2)}) %collective-permute-start.91) | collective-permute-done | bytes 327712 | tf_op jit(solution)/shard_map/ppermute | solution.py:76
  449.4 19.3 %collective-permute-done.114.refs_2_ = bf16[256,1792]{1,0:T(8,128)(2,1)S(1)} collective-permute-done((bf16[256,1792]{1,0:T(8,128)(2,1)S(1)}, bf16[256,1792]{1,0:T(8,128)(2,1)S(1)}, u32[]{:S(2)}, u32[]{:S(2)}) %collective-permute-start.114) | collective-permute-done | bytes 917536 | tf_op jit(solution)/shard_map/ppermute | solution.py:76
  468.7 19.1 %collective-permute-done.108.refs_1_ = bf16[256,1792]{1,0:T(8,128)(2,1)S(1)} collective-permute-done((bf16[256,1792]{1,0:T(8,128)(2,1)S(1)}, bf16[256,1792]{1,0:T(8,128)(2,1)S(1)}, u32[]{:S(2)}, u32[]{:S(2)}) %collective-permute-start.108) | collective-permute-done | bytes 917536 | tf_op jit(solution)/shard_map/ppermute | solution.py:76
  490.0 20.2 %collective-permute-done.109.refs_2_ = bf16[256,1792]{1,0:T(8,128)(2,1)S(1)} collective-permute-done((bf16[256,1792]{1,0:T(8,128)(2,1)S(1)}, bf16[256,1792]{1,0:T(8,128)(2,1)S(1)}, u32[]{:S(2)}, u32[]{:S(2)}) %collective-permute-start.109) | collective-permute-done | bytes 917536 | tf_op jit(solution)/shard_map/ppermute | solution.py:76
  (297 shorter events, 225.0 us)
Async XLA Ops:
  8.6 39.1 %collective-permute-start = (bf16[256,1792]{1,0:T(8,128)(2,1)S(1)}, bf16[256,1792]{1,0:T(8,128)(2,1)}, u32[]{:S(2)}, u32[]{:S(2)}) collective-permute-start(bf16[256,1792]{1,0:T(8,128)(2,1)S(1)} %get-tuple-element.123.top.refs_2_.refs_13_.refs_5_), channel_id=1, source_target_pairs={{8,0},{12,4},{4,8},{0,12},{24,16},{28,20},{20,24},{16,28},{9,1},{1... | collective-permute-start | bytes 2752520 | tf_op jit(solution)/shard_map/ppermute | solution.py:76
  9.6 40.0 %collective-permute-start.3 = (bf16[256,1792]{1,0:T(8,128)(2,1)S(1)}, bf16[256,1792]{1,0:T(8,128)(2,1)}, u32[]{:S(2)}, u32[]{:S(2)}) collective-permute-start(bf16[256,1792]{1,0:T(8,128)(2,1)S(1)} %get-tuple-element.122.bottom.refs_3_.refs_14_.refs_6_), channel_id=1, source_target_pairs={{16,0},{20,4},{28,8},{24,12},{4,16},{0,20},{8,24},{12,28},{17,1},{... | collective-permute-start | bytes 2752520 | tf_op jit(solution)/shard_map/ppermute | solution.py:76
  14.1 45.5 %collective-permute-start.13 = (bf16[5,64,256]{2,1,0:T(8,128)(2,1)S(1)}, bf16[5,64,256]{2,1,0:T(8,128)(2,1)S(1)}, u32[]{:S(2)}, u32[]{:S(2)}) collective-permute-start(bf16[5,64,256]{2,1,0:T(8,128)(2,1)S(1)} %get-tuple-element.75), channel_id=1, source_target_pairs={{0,1},{1,0},{2,3},{3,2},{4,5},{5,4},{6,7},{7,6},{8,9},{9,8},{10,11... | collective-permute-start | bytes 491528 | tf_op jit(solution)/shard_map/ppermute | solution.py:316
  107.9 43.7 %collective-permute-start.40 = (bf16[256,1792]{1,0:T(8,128)(2,1)}, bf16[256,1792]{1,0:T(8,128)(2,1)S(1)}, u32[]{:S(2)}, u32[]{:S(2)}) collective-permute-start(bf16[256,1792]{1,0:T(8,128)(2,1)} %collective-permute-done.1.x_bottom.refs_2_), channel_id=1, source_target_pairs={{0,16},{4,20},{8,28},{12,24},{16,4},{20,0},{24,8},{28,12},{1,17},{... | collective-permute-start | bytes 2752520 | tf_op jit(solution)/shard_map/ppermute | solution.py:76
  109.0 44.5 %collective-permute-start.39 = (bf16[256,1792]{1,0:T(8,128)(2,1)S(1)}, bf16[256,1792]{1,0:T(8,128)(2,1)S(1)}, u32[]{:S(2)}, u32[]{:S(2)}) collective-permute-start(bf16[256,1792]{1,0:T(8,128)(2,1)S(1)} %collective-permute-done.2.y_top.refs_3_), channel_id=1, source_target_pairs={{0,8},{4,12},{8,4},{12,0},{16,24},{20,28},{24,20},{28,16},{1,9},{5... | collective-permute-start | bytes 2752520 | tf_op jit(solution)/shard_map/ppermute | solution.py:76
  120.7 32.8 %collective-permute-start.36 = (bf16[256,1792]{1,0:T(8,128)(2,1)}, bf16[256,1792]{1,0:T(8,128)(2,1)S(1)}, u32[]{:S(2)}, u32[]{:S(2)}) collective-permute-start(bf16[256,1792]{1,0:T(8,128)(2,1)} %collective-permute-done.1.x_bottom.refs_2_), channel_id=1, source_target_pairs={{0,4},{4,0},{8,12},{12,8},{16,20},{20,16},{24,28},{28,24},{1,5},{5... | collective-permute-start | bytes 2752520 | tf_op jit(solution)/shard_map/ppermute | solution.py:76
  189.2 42.3 %collective-permute-start.47 = (bf16[256,1792]{1,0:T(8,128)(2,1)S(1)}, bf16[256,1792]{1,0:T(8,128)(2,1)S(1)}, u32[]{:S(2)}, u32[]{:S(2)}) collective-permute-start(bf16[256,1792]{1,0:T(8,128)(2,1)S(1)} %get-tuple-element.90.refs_3_), channel_id=1, source_target_pairs={{8,0},{12,4},{4,8},{0,12},{24,16},{28,20},{20,24},{16,28},{9,1},{1... | collective-permute-start | bytes 2752520 | tf_op jit(solution)/shard_map/ppermute | solution.py:76
  191.0 40.6 %collective-permute-start.50 = (bf16[256,1792]{1,0:T(8,128)(2,1)S(1)}, bf16[256,1792]{1,0:T(8,128)(2,1)S(1)}, u32[]{:S(2)}, u32[]{:S(2)}) collective-permute-start(bf16[256,1792]{1,0:T(8,128)(2,1)S(1)} %get-tuple-element.91.refs_2_), channel_id=1, source_target_pairs={{16,0},{20,4},{28,8},{24,12},{4,16},{0,20},{8,24},{12,28},{17,1},{... | collective-permute-start | bytes 2752520 | tf_op jit(solution)/shard_map/ppermute | solution.py:76
  191.0 41.5 %collective-permute-start.60 = (bf16[256,1792]{1,0:T(8,128)(2,1)S(1)}, bf16[256,1792]{1,0:T(8,128)(2,1)S(1)}, u32[]{:S(2)}, u32[]{:S(2)}) collective-permute-start(bf16[256,1792]{1,0:T(8,128)(2,1)S(1)} %get-tuple-element.90.refs_3_), channel_id=1, source_target_pairs={{0,4},{4,0},{8,12},{12,8},{16,20},{20,16},{24,28},{28,24},{1,5},{5... | collective-permute-start | bytes 2752520 | tf_op jit(solution)/shard_map/ppermute | solution.py:76
  191.6 41.7 %collective-permute-start.54 = (bf16[256,1792]{1,0:T(8,128)(2,1)S(1)}, bf16[256,1792]{1,0:T(8,128)(2,1)S(1)}, u32[]{:S(2)}, u32[]{:S(2)}) collective-permute-start(bf16[256,1792]{1,0:T(8,128)(2,1)S(1)} %get-tuple-element.90.refs_3_), channel_id=1, source_target_pairs={{16,0},{20,4},{28,8},{24,12},{4,16},{0,20},{8,24},{12,28},{17,1},{... | collective-permute-start | bytes 2752520 | tf_op jit(solution)/shard_map/ppermute | solution.py:76
  270.4 40.5 %collective-permute-start.61 = (bf16[256,1792]{1,0:T(8,128)(2,1)S(1)}, bf16[256,1792]{1,0:T(8,128)(2,1)S(1)}, u32[]{:S(2)}, u32[]{:S(2)}) collective-permute-start(bf16[256,1792]{1,0:T(8,128)(2,1)S(1)} %get-tuple-element.92.top.refs_2_.refs_13_.refs_5_), channel_id=1, source_target_pairs={{8,0},{12,4},{4,8},{0,12},{24,16},{28,20},{20,24},{16,28},{9,1},{1... | collective-permute-start | bytes 2752520 | tf_op jit(solution)/shard_map/ppermute | solution.py:76
  270.8 40.3 %collective-permute-start.64 = (bf16[256,1792]{1,0:T(8,128)(2,1)S(1)}, bf16[256,1792]{1,0:T(8,128)(2,1)S(1)}, u32[]{:S(2)}, u32[]{:S(2)}) collective-permute-start(bf16[256,1792]{1,0:T(8,128)(2,1)S(1)} %get-tuple-element.93.bottom.refs_3_.refs_14_.refs_6_), channel_id=1, source_target_pairs={{16,0},{20,4},{28,8},{24,12},{4,16},{0,20},{8,24},{12,28},{17,1},{... | collective-permute-start | bytes 2752520 | tf_op jit(solution)/shard_map/ppermute | solution.py:76
  273.8 43.4 %collective-permute-start.74 = (bf16[5,64,256]{2,1,0:T(8,128)(2,1)S(1)}, bf16[5,64,256]{2,1,0:T(8,128)(2,1)S(1)}, u32[]{:S(2)}, u32[]{:S(2)}) collective-permute-start(bf16[5,64,256]{2,1,0:T(8,128)(2,1)S(1)} %get-tuple-element.105), channel_id=1, source_target_pairs={{0,1},{1,0},{2,3},{3,2},{4,5},{5,4},{6,7},{7,6},{8,9},{9,8},{10,11... | collective-permute-start | bytes 491528 | tf_op jit(solution)/shard_map/ppermute | solution.py:316
  318.6 33.9 %collective-permute-start.65 = (bf16[7,64,256]{2,1,0:T(8,128)(2,1)S(1)}, bf16[7,64,256]{2,1,0:T(8,128)(2,1)S(1)}, u32[]{:S(2)}, u32[]{:S(2)}) collective-permute-start(bf16[7,64,256]{2,1,0:T(8,128)(2,1)S(1)} %get-tuple-element.95), channel_id=1, source_target_pairs={{0,1},{1,0},{2,3},{3,2},{4,5},{5,4},{6,7},{7,6},{8,9},{9,8},{10,11... | collective-permute-start | bytes 688136 | tf_op jit(solution)/shard_map/ppermute | solution.py:316
  365.8 44.9 %collective-permute-start.101 = (bf16[256,1792]{1,0:T(8,128)(2,1)S(1)}, bf16[256,1792]{1,0:T(8,128)(2,1)S(1)}, u32[]{:S(2)}, u32[]{:S(2)}) collective-permute-start(bf16[256,1792]{1,0:T(8,128)(2,1)S(1)} %collective-permute-done.62.x_bottom.refs_2_), channel_id=1, source_target_pairs={{0,16},{4,20},{8,28},{12,24},{16,4},{20,0},{24,8},{28,12},{1,17},{... | collective-permute-start | bytes 2752520 | tf_op jit(solution)/shard_map/ppermute | solution.py:76
  366.8 45.7 %collective-permute-start.100 = (bf16[256,1792]{1,0:T(8,128)(2,1)S(1)}, bf16[256,1792]{1,0:T(8,128)(2,1)S(1)}, u32[]{:S(2)}, u32[]{:S(2)}) collective-permute-start(bf16[256,1792]{1,0:T(8,128)(2,1)S(1)} %collective-permute-done.63.y_top.refs_3_), channel_id=1, source_target_pairs={{0,8},{4,12},{8,4},{12,0},{16,24},{20,28},{24,20},{28,16},{1,9},{5... | collective-permute-start | bytes 2752520 | tf_op jit(solution)/shard_map/ppermute | solution.py:76
  379.6 32.9 %collective-permute-start.96 = (bf16[256,1792]{1,0:T(8,128)(2,1)S(1)}, bf16[256,1792]{1,0:T(8,128)(2,1)S(1)}, u32[]{:S(2)}, u32[]{:S(2)}) collective-permute-start(bf16[256,1792]{1,0:T(8,128)(2,1)S(1)} %collective-permute-done.61.x_top.refs_4_), channel_id=1, source_target_pairs={{0,4},{4,0},{8,12},{12,8},{16,20},{20,16},{24,28},{28,24},{1,5},{5... | collective-permute-start | bytes 2752520 | tf_op jit(solution)/shard_map/ppermute | solution.py:76
  445.4 42.3 %collective-permute-start.108 = (bf16[256,1792]{1,0:T(8,128)(2,1)S(1)}, bf16[256,1792]{1,0:T(8,128)(2,1)S(1)}, u32[]{:S(2)}, u32[]{:S(2)}) collective-permute-start(bf16[256,1792]{1,0:T(8,128)(2,1)S(1)} %get-tuple-element.120.refs_3_), channel_id=1, source_target_pairs={{8,0},{12,4},{4,8},{0,12},{24,16},{28,20},{20,24},{16,28},{9,1},{1... | collective-permute-start | bytes 2752520 | tf_op jit(solution)/shard_map/ppermute | solution.py:76
  447.2 40.6 %collective-permute-start.111 = (bf16[256,1792]{1,0:T(8,128)(2,1)S(1)}, bf16[256,1792]{1,0:T(8,128)(2,1)S(1)}, u32[]{:S(2)}, u32[]{:S(2)}) collective-permute-start(bf16[256,1792]{1,0:T(8,128)(2,1)S(1)} %get-tuple-element.121.refs_2_), channel_id=1, source_target_pairs={{16,0},{20,4},{28,8},{24,12},{4,16},{0,20},{8,24},{12,28},{17,1},{... | collective-permute-start | bytes 2752520 | tf_op jit(solution)/shard_map/ppermute | solution.py:76
  447.2 41.6 %collective-permute-start.121 = (bf16[256,1792]{1,0:T(8,128)(2,1)S(1)}, bf16[256,1792]{1,0:T(8,128)(2,1)S(1)}, u32[]{:S(2)}, u32[]{:S(2)}) collective-permute-start(bf16[256,1792]{1,0:T(8,128)(2,1)S(1)} %get-tuple-element.120.refs_3_), channel_id=1, source_target_pairs={{0,4},{4,0},{8,12},{12,8},{16,20},{20,16},{24,28},{28,24},{1,5},{5... | collective-permute-start | bytes 2752520 | tf_op jit(solution)/shard_map/ppermute | solution.py:76
  447.8 41.7 %collective-permute-start.115 = (bf16[256,1792]{1,0:T(8,128)(2,1)S(1)}, bf16[256,1792]{1,0:T(8,128)(2,1)S(1)}, u32[]{:S(2)}, u32[]{:S(2)}) collective-permute-start(bf16[256,1792]{1,0:T(8,128)(2,1)S(1)} %get-tuple-element.120.refs_3_), channel_id=1, source_target_pairs={{16,0},{20,4},{28,8},{24,12},{4,16},{0,20},{8,24},{12,28},{17,1},{... | collective-permute-start | bytes 2752520 | tf_op jit(solution)/shard_map/ppermute | solution.py:76
  488.8 29.4 %collective-permute-start.117 = (bf16[256,1792]{1,0:T(8,128)(2,1)S(1)}, bf16[256,1792]{1,0:T(8,128)(2,1)S(1)}, u32[]{:S(2)}, u32[]{:S(2)}) collective-permute-start(bf16[256,1792]{1,0:T(8,128)(2,1)S(1)} %collective-permute-done.108.refs_1_), channel_id=1, source_target_pairs={{0,4},{4,0},{8,12},{12,8},{16,20},{20,16},{24,28},{28,24},{1,5},{5... | collective-permute-start | bytes 2752520 | tf_op jit(solution)/shard_map/ppermute | solution.py:76
  489.5 28.8 %collective-permute-start.118 = (bf16[256,1792]{1,0:T(8,128)(2,1)S(1)}, bf16[256,1792]{1,0:T(8,128)(2,1)S(1)}, u32[]{:S(2)}, u32[]{:S(2)}) collective-permute-start(bf16[256,1792]{1,0:T(8,128)(2,1)S(1)} %collective-permute-done.111.refs_2_), channel_id=1, source_target_pairs={{0,4},{4,0},{8,12},{12,8},{16,20},{20,16},{24,28},{28,24},{1,5},{5... | collective-permute-start | bytes 2752520 | tf_op jit(solution)/shard_map/ppermute | solution.py:76
  489.5 28.8 %collective-permute-start.119 = (bf16[256,1792]{1,0:T(8,128)(2,1)S(1)}, bf16[256,1792]{1,0:T(8,128)(2,1)S(1)}, u32[]{:S(2)}, u32[]{:S(2)}) collective-permute-start(bf16[256,1792]{1,0:T(8,128)(2,1)S(1)} %collective-permute-done.115.refs_3_), channel_id=1, source_target_pairs={{0,4},{4,0},{8,12},{12,8},{16,20},{20,16},{24,28},{28,24},{1,5},{5... | collective-permute-start | bytes 2752520 | tf_op jit(solution)/shard_map/ppermute | solution.py:76
  (103 other events, 1592.8 us)

commit v6 on v5

--- a/solution.py
+++ b/solution.py
@@ -317,10 +317,9 @@
 
 
 def total_of(value):
-    value = value + exchanged(value, 1) + (exchanged(value, 2) + exchanged(value, 3))
-    for step in (1, 2, 4):
-        value = value + over_dp(value, [(i, i ^ step) for i in range(ROW_DEVICES)])
-    return value
+    value = value + over_dp(value, CORE)
+    x_side, y_side, diagonal = (over_dp(value, [(i, i ^ k) for i in range(ROW_DEVICES)]) for k in (2, 4, 6))
+    return (value + x_side) + (y_side + diagonal)
 
 
 def gather(block):
@@ -336,33 +335,36 @@
     return core, (x_bottom, y_top), (x_top, y_bottom), side, (d_sel_top, d_oth_bottom), crossed
 
 
-def add_kernel(kept, piece, out):
-    out[...] = (kept[...] + piece[...].astype(f32)).astype(out.dtype)
-
-
-def fold_kernel(weights, *refs):
-    kept, *pieces, before, out, squares = refs
+def add_kernel(kept, *refs):
     total = kept[...]
-    for piece in pieces:
+    for piece in refs[:-1]:
         total = total + piece[...].astype(f32)
-    part = total.astype(bf16)
-    out[...] = part
-    total = before[...]
-    for index, weight in enumerate(weights):
-        square = jnp.square(part[index].astype(f32))
-        square = sum(square[:, k : k + 128] for k in range(0, square.shape[1], 128))
-        total = total + weight * jnp.sum(square.reshape(-1, 8, 128), axis=0)
-    squares[...] = total
-
-
-def reduce_parts(pieces, before, weights):
+    refs[-1][...] = total.astype(bf16)
+
+
+def reduce_parts(pieces):
     kept, one, passed, three = pieces
     three, one = exchanged(three, 1), exchanged(one, 1)
     out = jax.ShapeDtypeStruct(kept.shape, bf16)
     (two,) = call(add_kernel, [out], [passed, three])
     two = exchanged(two, 2)
-    outs = [out, jax.ShapeDtypeStruct(before.shape, f32)]
-    return call(functools.partial(fold_kernel, weights), outs, [kept, one, two, before])
+    return call(add_kernel, [out], [kept, one, two])[0]
+
+
+def squares_kernel(weights, *refs):
+    *parts, before, out = refs
+    total = before[...]
+    for part, part_weights in zip(parts, weights):
+        for weight in sorted(set(part_weights)):
+            square = sum(jnp.square(part[q].astype(f32)) for q, w in enumerate(part_weights) if w == weight)
+            square = sum(square[:, k : k + 128] for k in range(0, square.shape[1], 128))
+            total = total + weight * jnp.sum(square.reshape(-1, 8, 128), axis=0)
+    out[...] = total
+
+
+def squares_of(parts, weights, before):
+    out = jax.ShapeDtypeStruct(before.shape, f32)
+    return call(functools.partial(squares_kernel, weights), [out], [*parts, before])[0]
 
 
 def spread(part):
@@ -378,17 +380,20 @@
     (x_bottom, y_top), (x_top, y_bottom) = one, two
     half = matrix[0].shape[0]
     own_pieces = gram(own_gram_kernel, (5, half, half), [z, side_index], [*matrix, *core])
-    own_part, squares = reduce_parts(own_pieces, jnp.zeros((8, 128), f32), (1.0, 1.0, 2.0, 2.0, 2.0))
+    own_part = reduce_parts(own_pieces)
     own_parts = spread(own_part)
     early_pieces = gram(early_gram_kernel, (5, half, half), [z], [*matrix, x_bottom, y_top])
-    early_part, squares = reduce_parts(early_pieces, squares, (2.0,) * 5)
+    early_part = reduce_parts(early_pieces)
     late_pieces = gram(
         late_gram_kernel, (7, half, half), [z], [*matrix, x_top, x_bottom, y_top, y_bottom]
     )
-    late_part, squares = reduce_parts(late_pieces, squares, (2.0,) * 7)
-    squares = total_of(squares)
+    late_part = reduce_parts(late_pieces)
     early_parts = spread(early_part)
     late_parts = spread(late_part)
+    weights = [(1.0, 1.0, 2.0, 2.0, 2.0)] * 4 + [(2.0,) * 5] * 4 + [(2.0,) * 7] * 3
+    squares = squares_of([*own_parts, *early_parts, *late_parts[:3]], weights, jnp.zeros((8, 128), f32))
+    squares = squares_of(late_parts[3:], [(2.0,) * 7], squares)
+    squares = total_of(squares)
     near_one, x_whole, y_whole = near_assemble(z, early_parts, True)
     early = over_dp(x_whole, GIVE_X), over_dp(y_whole, GIVE_Y)
     late = []

time: 528 us -> 525 us (level)
  waiting for transfers between devices: 348 us -> 335 us
  starting transfers between devices: 99.2 us -> 109 us
    ppermute x80 -> x82, waiting for transfers between devices: 264 us -> 247 us  [over_dp(): return lax.ppermute(value, 'dp', pairs)]
    ppermute x80 -> x82, starting transfers between devices: 42.1 us -> 50.1 us  [over_dp(): return lax.ppermute(value, 'dp', pairs)]
    ppermute x42 -> x36, waiting for transfers between devices: 84.2 us -> 87.9 us  [exchanged(): lax.ppermute(value, 'shard', [(z, z ^ distance) for z in range(COLUMN_DEV...]
    ppermute x42 -> x36, starting transfers between devices: 57.1 us -> 58.5 us  [exchanged(): lax.ppermute(value, 'shard', [(z, z ^ distance) for z in range(COLUMN_DEV...]
    pallas_call x44 -> x48, Pallas kernels: 71.2 us -> 71.6 us  [call(): pl.pallas_call(kernel, out_shape=outs, in_specs=[pl.BlockSpec(memory_spac...]
  transfers between devices with their start and end apart: 122 -> 118, of which waited for: 50 -> 48; matrix products, arithmetic and copies ran while one was open for 0% -> 0% of each run, Pallas kernels for 10% -> 11%
where the time goes in v6:
time: 525 us
  waiting for transfers between devices  335 us (64%)
  starting transfers between devices  109 us (21%)
  Pallas kernels  71.6 us (14%)
  other arithmetic  5.65 us (1%)
    ppermute x82, waiting for transfers between devices, over_dp(): return lax.ppermute(value, 'dp', pairs)  247 us
    ppermute x36, waiting for transfers between devices, exchanged(): lax.ppermute(value, 'shard', [(z, z ^ distance) for z in range(COLUMN_DEV...  87.9 us
    pallas_call x48, Pallas kernels, call(): pl.pallas_call(kernel, out_shape=outs, in_specs=[pl.BlockSpec(memory_spac...  71.6 us
    ppermute x36, starting transfers between devices, exchanged(): lax.ppermute(value, 'shard', [(z, z ^ distance) for z in range(COLUMN_DEV...  58.5 us
    ppermute x82, starting transfers between devices, over_dp(): return lax.ppermute(value, 'dp', pairs)  50.1 us
  transfers between devices with their start and end apart: 118, of which 48 were waited for; matrix products, arithmetic and copies ran while one was open for 0% of the time, Pallas kernels for 11%

profile of v6, /device:TPU:0, one launch (start us, length us, event | category | flops | bytes accessed | tf_op | source)
XLA Modules:
  0.0 524.9 jit_solution(3324063038119752652)
XLA Ops:
  15.8 12.9 %collective-permute-done.1.x_bottom.refs_2_ = bf16[256,1792]{1,0:T(8,128)(2,1)} collective-permute-done((bf16[256,1792]{1,0:T(8,128)(2,1)S(1)}, bf16[256,1792]{1,0:T(8,128)(2,1)}, u32[]{:S(2)}, u32[]{:S(2)}) %collective-permute-start.1) | collective-permute-done | bytes 917536 | tf_op jit(solution)/shard_map/ppermute | solution.py:76
  30.3 17.4 %collective-permute-done.x_top.refs_4_ = bf16[256,1792]{1,0:T(8,128)(2,1)} collective-permute-done((bf16[256,1792]{1,0:T(8,128)(2,1)S(1)}, bf16[256,1792]{1,0:T(8,128)(2,1)}, u32[]{:S(2)}, u32[]{:S(2)}) %collective-permute-start) | collective-permute-done | bytes 917536 | tf_op jit(solution)/shard_map/ppermute | solution.py:76
  62.8 5.5 %collective-permute-done.18.refs_0_ = bf16[5,64,256]{2,1,0:T(8,128)(2,1)S(1)} collective-permute-done((bf16[5,64,256]{2,1,0:T(8,128)(2,1)S(1)}, bf16[5,64,256]{2,1,0:T(8,128)(2,1)S(1)}, u32[]{:S(2)}, u32[]{:S(2)}) %collective-permute-start.18) | collective-permute-done | bytes 163872 | tf_op jit(solution)/shard_map/ppermute | solution.py:316
  88.8 8.0 %collective-permute-done.6.refs_1_ = bf16[7,64,256]{2,1,0:T(8,128)(2,1)S(1)} collective-permute-done((bf16[7,64,256]{2,1,0:T(8,128)(2,1)S(1)}, bf16[7,64,256]{2,1,0:T(8,128)(2,1)S(1)}, u32[]{:S(2)}, u32[]{:S(2)}) %collective-permute-start.6) | collective-permute-done | bytes 229408 | tf_op jit(solution)/shard_map/ppermute | solution.py:316
  122.3 6.2 %collective-permute-done.23.refs_9_.refs_1_ = bf16[7,64,256]{2,1,0:T(8,128)(2,1)S(1)} collective-permute-done((bf16[7,64,256]{2,1,0:T(8,128)(2,1)S(1)}, bf16[7,64,256]{2,1,0:T(8,128)(2,1)S(1)}, u32[]{:S(2)}, u32[]{:S(2)}) %collective-permute-start.23) | collective-permute-done | bytes 229408 | tf_op jit(solution)/shard_map/ppermute | solution.py:316
  131.3 5.4 %collective-permute-done.30.refs_2_ = bf16[5,64,256]{2,1,0:T(8,128)(2,1)S(1)} collective-permute-done((bf16[5,64,256]{2,1,0:T(8,128)(2,1)S(1)}, bf16[5,64,256]{2,1,0:T(8,128)(2,1)S(1)}, u32[]{:S(2)}, u32[]{:S(2)}) %collective-permute-start.30) | collective-permute-done | bytes 163872 | tf_op jit(solution)/shard_map/ppermute | solution.py:76
  154.2 10.0 %collective-permute-done.27 = f32[8,128]{1,0:T(8,128)S(1)} collective-permute-done((f32[8,128]{1,0:T(8,128)S(1)}, f32[8,128]{1,0:T(8,128)S(1)}, u32[]{:S(2)}, u32[]{:S(2)}) %collective-permute-start.27) | collective-permute-done | bytes 4128 | tf_op jit(solution)/shard_map/ppermute | solution.py:76
  190.1 19.3 %collective-permute-done.51.refs_2_ = bf16[256,1792]{1,0:T(8,128)(2,1)S(1)} collective-permute-done((bf16[256,1792]{1,0:T(8,128)(2,1)S(1)}, bf16[256,1792]{1,0:T(8,128)(2,1)S(1)}, u32[]{:S(2)}, u32[]{:S(2)}) %collective-permute-start.51) | collective-permute-done | bytes 917536 | tf_op jit(solution)/shard_map/ppermute | solution.py:76
  209.4 19.1 %collective-permute-done.45.refs_1_ = bf16[256,1792]{1,0:T(8,128)(2,1)S(1)} collective-permute-done((bf16[256,1792]{1,0:T(8,128)(2,1)S(1)}, bf16[256,1792]{1,0:T(8,128)(2,1)S(1)}, u32[]{:S(2)}, u32[]{:S(2)}) %collective-permute-start.45) | collective-permute-done | bytes 917536 | tf_op jit(solution)/shard_map/ppermute | solution.py:76
  230.8 20.1 %collective-permute-done.46.refs_2_ = bf16[256,1792]{1,0:T(8,128)(2,1)S(1)} collective-permute-done((bf16[256,1792]{1,0:T(8,128)(2,1)S(1)}, bf16[256,1792]{1,0:T(8,128)(2,1)S(1)}, u32[]{:S(2)}, u32[]{:S(2)}) %collective-permute-start.46) | collective-permute-done | bytes 917536 | tf_op jit(solution)/shard_map/ppermute | solution.py:76
  272.3 16.5 %collective-permute-done.59.x_top.refs_4_ = bf16[256,1792]{1,0:T(8,128)(2,1)S(1)} collective-permute-done((bf16[256,1792]{1,0:T(8,128)(2,1)S(1)}, bf16[256,1792]{1,0:T(8,128)(2,1)S(1)}, u32[]{:S(2)}, u32[]{:S(2)}) %collective-permute-start.59) | collective-permute-done | bytes 917536 | tf_op jit(solution)/shard_map/ppermute | solution.py:76
  288.8 18.9 %collective-permute-done.60.x_bottom.refs_2_ = bf16[256,1792]{1,0:T(8,128)(2,1)S(1)} collective-permute-done((bf16[256,1792]{1,0:T(8,128)(2,1)S(1)}, bf16[256,1792]{1,0:T(8,128)(2,1)S(1)}, u32[]{:S(2)}, u32[]{:S(2)}) %collective-permute-start.60) | collective-permute-done | bytes 917536 | tf_op jit(solution)/shard_map/ppermute | solution.py:76
  320.4 6.8 %collective-permute-done.77.refs_0_ = bf16[5,64,256]{2,1,0:T(8,128)(2,1)S(1)} collective-permute-done((bf16[5,64,256]{2,1,0:T(8,128)(2,1)S(1)}, bf16[5,64,256]{2,1,0:T(8,128)(2,1)S(1)}, u32[]{:S(2)}, u32[]{:S(2)}) %collective-permute-start.77) | collective-permute-done | bytes 163872 | tf_op jit(solution)/shard_map/ppermute | solution.py:316
  348.3 7.4 %collective-permute-done.65.refs_1_ = bf16[7,64,256]{2,1,0:T(8,128)(2,1)S(1)} collective-permute-done((bf16[7,64,256]{2,1,0:T(8,128)(2,1)S(1)}, bf16[7,64,256]{2,1,0:T(8,128)(2,1)S(1)}, u32[]{:S(2)}, u32[]{:S(2)}) %collective-permute-start.65) | collective-permute-done | bytes 229408 | tf_op jit(solution)/shard_map/ppermute | solution.py:316
  358.8 5.3 %collective-permute-done.74.refs_2_ = bf16[5,64,256]{2,1,0:T(8,128)(2,1)S(1)} collective-permute-done((bf16[5,64,256]{2,1,0:T(8,128)(2,1)S(1)}, bf16[5,64,256]{2,1,0:T(8,128)(2,1)S(1)}, u32[]{:S(2)}, u32[]{:S(2)}) %collective-permute-start.74) | collective-permute-done | bytes 163872 | tf_op jit(solution)/shard_map/ppermute | solution.py:316
  370.1 5.3 %collective-permute-done.75.refs_3_ = bf16[5,64,256]{2,1,0:T(8,128)(2,1)S(1)} collective-permute-done((bf16[5,64,256]{2,1,0:T(8,128)(2,1)S(1)}, bf16[5,64,256]{2,1,0:T(8,128)(2,1)S(1)}, u32[]{:S(2)}, u32[]{:S(2)}) %collective-permute-start.75) | collective-permute-done | bytes 163872 | tf_op jit(solution)/shard_map/ppermute | solution.py:316
  379.5 6.2 %collective-permute-done.82.refs_9_.refs_1_ = bf16[7,64,256]{2,1,0:T(8,128)(2,1)S(1)} collective-permute-done((bf16[7,64,256]{2,1,0:T(8,128)(2,1)S(1)}, bf16[7,64,256]{2,1,0:T(8,128)(2,1)S(1)}, u32[]{:S(2)}, u32[]{:S(2)}) %collective-permute-start.82) | collective-permute-done | bytes 229408 | tf_op jit(solution)/shard_map/ppermute | solution.py:316
  388.7 6.3 %collective-permute-done.89.refs_2_ = bf16[5,64,256]{2,1,0:T(8,128)(2,1)S(1)} collective-permute-done((bf16[5,64,256]{2,1,0:T(8,128)(2,1)S(1)}, bf16[5,64,256]{2,1,0:T(8,128)(2,1)S(1)}, u32[]{:S(2)}, u32[]{:S(2)}) %collective-permute-start.89) | collective-permute-done | bytes 163872 | tf_op jit(solution)/shard_map/ppermute | solution.py:76
  395.5 5.6 %collective-permute-done.90.refs_3_ = bf16[5,64,256]{2,1,0:T(8,128)(2,1)S(1)} collective-permute-done((bf16[5,64,256]{2,1,0:T(8,128)(2,1)S(1)}, bf16[5,64,256]{2,1,0:T(8,128)(2,1)S(1)}, u32[]{:S(2)}, u32[]{:S(2)}) %collective-permute-start.90) | collective-permute-done | bytes 163872 | tf_op jit(solution)/shard_map/ppermute | solution.py:76
  412.9 9.9 %collective-permute-done.86 = f32[8,128]{1,0:T(8,128)S(1)} collective-permute-done((f32[8,128]{1,0:T(8,128)S(1)}, f32[8,128]{1,0:T(8,128)S(1)}, u32[]{:S(2)}, u32[]{:S(2)}) %collective-permute-start.86) | collective-permute-done | bytes 4128 | tf_op jit(solution)/shard_map/ppermute | solution.py:76
  436.7 5.2 shard_map.83
  446.0 19.3 %collective-permute-done.110.refs_2_ = bf16[256,1792]{1,0:T(8,128)(2,1)S(1)} collective-permute-done((bf16[256,1792]{1,0:T(8,128)(2,1)S(1)}, bf16[256,1792]{1,0:T(8,128)(2,1)S(1)}, u32[]{:S(2)}, u32[]{:S(2)}) %collective-permute-start.110) | collective-permute-done | bytes 917536 | tf_op jit(solution)/shard_map/ppermute | solution.py:76
  465.4 19.1 %collective-permute-done.104.refs_1_ = bf16[256,1792]{1,0:T(8,128)(2,1)S(1)} collective-permute-done((bf16[256,1792]{1,0:T(8,128)(2,1)S(1)}, bf16[256,1792]{1,0:T(8,128)(2,1)S(1)}, u32[]{:S(2)}, u32[]{:S(2)}) %collective-permute-start.104) | collective-permute-done | bytes 917536 | tf_op jit(solution)/shard_map/ppermute | solution.py:76
  487.6 19.2 %collective-permute-done.105.refs_2_ = bf16[256,1792]{1,0:T(8,128)(2,1)S(1)} collective-permute-done((bf16[256,1792]{1,0:T(8,128)(2,1)S(1)}, bf16[256,1792]{1,0:T(8,128)(2,1)S(1)}, u32[]{:S(2)}, u32[]{:S(2)}) %collective-permute-start.105) | collective-permute-done | bytes 917536 | tf_op jit(solution)/shard_map/ppermute | solution.py:76
  (289 shorter events, 248.3 us)
Async XLA Ops:
  8.6 39.1 %collective-permute-start = (bf16[256,1792]{1,0:T(8,128)(2,1)S(1)}, bf16[256,1792]{1,0:T(8,128)(2,1)}, u32[]{:S(2)}, u32[]{:S(2)}) collective-permute-start(bf16[256,1792]{1,0:T(8,128)(2,1)S(1)} %get-tuple-element.99.top.refs_2_.refs_13_.refs_5_), channel_id=1, source_target_pairs={{8,0},{12,4},{4,8},{0,12},{24,16},{28,20},{20,24},{16,28},{9,1},{1... | collective-permute-start | bytes 2752520 | tf_op jit(solution)/shard_map/ppermute | solution.py:76
  9.6 40.0 %collective-permute-start.3 = (bf16[256,1792]{1,0:T(8,128)(2,1)S(1)}, bf16[256,1792]{1,0:T(8,128)(2,1)}, u32[]{:S(2)}, u32[]{:S(2)}) collective-permute-start(bf16[256,1792]{1,0:T(8,128)(2,1)S(1)} %get-tuple-element.98.bottom.refs_3_.refs_14_.refs_6_), channel_id=1, source_target_pairs={{16,0},{20,4},{28,8},{24,12},{4,16},{0,20},{8,24},{12,28},{17,1},{... | collective-permute-start | bytes 2752520 | tf_op jit(solution)/shard_map/ppermute | solution.py:76
  14.1 45.5 %collective-permute-start.12 = (bf16[5,64,256]{2,1,0:T(8,128)(2,1)S(1)}, bf16[5,64,256]{2,1,0:T(8,128)(2,1)S(1)}, u32[]{:S(2)}, u32[]{:S(2)}) collective-permute-start(bf16[5,64,256]{2,1,0:T(8,128)(2,1)S(1)} %get-tuple-element.59), channel_id=1, source_target_pairs={{0,1},{1,0},{2,3},{3,2},{4,5},{5,4},{6,7},{7,6},{8,9},{9,8},{10,11... | collective-permute-start | bytes 491528 | tf_op jit(solution)/shard_map/ppermute | solution.py:316
  80.0 29.4 %collective-permute-start.21 = (bf16[5,64,256]{2,1,0:T(8,128)(2,1)S(1)}, bf16[5,64,256]{2,1,0:T(8,128)(2,1)S(1)}, u32[]{:S(2)}, u32[]{:S(2)}) collective-permute-start(bf16[5,64,256]{2,1,0:T(8,128)(2,1)S(1)} %shard_map.49.refs_4_.refs_0_), channel_id=1, source_target_pairs={{0,2},{1,3},{2,0},{3,1},{4,6},{5,7},{6,4},{7,5},{8,10},{9,11},{10,... | collective-permute-start | bytes 491528 | tf_op jit(solution)/shard_map/ppermute | solution.py:316
  109.7 34.3 %collective-permute-start.41 = (bf16[256,1792]{1,0:T(8,128)(2,1)}, bf16[256,1792]{1,0:T(8,128)(2,1)S(1)}, u32[]{:S(2)}, u32[]{:S(2)}) collective-permute-start(bf16[256,1792]{1,0:T(8,128)(2,1)} %collective-permute-done.1.x_bottom.refs_2_), channel_id=1, source_target_pairs={{0,16},{4,20},{8,28},{12,24},{16,4},{20,0},{24,8},{28,12},{1,17},{... | collective-permute-start | bytes 2752520 | tf_op jit(solution)/shard_map/ppermute | solution.py:76
  114.9 30.0 %collective-permute-start.40 = (bf16[256,1792]{1,0:T(8,128)(2,1)S(1)}, bf16[256,1792]{1,0:T(8,128)(2,1)S(1)}, u32[]{:S(2)}, u32[]{:S(2)}) collective-permute-start(bf16[256,1792]{1,0:T(8,128)(2,1)S(1)} %collective-permute-done.2.y_top.refs_3_), channel_id=1, source_target_pairs={{0,8},{4,12},{8,4},{12,0},{16,24},{20,28},{24,20},{28,16},{1,9},{5... | collective-permute-start | bytes 2752520 | tf_op jit(solution)/shard_map/ppermute | solution.py:76
  187.8 40.7 %collective-permute-start.45 = (bf16[256,1792]{1,0:T(8,128)(2,1)S(1)}, bf16[256,1792]{1,0:T(8,128)(2,1)S(1)}, u32[]{:S(2)}, u32[]{:S(2)}) collective-permute-start(bf16[256,1792]{1,0:T(8,128)(2,1)S(1)} %get-tuple-element.72.refs_3_), channel_id=1, source_target_pairs={{8,0},{12,4},{4,8},{0,12},{24,16},{28,20},{20,24},{16,28},{9,1},{1... | collective-permute-start | bytes 2752520 | tf_op jit(solution)/shard_map/ppermute | solution.py:76
  187.9 40.6 %collective-permute-start.48 = (bf16[256,1792]{1,0:T(8,128)(2,1)S(1)}, bf16[256,1792]{1,0:T(8,128)(2,1)S(1)}, u32[]{:S(2)}, u32[]{:S(2)}) collective-permute-start(bf16[256,1792]{1,0:T(8,128)(2,1)S(1)} %get-tuple-element.73.refs_2_), channel_id=1, source_target_pairs={{16,0},{20,4},{28,8},{24,12},{4,16},{0,20},{8,24},{12,28},{17,1},{... | collective-permute-start | bytes 2752520 | tf_op jit(solution)/shard_map/ppermute | solution.py:76
  188.1 42.1 %collective-permute-start.58 = (bf16[256,1792]{1,0:T(8,128)(2,1)S(1)}, bf16[256,1792]{1,0:T(8,128)(2,1)S(1)}, u32[]{:S(2)}, u32[]{:S(2)}) collective-permute-start(bf16[256,1792]{1,0:T(8,128)(2,1)S(1)} %get-tuple-element.72.refs_3_), channel_id=1, source_target_pairs={{0,4},{4,0},{8,12},{12,8},{16,20},{20,16},{24,28},{28,24},{1,5},{5... | collective-permute-start | bytes 2752520 | tf_op jit(solution)/shard_map/ppermute | solution.py:76
  188.5 41.7 %collective-permute-start.52 = (bf16[256,1792]{1,0:T(8,128)(2,1)S(1)}, bf16[256,1792]{1,0:T(8,128)(2,1)S(1)}, u32[]{:S(2)}, u32[]{:S(2)}) collective-permute-start(bf16[256,1792]{1,0:T(8,128)(2,1)S(1)} %get-tuple-element.72.refs_3_), channel_id=1, source_target_pairs={{16,0},{20,4},{28,8},{24,12},{4,16},{0,20},{8,24},{12,28},{17,1},{... | collective-permute-start | bytes 2752520 | tf_op jit(solution)/shard_map/ppermute | solution.py:76
  267.2 40.6 %collective-permute-start.60 = (bf16[256,1792]{1,0:T(8,128)(2,1)S(1)}, bf16[256,1792]{1,0:T(8,128)(2,1)S(1)}, u32[]{:S(2)}, u32[]{:S(2)}) collective-permute-start(bf16[256,1792]{1,0:T(8,128)(2,1)S(1)} %get-tuple-element.75.bottom.refs_3_.refs_14_.refs_6_), channel_id=1, source_target_pairs={{8,0},{12,4},{4,8},{0,12},{24,16},{28,20},{20,24},{16,28},{9,1},{1... | collective-permute-start | bytes 2752520 | tf_op jit(solution)/shard_map/ppermute | solution.py:76
  267.2 40.5 %collective-permute-start.61 = (bf16[256,1792]{1,0:T(8,128)(2,1)S(1)}, bf16[256,1792]{1,0:T(8,128)(2,1)S(1)}, u32[]{:S(2)}, u32[]{:S(2)}) collective-permute-start(bf16[256,1792]{1,0:T(8,128)(2,1)S(1)} %get-tuple-element.74.top.refs_2_.refs_13_.refs_5_), channel_id=1, source_target_pairs={{16,0},{20,4},{28,8},{24,12},{4,16},{0,20},{8,24},{12,28},{17,1},{... | collective-permute-start | bytes 2752520 | tf_op jit(solution)/shard_map/ppermute | solution.py:76
  268.6 41.1 %collective-permute-start.62 = (bf16[256,1792]{1,0:T(8,128)(2,1)S(1)}, bf16[256,1792]{1,0:T(8,128)(2,1)S(1)}, u32[]{:S(2)}, u32[]{:S(2)}) collective-permute-start(bf16[256,1792]{1,0:T(8,128)(2,1)S(1)} %get-tuple-element.75.bottom.refs_3_.refs_14_.refs_6_), channel_id=1, source_target_pairs={{16,0},{20,4},{28,8},{24,12},{4,16},{0,20},{8,24},{12,28},{17,1},{... | collective-permute-start | bytes 2752520 | tf_op jit(solution)/shard_map/ppermute | solution.py:76
  270.8 46.0 %collective-permute-start.71 = (bf16[5,64,256]{2,1,0:T(8,128)(2,1)S(1)}, bf16[5,64,256]{2,1,0:T(8,128)(2,1)S(1)}, u32[]{:S(2)}, u32[]{:S(2)}) collective-permute-start(bf16[5,64,256]{2,1,0:T(8,128)(2,1)S(1)} %get-tuple-element.83), channel_id=1, source_target_pairs={{0,1},{1,0},{2,3},{3,2},{4,5},{5,4},{6,7},{7,6},{8,9},{9,8},{10,11... | collective-permute-start | bytes 491528 | tf_op jit(solution)/shard_map/ppermute | solution.py:316
  332.5 31.7 %collective-permute-start.74 = (bf16[5,64,256]{2,1,0:T(8,128)(2,1)S(1)}, bf16[5,64,256]{2,1,0:T(8,128)(2,1)S(1)}, u32[]{:S(2)}, u32[]{:S(2)}) collective-permute-start(bf16[5,64,256]{2,1,0:T(8,128)(2,1)S(1)} %shard_map.70.refs_0_), channel_id=1, source_target_pairs={{0,2},{1,3},{2,0},{3,1},{4,6},{5,7},{6,4},{7,5},{8,10},{9,11},{10,... | collective-permute-start | bytes 491528 | tf_op jit(solution)/shard_map/ppermute | solution.py:316
  339.3 29.1 %collective-permute-start.80 = (bf16[5,64,256]{2,1,0:T(8,128)(2,1)S(1)}, bf16[5,64,256]{2,1,0:T(8,128)(2,1)S(1)}, u32[]{:S(2)}, u32[]{:S(2)}) collective-permute-start(bf16[5,64,256]{2,1,0:T(8,128)(2,1)S(1)} %shard_map.73.refs_4_.refs_0_), channel_id=1, source_target_pairs={{0,2},{1,3},{2,0},{3,1},{4,6},{5,7},{6,4},{7,5},{8,10},{9,11},{10,... | collective-permute-start | bytes 491528 | tf_op jit(solution)/shard_map/ppermute | solution.py:316
  368.4 34.3 %collective-permute-start.100 = (bf16[256,1792]{1,0:T(8,128)(2,1)S(1)}, bf16[256,1792]{1,0:T(8,128)(2,1)S(1)}, u32[]{:S(2)}, u32[]{:S(2)}) collective-permute-start(bf16[256,1792]{1,0:T(8,128)(2,1)S(1)} %collective-permute-done.60.x_bottom.refs_2_), channel_id=1, source_target_pairs={{0,16},{4,20},{8,28},{12,24},{16,4},{20,0},{24,8},{28,12},{1,17},{... | collective-permute-start | bytes 2752520 | tf_op jit(solution)/shard_map/ppermute | solution.py:76
  369.7 35.1 %collective-permute-start.99 = (bf16[256,1792]{1,0:T(8,128)(2,1)S(1)}, bf16[256,1792]{1,0:T(8,128)(2,1)S(1)}, u32[]{:S(2)}, u32[]{:S(2)}) collective-permute-start(bf16[256,1792]{1,0:T(8,128)(2,1)S(1)} %collective-permute-done.61.y_top.refs_3_), channel_id=1, source_target_pairs={{0,8},{4,12},{8,4},{12,0},{16,24},{20,28},{24,20},{28,16},{1,9},{5... | collective-permute-start | bytes 2752520 | tf_op jit(solution)/shard_map/ppermute | solution.py:76
  375.4 29.5 %collective-permute-start.95 = (bf16[256,1792]{1,0:T(8,128)(2,1)S(1)}, bf16[256,1792]{1,0:T(8,128)(2,1)S(1)}, u32[]{:S(2)}, u32[]{:S(2)}) collective-permute-start(bf16[256,1792]{1,0:T(8,128)(2,1)S(1)} %collective-permute-done.59.x_top.refs_4_), channel_id=1, source_target_pairs={{0,4},{4,0},{8,12},{12,8},{16,20},{20,16},{24,28},{28,24},{1,5},{5... | collective-permute-start | bytes 2752520 | tf_op jit(solution)/shard_map/ppermute | solution.py:76
  443.7 40.7 %collective-permute-start.104 = (bf16[256,1792]{1,0:T(8,128)(2,1)S(1)}, bf16[256,1792]{1,0:T(8,128)(2,1)S(1)}, u32[]{:S(2)}, u32[]{:S(2)}) collective-permute-start(bf16[256,1792]{1,0:T(8,128)(2,1)S(1)} %get-tuple-element.96.refs_3_), channel_id=1, source_target_pairs={{8,0},{12,4},{4,8},{0,12},{24,16},{28,20},{20,24},{16,28},{9,1},{1... | collective-permute-start | bytes 2752520 | tf_op jit(solution)/shard_map/ppermute | solution.py:76
  443.9 41.4 %collective-permute-start.107 = (bf16[256,1792]{1,0:T(8,128)(2,1)S(1)}, bf16[256,1792]{1,0:T(8,128)(2,1)S(1)}, u32[]{:S(2)}, u32[]{:S(2)}) collective-permute-start(bf16[256,1792]{1,0:T(8,128)(2,1)S(1)} %get-tuple-element.97.refs_2_), channel_id=1, source_target_pairs={{16,0},{20,4},{28,8},{24,12},{4,16},{0,20},{8,24},{12,28},{17,1},{... | collective-permute-start | bytes 2752520 | tf_op jit(solution)/shard_map/ppermute | solution.py:76
  444.8 42.2 %collective-permute-start.117 = (bf16[256,1792]{1,0:T(8,128)(2,1)S(1)}, bf16[256,1792]{1,0:T(8,128)(2,1)S(1)}, u32[]{:S(2)}, u32[]{:S(2)}) collective-permute-start(bf16[256,1792]{1,0:T(8,128)(2,1)S(1)} %get-tuple-element.96.refs_3_), channel_id=1, source_target_pairs={{0,4},{4,0},{8,12},{12,8},{16,20},{20,16},{24,28},{28,24},{1,5},{5... | collective-permute-start | bytes 2752520 | tf_op jit(solution)/shard_map/ppermute | solution.py:76
  444.9 42.2 %collective-permute-start.111 = (bf16[256,1792]{1,0:T(8,128)(2,1)S(1)}, bf16[256,1792]{1,0:T(8,128)(2,1)S(1)}, u32[]{:S(2)}, u32[]{:S(2)}) collective-permute-start(bf16[256,1792]{1,0:T(8,128)(2,1)S(1)} %get-tuple-element.96.refs_3_), channel_id=1, source_target_pairs={{16,0},{20,4},{28,8},{24,12},{4,16},{0,20},{8,24},{12,28},{17,1},{... | collective-permute-start | bytes 2752520 | tf_op jit(solution)/shard_map/ppermute | solution.py:76
  487.0 28.2 %collective-permute-start.114 = (bf16[256,1792]{1,0:T(8,128)(2,1)S(1)}, bf16[256,1792]{1,0:T(8,128)(2,1)S(1)}, u32[]{:S(2)}, u32[]{:S(2)}) collective-permute-start(bf16[256,1792]{1,0:T(8,128)(2,1)S(1)} %collective-permute-done.107.refs_2_), channel_id=1, source_target_pairs={{0,4},{4,0},{8,12},{12,8},{16,20},{20,16},{24,28},{28,24},{1,5},{5... | collective-permute-start | bytes 2752520 | tf_op jit(solution)/shard_map/ppermute | solution.py:76
  (99 other events, 1596.1 us)

commit v7 on v6

--- a/solution.py
+++ b/solution.py
@@ -390,9 +390,10 @@
     late_part = reduce_parts(late_pieces)
     early_parts = spread(early_part)
     late_parts = spread(late_part)
+    zeros = jnp.zeros((8, 128), f32)
+    last_squares = exchanged(squares_of([late_part], [(2.0,) * 7], zeros), 3)
     weights = [(1.0, 1.0, 2.0, 2.0, 2.0)] * 4 + [(2.0,) * 5] * 4 + [(2.0,) * 7] * 3
-    squares = squares_of([*own_parts, *early_parts, *late_parts[:3]], weights, jnp.zeros((8, 128), f32))
-    squares = squares_of(late_parts[3:], [(2.0,) * 7], squares)
+    squares = squares_of([*own_parts, *early_parts, *late_parts[:3]], weights, last_squares)
     squares = total_of(squares)
     near_one, x_whole, y_whole = near_assemble(z, early_parts, True)
     early = over_dp(x_whole, GIVE_X), over_dp(y_whole, GIVE_Y)

time: 525 us -> 502 us (0.956)
  starting transfers between devices: 109 us -> 85.7 us
    ppermute x36 -> x38, starting transfers between devices: 58.5 us -> 42.3 us  [exchanged(): lax.ppermute(value, 'shard', [(z, z ^ distance) for z in range(COLUMN_DEV...]
    ppermute x82, waiting for transfers between devices: 247 us -> 238 us  [over_dp(): return lax.ppermute(value, 'dp', pairs)]
    ppermute x36 -> x38, waiting for transfers between devices: 87.9 us -> 96.4 us  [exchanged(): lax.ppermute(value, 'shard', [(z, z ^ distance) for z in range(COLUMN_DEV...]
    ppermute x82, starting transfers between devices: 50.1 us -> 43.5 us  [over_dp(): return lax.ppermute(value, 'dp', pairs)]
  transfers between devices with their start and end apart: 118 -> 120, of which waited for: 48 -> 48; matrix products, arithmetic and copies ran while one was open for 0% -> 1% of each run, Pallas kernels for 11% -> 11%
where the time goes in v7:
time: 502 us; the launch traced here: 501 us
  waiting for transfers between devices  335 us (67%)
  starting transfers between devices  85.7 us (17%)
  Pallas kernels  71.6 us (14%)
  other arithmetic  5.64 us (1%)
    ppermute x82, waiting for transfers between devices, over_dp(): return lax.ppermute(value, 'dp', pairs)  238 us
    ppermute x38, waiting for transfers between devices, exchanged(): lax.ppermute(value, 'shard', [(z, z ^ distance) for z in range(COLUMN_DEV...  96.4 us
    pallas_call x48, Pallas kernels, call(): pl.pallas_call(kernel, out_shape=outs, in_specs=[pl.BlockSpec(memory_spac...  71.6 us
    ppermute x82, starting transfers between devices, over_dp(): return lax.ppermute(value, 'dp', pairs)  43.5 us
    ppermute x38, starting transfers between devices, exchanged(): lax.ppermute(value, 'shard', [(z, z ^ distance) for z in range(COLUMN_DEV...  42.3 us
  transfers between devices with their start and end apart: 120, of which 48 were waited for; matrix products, arithmetic and copies ran while one was open for 1% of the time, Pallas kernels for 11%

profile of v7, /device:TPU:0, one launch (start us, length us, event | category | flops | bytes accessed | tf_op | source)
XLA Modules:
  0.0 501.5 jit_solution(3163832152464825260)
XLA Ops:
  15.8 12.9 %collective-permute-done.8.x_bottom.refs_2_ = bf16[256,1792]{1,0:T(8,128)(2,1)} collective-permute-done((bf16[256,1792]{1,0:T(8,128)(2,1)S(1)}, bf16[256,1792]{1,0:T(8,128)(2,1)}, u32[]{:S(2)}, u32[]{:S(2)}) %collective-permute-start.8) | collective-permute-done | bytes 917536 | tf_op jit(solution)/shard_map/ppermute | solution.py:76
  37.3 10.4 %collective-permute-done.16.x_top.refs_4_ = bf16[256,1792]{1,0:T(8,128)(2,1)} collective-permute-done((bf16[256,1792]{1,0:T(8,128)(2,1)S(1)}, bf16[256,1792]{1,0:T(8,128)(2,1)}, u32[]{:S(2)}, u32[]{:S(2)}) %collective-permute-start.16) | collective-permute-done | bytes 917536 | tf_op jit(solution)/shard_map/ppermute | solution.py:76
  60.1 9.7 %collective-permute-done.19.refs_0_ = bf16[7,64,256]{2,1,0:T(8,128)(2,1)S(1)} collective-permute-done((bf16[7,64,256]{2,1,0:T(8,128)(2,1)S(1)}, bf16[7,64,256]{2,1,0:T(8,128)(2,1)S(1)}, u32[]{:S(2)}, u32[]{:S(2)}) %collective-permute-start.19) | collective-permute-done | bytes 229408 | tf_op jit(solution)/shard_map/ppermute | solution.py:316
  70.6 7.5 %collective-permute-done.10.refs_0_ = bf16[5,64,256]{2,1,0:T(8,128)(2,1)S(1)} collective-permute-done((bf16[5,64,256]{2,1,0:T(8,128)(2,1)S(1)}, bf16[5,64,256]{2,1,0:T(8,128)(2,1)S(1)}, u32[]{:S(2)}, u32[]{:S(2)}) %collective-permute-start.10) | collective-permute-done | bytes 163872 | tf_op jit(solution)/shard_map/ppermute | solution.py:316
  82.4 7.8 %collective-permute-done.20.refs_1_ = bf16[7,64,256]{2,1,0:T(8,128)(2,1)S(1)} collective-permute-done((bf16[7,64,256]{2,1,0:T(8,128)(2,1)S(1)}, bf16[7,64,256]{2,1,0:T(8,128)(2,1)S(1)}, u32[]{:S(2)}, u32[]{:S(2)}) %collective-permute-start.20) | collective-permute-done | bytes 229408 | tf_op jit(solution)/shard_map/ppermute | solution.py:316
  101.0 14.2 %collective-permute-done.15.refs_7_.refs_3_ = bf16[5,64,256]{2,1,0:T(8,128)(2,1)S(1)} collective-permute-done((bf16[5,64,256]{2,1,0:T(8,128)(2,1)S(1)}, bf16[5,64,256]{2,1,0:T(8,128)(2,1)S(1)}, u32[]{:S(2)}, u32[]{:S(2)}) %collective-permute-start.15) | collective-permute-done | bytes 163872 | tf_op jit(solution)/shard_map/ppermute | solution.py:316
  118.7 5.4 %collective-permute-done.30.refs_2_ = bf16[5,64,256]{2,1,0:T(8,128)(2,1)S(1)} collective-permute-done((bf16[5,64,256]{2,1,0:T(8,128)(2,1)S(1)}, bf16[5,64,256]{2,1,0:T(8,128)(2,1)S(1)}, u32[]{:S(2)}, u32[]{:S(2)}) %collective-permute-start.30) | collective-permute-done | bytes 163872 | tf_op jit(solution)/shard_map/ppermute | solution.py:76
  133.5 5.9 %collective-permute-done.34.refs_3_ = bf16[7,64,256]{2,1,0:T(8,128)(2,1)S(1)} collective-permute-done((bf16[7,64,256]{2,1,0:T(8,128)(2,1)S(1)}, bf16[7,64,256]{2,1,0:T(8,128)(2,1)S(1)}, u32[]{:S(2)}, u32[]{:S(2)}) %collective-permute-start.34) | collective-permute-done | bytes 229408 | tf_op jit(solution)/shard_map/ppermute | solution.py:316
  144.1 13.7 %collective-permute-done.32.refs_4_ = bf16[5,128,256]{2,1,0:T(8,128)(2,1)S(1)} collective-permute-done((bf16[5,128,256]{2,1,0:T(8,128)(2,1)S(1)}, bf16[5,128,256]{2,1,0:T(8,128)(2,1)S(1)}, u32[]{:S(2)}, u32[]{:S(2)}) %collective-permute-start.32) | collective-permute-done | bytes 327712 | tf_op jit(solution)/shard_map/ppermute | solution.py:76
  171.2 5.3 %shard_map.59 = (bf16[256,1792]{1,0:T(8,128)(2,1)S(1)}, bf16[256,1792]{1,0:T(8,128)(2,1)S(1)}) custom-call(f32[8,128]{1,0:T(8,128)S(1)} %add_add_fusion.1.refs_0_, bf16[512,1024]{1,0:T(8,128)(2,1)S(1)} %get-tuple-element.67.refs_1_, bf16[512,512]{1,0:T(8,128)(2,1)S(1)} %get-tuple-element.68.refs_2_.refs_0_, ...), custom_call_target="tpu_custom_call" | custom-call | flops 3758096384 | bytes 16781312 | tf_op jit(solution)/shard_map/pallas_call | solution.py:82
  180.6 19.3 %collective-permute-done.52.refs_2_ = bf16[256,1792]{1,0:T(8,128)(2,1)S(1)} collective-permute-done((bf16[256,1792]{1,0:T(8,128)(2,1)S(1)}, bf16[256,1792]{1,0:T(8,128)(2,1)S(1)}, u32[]{:S(2)}, u32[]{:S(2)}) %collective-permute-start.52) | collective-permute-done | bytes 917536 | tf_op jit(solution)/shard_map/ppermute | solution.py:76
  199.8 19.1 %collective-permute-done.46.refs_1_ = bf16[256,1792]{1,0:T(8,128)(2,1)S(1)} collective-permute-done((bf16[256,1792]{1,0:T(8,128)(2,1)S(1)}, bf16[256,1792]{1,0:T(8,128)(2,1)S(1)}, u32[]{:S(2)}, u32[]{:S(2)}) %collective-permute-start.46) | collective-permute-done | bytes 917536 | tf_op jit(solution)/shard_map/ppermute | solution.py:76
  221.2 20.2 %collective-permute-done.47.refs_2_ = bf16[256,1792]{1,0:T(8,128)(2,1)S(1)} collective-permute-done((bf16[256,1792]{1,0:T(8,128)(2,1)S(1)}, bf16[256,1792]{1,0:T(8,128)(2,1)S(1)}, u32[]{:S(2)}, u32[]{:S(2)}) %collective-permute-start.47) | collective-permute-done | bytes 917536 | tf_op jit(solution)/shard_map/ppermute | solution.py:76
  261.5 18.0 %collective-permute-done.68.x_bottom.refs_2_ = bf16[256,1792]{1,0:T(8,128)(2,1)S(1)} collective-permute-done((bf16[256,1792]{1,0:T(8,128)(2,1)S(1)}, bf16[256,1792]{1,0:T(8,128)(2,1)S(1)}, u32[]{:S(2)}, u32[]{:S(2)}) %collective-permute-start.68) | collective-permute-done | bytes 917536 | tf_op jit(solution)/shard_map/ppermute | solution.py:76
  283.4 14.9 %collective-permute-done.76.x_top.refs_4_ = bf16[256,1792]{1,0:T(8,128)(2,1)S(1)} collective-permute-done((bf16[256,1792]{1,0:T(8,128)(2,1)S(1)}, bf16[256,1792]{1,0:T(8,128)(2,1)S(1)}, u32[]{:S(2)}, u32[]{:S(2)}) %collective-permute-start.76) | collective-permute-done | bytes 917536 | tf_op jit(solution)/shard_map/ppermute | solution.py:76
  306.1 10.1 %collective-permute-done.79.refs_0_ = bf16[7,64,256]{2,1,0:T(8,128)(2,1)S(1)} collective-permute-done((bf16[7,64,256]{2,1,0:T(8,128)(2,1)S(1)}, bf16[7,64,256]{2,1,0:T(8,128)(2,1)S(1)}, u32[]{:S(2)}, u32[]{:S(2)}) %collective-permute-start.79) | collective-permute-done | bytes 229408 | tf_op jit(solution)/shard_map/ppermute | solution.py:316
  316.3 7.1 %collective-permute-done.70.refs_0_ = bf16[5,64,256]{2,1,0:T(8,128)(2,1)S(1)} collective-permute-done((bf16[5,64,256]{2,1,0:T(8,128)(2,1)S(1)}, bf16[5,64,256]{2,1,0:T(8,128)(2,1)S(1)}, u32[]{:S(2)}, u32[]{:S(2)}) %collective-permute-start.70) | collective-permute-done | bytes 163872 | tf_op jit(solution)/shard_map/ppermute | solution.py:316
  327.9 8.2 %collective-permute-done.80.refs_1_ = bf16[7,64,256]{2,1,0:T(8,128)(2,1)S(1)} collective-permute-done((bf16[7,64,256]{2,1,0:T(8,128)(2,1)S(1)}, bf16[7,64,256]{2,1,0:T(8,128)(2,1)S(1)}, u32[]{:S(2)}, u32[]{:S(2)}) %collective-permute-start.80) | collective-permute-done | bytes 229408 | tf_op jit(solution)/shard_map/ppermute | solution.py:316
  347.8 13.5 %collective-permute-done.75.refs_7_.refs_3_ = bf16[5,64,256]{2,1,0:T(8,128)(2,1)S(1)} collective-permute-done((bf16[5,64,256]{2,1,0:T(8,128)(2,1)S(1)}, bf16[5,64,256]{2,1,0:T(8,128)(2,1)S(1)}, u32[]{:S(2)}, u32[]{:S(2)}) %collective-permute-start.75) | collective-permute-done | bytes 163872 | tf_op jit(solution)/shard_map/ppermute | solution.py:316
  379.3 5.3 %collective-permute-done.94.refs_3_ = bf16[7,64,256]{2,1,0:T(8,128)(2,1)S(1)} collective-permute-done((bf16[7,64,256]{2,1,0:T(8,128)(2,1)S(1)}, bf16[7,64,256]{2,1,0:T(8,128)(2,1)S(1)}, u32[]{:S(2)}, u32[]{:S(2)}) %collective-permute-start.94) | collective-permute-done | bytes 229408 | tf_op jit(solution)/shard_map/ppermute | solution.py:316
  389.5 13.5 %collective-permute-done.92.refs_4_ = bf16[5,128,256]{2,1,0:T(8,128)(2,1)S(1)} collective-permute-done((bf16[5,128,256]{2,1,0:T(8,128)(2,1)S(1)}, bf16[5,128,256]{2,1,0:T(8,128)(2,1)S(1)}, u32[]{:S(2)}, u32[]{:S(2)}) %collective-permute-start.92) | collective-permute-done | bytes 327712 | tf_op jit(solution)/shard_map/ppermute | solution.py:76
  423.1 19.3 %collective-permute-done.112.refs_2_ = bf16[256,1792]{1,0:T(8,128)(2,1)S(1)} collective-permute-done((bf16[256,1792]{1,0:T(8,128)(2,1)S(1)}, bf16[256,1792]{1,0:T(8,128)(2,1)S(1)}, u32[]{:S(2)}, u32[]{:S(2)}) %collective-permute-start.112) | collective-permute-done | bytes 917536 | tf_op jit(solution)/shard_map/ppermute | solution.py:76
  442.4 19.1 %collective-permute-done.106.refs_1_ = bf16[256,1792]{1,0:T(8,128)(2,1)S(1)} collective-permute-done((bf16[256,1792]{1,0:T(8,128)(2,1)S(1)}, bf16[256,1792]{1,0:T(8,128)(2,1)S(1)}, u32[]{:S(2)}, u32[]{:S(2)}) %collective-permute-start.106) | collective-permute-done | bytes 917536 | tf_op jit(solution)/shard_map/ppermute | solution.py:76
  463.8 20.2 %collective-permute-done.107.refs_2_ = bf16[256,1792]{1,0:T(8,128)(2,1)S(1)} collective-permute-done((bf16[256,1792]{1,0:T(8,128)(2,1)S(1)}, bf16[256,1792]{1,0:T(8,128)(2,1)S(1)}, u32[]{:S(2)}, u32[]{:S(2)}) %collective-permute-start.107) | collective-permute-done | bytes 917536 | tf_op jit(solution)/shard_map/ppermute | solution.py:76
  (293 shorter events, 199.2 us)
Async XLA Ops:
  8.6 39.1 %collective-permute-start.16 = (bf16[256,1792]{1,0:T(8,128)(2,1)S(1)}, bf16[256,1792]{1,0:T(8,128)(2,1)}, u32[]{:S(2)}, u32[]{:S(2)}) collective-permute-start(bf16[256,1792]{1,0:T(8,128)(2,1)S(1)} %get-tuple-element.99.top.refs_2_.refs_13_.refs_5_), channel_id=1, source_target_pairs={{8,0},{12,4},{4,8},{0,12},{24,16},{28,20},{20,24},{16,28},{9,1},{1... | collective-permute-start | bytes 2752520 | tf_op jit(solution)/shard_map/ppermute | solution.py:76
  9.6 40.0 %collective-permute-start.17 = (bf16[256,1792]{1,0:T(8,128)(2,1)S(1)}, bf16[256,1792]{1,0:T(8,128)(2,1)}, u32[]{:S(2)}, u32[]{:S(2)}) collective-permute-start(bf16[256,1792]{1,0:T(8,128)(2,1)S(1)} %get-tuple-element.98.bottom.refs_3_.refs_14_.refs_6_), channel_id=1, source_target_pairs={{16,0},{20,4},{28,8},{24,12},{4,16},{0,20},{8,24},{12,28},{17,1},{... | collective-permute-start | bytes 2752520 | tf_op jit(solution)/shard_map/ppermute | solution.py:76
  28.7 28.2 %collective-permute-start.2 = (bf16[5,64,256]{2,1,0:T(8,128)(2,1)S(1)}, bf16[5,64,256]{2,1,0:T(8,128)(2,1)S(1)}, u32[]{:S(2)}, u32[]{:S(2)}) collective-permute-start(bf16[5,64,256]{2,1,0:T(8,128)(2,1)S(1)} %get-tuple-element.53), channel_id=1, source_target_pairs={{0,1},{1,0},{2,3},{3,2},{4,5},{5,4},{6,7},{7,6},{8,9},{9,8},{10,11... | collective-permute-start | bytes 491528 | tf_op jit(solution)/shard_map/ppermute | solution.py:316
  54.9 25.5 %collective-permute-start.18 = (bf16[7,64,256]{2,1,0:T(8,128)(2,1)S(1)}, bf16[7,64,256]{2,1,0:T(8,128)(2,1)S(1)}, u32[]{:S(2)}, u32[]{:S(2)}) collective-permute-start(bf16[7,64,256]{2,1,0:T(8,128)(2,1)S(1)} %get-tuple-element.61), channel_id=1, source_target_pairs={{0,1},{1,0},{2,3},{3,2},{4,5},{5,4},{6,7},{7,6},{8,9},{9,8},{10,11... | collective-permute-start | bytes 688136 | tf_op jit(solution)/shard_map/ppermute | solution.py:316
  96.9 43.3 %collective-permute-start.42 = (bf16[256,1792]{1,0:T(8,128)(2,1)}, bf16[256,1792]{1,0:T(8,128)(2,1)S(1)}, u32[]{:S(2)}, u32[]{:S(2)}) collective-permute-start(bf16[256,1792]{1,0:T(8,128)(2,1)} %collective-permute-done.8.x_bottom.refs_2_), channel_id=1, source_target_pairs={{0,16},{4,20},{8,28},{12,24},{16,4},{20,0},{24,8},{28,12},{1,17},{... | collective-permute-start | bytes 2752520 | tf_op jit(solution)/shard_map/ppermute | solution.py:76
  98.8 41.9 %collective-permute-start.41 = (bf16[256,1792]{1,0:T(8,128)(2,1)S(1)}, bf16[256,1792]{1,0:T(8,128)(2,1)S(1)}, u32[]{:S(2)}, u32[]{:S(2)}) collective-permute-start(bf16[256,1792]{1,0:T(8,128)(2,1)S(1)} %collective-permute-done.9.y_top.refs_3_), channel_id=1, source_target_pairs={{0,8},{4,12},{8,4},{12,0},{16,24},{20,28},{24,20},{28,16},{1,9},{5... | collective-permute-start | bytes 2752520 | tf_op jit(solution)/shard_map/ppermute | solution.py:76
  176.6 42.3 %collective-permute-start.46 = (bf16[256,1792]{1,0:T(8,128)(2,1)S(1)}, bf16[256,1792]{1,0:T(8,128)(2,1)S(1)}, u32[]{:S(2)}, u32[]{:S(2)}) collective-permute-start(bf16[256,1792]{1,0:T(8,128)(2,1)S(1)} %get-tuple-element.72.refs_3_), channel_id=1, source_target_pairs={{8,0},{12,4},{4,8},{0,12},{24,16},{28,20},{20,24},{16,28},{9,1},{1... | collective-permute-start | bytes 2752520 | tf_op jit(solution)/shard_map/ppermute | solution.py:76
  178.4 41.0 %collective-permute-start.49 = (bf16[256,1792]{1,0:T(8,128)(2,1)S(1)}, bf16[256,1792]{1,0:T(8,128)(2,1)S(1)}, u32[]{:S(2)}, u32[]{:S(2)}) collective-permute-start(bf16[256,1792]{1,0:T(8,128)(2,1)S(1)} %get-tuple-element.73.refs_2_), channel_id=1, source_target_pairs={{16,0},{20,4},{28,8},{24,12},{4,16},{0,20},{8,24},{12,28},{17,1},{... | collective-permute-start | bytes 2752520 | tf_op jit(solution)/shard_map/ppermute | solution.py:76
  178.7 40.6 %collective-permute-start.59 = (bf16[256,1792]{1,0:T(8,128)(2,1)S(1)}, bf16[256,1792]{1,0:T(8,128)(2,1)S(1)}, u32[]{:S(2)}, u32[]{:S(2)}) collective-permute-start(bf16[256,1792]{1,0:T(8,128)(2,1)S(1)} %get-tuple-element.72.refs_3_), channel_id=1, source_target_pairs={{0,4},{4,0},{8,12},{12,8},{16,20},{20,16},{24,28},{28,24},{1,5},{5... | collective-permute-start | bytes 2752520 | tf_op jit(solution)/shard_map/ppermute | solution.py:76
  179.0 41.7 %collective-permute-start.53 = (bf16[256,1792]{1,0:T(8,128)(2,1)S(1)}, bf16[256,1792]{1,0:T(8,128)(2,1)S(1)}, u32[]{:S(2)}, u32[]{:S(2)}) collective-permute-start(bf16[256,1792]{1,0:T(8,128)(2,1)S(1)} %get-tuple-element.72.refs_3_), channel_id=1, source_target_pairs={{16,0},{20,4},{28,8},{24,12},{4,16},{0,20},{8,24},{12,28},{17,1},{... | collective-permute-start | bytes 2752520 | tf_op jit(solution)/shard_map/ppermute | solution.py:76
  219.4 27.7 %collective-permute-start.55 = (bf16[256,1792]{1,0:T(8,128)(2,1)S(1)}, bf16[256,1792]{1,0:T(8,128)(2,1)S(1)}, u32[]{:S(2)}, u32[]{:S(2)}) collective-permute-start(bf16[256,1792]{1,0:T(8,128)(2,1)S(1)} %collective-permute-done.46.refs_1_), channel_id=1, source_target_pairs={{0,4},{4,0},{8,12},{12,8},{16,20},{20,16},{24,28},{28,24},{1,5},{5... | collective-permute-start | bytes 2752520 | tf_op jit(solution)/shard_map/ppermute | solution.py:76
  220.7 26.5 %collective-permute-start.56 = (bf16[256,1792]{1,0:T(8,128)(2,1)S(1)}, bf16[256,1792]{1,0:T(8,128)(2,1)S(1)}, u32[]{:S(2)}, u32[]{:S(2)}) collective-permute-start(bf16[256,1792]{1,0:T(8,128)(2,1)S(1)} %collective-permute-done.49.refs_2_), channel_id=1, source_target_pairs={{0,4},{4,0},{8,12},{12,8},{16,20},{20,16},{24,28},{28,24},{1,5},{5... | collective-permute-start | bytes 2752520 | tf_op jit(solution)/shard_map/ppermute | solution.py:76
  220.7 26.5 %collective-permute-start.57 = (bf16[256,1792]{1,0:T(8,128)(2,1)S(1)}, bf16[256,1792]{1,0:T(8,128)(2,1)S(1)}, u32[]{:S(2)}, u32[]{:S(2)}) collective-permute-start(bf16[256,1792]{1,0:T(8,128)(2,1)S(1)} %collective-permute-done.53.refs_3_), channel_id=1, source_target_pairs={{0,4},{4,0},{8,12},{12,8},{16,20},{20,16},{24,28},{28,24},{1,5},{5... | collective-permute-start | bytes 2752520 | tf_op jit(solution)/shard_map/ppermute | solution.py:76
  257.9 40.5 %collective-permute-start.76 = (bf16[256,1792]{1,0:T(8,128)(2,1)S(1)}, bf16[256,1792]{1,0:T(8,128)(2,1)S(1)}, u32[]{:S(2)}, u32[]{:S(2)}) collective-permute-start(bf16[256,1792]{1,0:T(8,128)(2,1)S(1)} %get-tuple-element.74.top.refs_2_.refs_13_.refs_5_), channel_id=1, source_target_pairs={{8,0},{12,4},{4,8},{0,12},{24,16},{28,20},{20,24},{16,28},{9,1},{1... | collective-permute-start | bytes 2752520 | tf_op jit(solution)/shard_map/ppermute | solution.py:76
  258.3 40.3 %collective-permute-start.77 = (bf16[256,1792]{1,0:T(8,128)(2,1)S(1)}, bf16[256,1792]{1,0:T(8,128)(2,1)S(1)}, u32[]{:S(2)}, u32[]{:S(2)}) collective-permute-start(bf16[256,1792]{1,0:T(8,128)(2,1)S(1)} %get-tuple-element.75.bottom.refs_3_.refs_14_.refs_6_), channel_id=1, source_target_pairs={{16,0},{20,4},{28,8},{24,12},{4,16},{0,20},{8,24},{12,28},{17,1},{... | collective-permute-start | bytes 2752520 | tf_op jit(solution)/shard_map/ppermute | solution.py:76
  341.9 43.6 %collective-permute-start.102 = (bf16[256,1792]{1,0:T(8,128)(2,1)S(1)}, bf16[256,1792]{1,0:T(8,128)(2,1)S(1)}, u32[]{:S(2)}, u32[]{:S(2)}) collective-permute-start(bf16[256,1792]{1,0:T(8,128)(2,1)S(1)} %collective-permute-done.68.x_bottom.refs_2_), channel_id=1, source_target_pairs={{0,16},{4,20},{8,28},{12,24},{16,4},{20,0},{24,8},{28,12},{1,17},{... | collective-permute-start | bytes 2752520 | tf_op jit(solution)/shard_map/ppermute | solution.py:76
  344.3 41.7 %collective-permute-start.101 = (bf16[256,1792]{1,0:T(8,128)(2,1)S(1)}, bf16[256,1792]{1,0:T(8,128)(2,1)S(1)}, u32[]{:S(2)}, u32[]{:S(2)}) collective-permute-start(bf16[256,1792]{1,0:T(8,128)(2,1)S(1)} %collective-permute-done.69.y_top.refs_3_), channel_id=1, source_target_pairs={{0,8},{4,12},{8,4},{12,0},{16,24},{20,28},{24,20},{28,16},{1,9},{5... | collective-permute-start | bytes 2752520 | tf_op jit(solution)/shard_map/ppermute | solution.py:76
  419.2 42.3 %collective-permute-start.106 = (bf16[256,1792]{1,0:T(8,128)(2,1)S(1)}, bf16[256,1792]{1,0:T(8,128)(2,1)S(1)}, u32[]{:S(2)}, u32[]{:S(2)}) collective-permute-start(bf16[256,1792]{1,0:T(8,128)(2,1)S(1)} %get-tuple-element.96.refs_3_), channel_id=1, source_target_pairs={{8,0},{12,4},{4,8},{0,12},{24,16},{28,20},{20,24},{16,28},{9,1},{1... | collective-permute-start | bytes 2752520 | tf_op jit(solution)/shard_map/ppermute | solution.py:76
  421.0 41.0 %collective-permute-start.109 = (bf16[256,1792]{1,0:T(8,128)(2,1)S(1)}, bf16[256,1792]{1,0:T(8,128)(2,1)S(1)}, u32[]{:S(2)}, u32[]{:S(2)}) collective-permute-start(bf16[256,1792]{1,0:T(8,128)(2,1)S(1)} %get-tuple-element.97.refs_2_), channel_id=1, source_target_pairs={{16,0},{20,4},{28,8},{24,12},{4,16},{0,20},{8,24},{12,28},{17,1},{... | collective-permute-start | bytes 2752520 | tf_op jit(solution)/shard_map/ppermute | solution.py:76
  421.4 40.6 %collective-permute-start.119 = (bf16[256,1792]{1,0:T(8,128)(2,1)S(1)}, bf16[256,1792]{1,0:T(8,128)(2,1)S(1)}, u32[]{:S(2)}, u32[]{:S(2)}) collective-permute-start(bf16[256,1792]{1,0:T(8,128)(2,1)S(1)} %get-tuple-element.96.refs_3_), channel_id=1, source_target_pairs={{0,4},{4,0},{8,12},{12,8},{16,20},{20,16},{24,28},{28,24},{1,5},{5... | collective-permute-start | bytes 2752520 | tf_op jit(solution)/shard_map/ppermute | solution.py:76
  421.6 41.7 %collective-permute-start.113 = (bf16[256,1792]{1,0:T(8,128)(2,1)S(1)}, bf16[256,1792]{1,0:T(8,128)(2,1)S(1)}, u32[]{:S(2)}, u32[]{:S(2)}) collective-permute-start(bf16[256,1792]{1,0:T(8,128)(2,1)S(1)} %get-tuple-element.96.refs_3_), channel_id=1, source_target_pairs={{16,0},{20,4},{28,8},{24,12},{4,16},{0,20},{8,24},{12,28},{17,1},{... | collective-permute-start | bytes 2752520 | tf_op jit(solution)/shard_map/ppermute | solution.py:76
  462.0 30.0 %collective-permute-start.115 = (bf16[256,1792]{1,0:T(8,128)(2,1)S(1)}, bf16[256,1792]{1,0:T(8,128)(2,1)S(1)}, u32[]{:S(2)}, u32[]{:S(2)}) collective-permute-start(bf16[256,1792]{1,0:T(8,128)(2,1)S(1)} %collective-permute-done.106.refs_1_), channel_id=1, source_target_pairs={{0,4},{4,0},{8,12},{12,8},{16,20},{20,16},{24,28},{28,24},{1,5},{5... | collective-permute-start | bytes 2752520 | tf_op jit(solution)/shard_map/ppermute | solution.py:76
  463.3 28.8 %collective-permute-start.116 = (bf16[256,1792]{1,0:T(8,128)(2,1)S(1)}, bf16[256,1792]{1,0:T(8,128)(2,1)S(1)}, u32[]{:S(2)}, u32[]{:S(2)}) collective-permute-start(bf16[256,1792]{1,0:T(8,128)(2,1)S(1)} %collective-permute-done.109.refs_2_), channel_id=1, source_target_pairs={{0,4},{4,0},{8,12},{12,8},{16,20},{20,16},{24,28},{28,24},{1,5},{5... | collective-permute-start | bytes 2752520 | tf_op jit(solution)/shard_map/ppermute | solution.py:76
  463.3 28.8 %collective-permute-start.117 = (bf16[256,1792]{1,0:T(8,128)(2,1)S(1)}, bf16[256,1792]{1,0:T(8,128)(2,1)S(1)}, u32[]{:S(2)}, u32[]{:S(2)}) collective-permute-start(bf16[256,1792]{1,0:T(8,128)(2,1)S(1)} %collective-permute-done.113.refs_3_), channel_id=1, source_target_pairs={{0,4},{4,0},{8,12},{12,8},{16,20},{20,16},{24,28},{28,24},{1,5},{5... | collective-permute-start | bytes 2752520 | tf_op jit(solution)/shard_map/ppermute | solution.py:76
  (101 other events, 1626.2 us)

commit v8 on v7

--- a/solution.py
+++ b/solution.py
@@ -292,9 +292,9 @@
         lax.fori_loop(0, columns // tile, wait, 0)
 
 
-def product(grams, halves, summed=None, finish=None, dtype=f32, parts=1):
+def product(grams, halves, summed=None, finish=None, dtype=f32, parts=1, wide=False):
     half, columns = halves[0].shape
-    tile = 256 if columns % 256 == 0 else columns
+    tile = columns if wide or columns % 256 else 256
     args = ([finish[1]] if finish else []) + list(grams) + list(halves)
     args += [] if summed is None else [summed]
     args += list(finish[2]) if finish else []
@@ -424,13 +424,14 @@
         (mixing, squares, matrix),
         bf16,
         2,
+        True,
     )
     core, one, two, side, linked, crossed = gather(mixture)
     (second,) = product([own, beside], [*mixture, *core])
     (second,) = product([near_one], one, second)
     (second,) = product([near_two, side_gram], [*two, *side], second)
-    (second,) = product([linked_gram], linked, second)
-    return product([crossed_gram], crossed, second, (ending, squares, matrix), dtype, parts)
+    (second,) = product([linked_gram], linked, second, wide=True)
+    return product([crossed_gram], crossed, second, (ending, squares, matrix), dtype, parts, parts == 2)
 
 
 def current_of(momentum, gradient):

time: 502 us -> 497 us (0.990)
  no operation moved by 1% of the time
where the time goes in v8:
time: 497 us
  waiting for transfers between devices  334 us (67%)
  starting transfers between devices  85.7 us (17%)
  Pallas kernels  66.9 us (13%)
  other arithmetic  5.64 us (1%)
    ppermute x82, waiting for transfers between devices, over_dp(): return lax.ppermute(value, 'dp', pairs)  238 us
    ppermute x38, waiting for transfers between devices, exchanged(): lax.ppermute(value, 'shard', [(z, z ^ distance) for z in range(COLUMN_DEV...  96.4 us
    pallas_call x48, Pallas kernels, call(): pl.pallas_call(kernel, out_shape=outs, in_specs=[pl.BlockSpec(memory_spac...  66.9 us
    ppermute x82, starting transfers between devices, over_dp(): return lax.ppermute(value, 'dp', pairs)  43.5 us
    ppermute x38, starting transfers between devices, exchanged(): lax.ppermute(value, 'shard', [(z, z ^ distance) for z in range(COLUMN_DEV...  42.3 us
  transfers between devices with their start and end apart: 120, of which 48 were waited for; matrix products, arithmetic and copies ran while one was open for 1% of the time, Pallas kernels for 11%

profile of v8, /device:TPU:0, one launch (start us, length us, event | category | flops | bytes accessed | tf_op | source)
XLA Modules:
  0.0 496.5 jit_solution(3980712173575296189)
XLA Ops:
  15.8 12.9 %collective-permute-done.8.x_bottom.refs_2_ = bf16[256,1792]{1,0:T(8,128)(2,1)} collective-permute-done((bf16[256,1792]{1,0:T(8,128)(2,1)S(1)}, bf16[256,1792]{1,0:T(8,128)(2,1)}, u32[]{:S(2)}, u32[]{:S(2)}) %collective-permute-start.8) | collective-permute-done | bytes 917536 | tf_op jit(solution)/shard_map/ppermute | solution.py:76
  37.3 10.4 %collective-permute-done.16.x_top.refs_4_ = bf16[256,1792]{1,0:T(8,128)(2,1)} collective-permute-done((bf16[256,1792]{1,0:T(8,128)(2,1)S(1)}, bf16[256,1792]{1,0:T(8,128)(2,1)}, u32[]{:S(2)}, u32[]{:S(2)}) %collective-permute-start.16) | collective-permute-done | bytes 917536 | tf_op jit(solution)/shard_map/ppermute | solution.py:76
  60.1 9.7 %collective-permute-done.19.refs_0_ = bf16[7,64,256]{2,1,0:T(8,128)(2,1)S(1)} collective-permute-done((bf16[7,64,256]{2,1,0:T(8,128)(2,1)S(1)}, bf16[7,64,256]{2,1,0:T(8,128)(2,1)S(1)}, u32[]{:S(2)}, u32[]{:S(2)}) %collective-permute-start.19) | collective-permute-done | bytes 229408 | tf_op jit(solution)/shard_map/ppermute | solution.py:316
  70.6 7.5 %collective-permute-done.10.refs_0_ = bf16[5,64,256]{2,1,0:T(8,128)(2,1)S(1)} collective-permute-done((bf16[5,64,256]{2,1,0:T(8,128)(2,1)S(1)}, bf16[5,64,256]{2,1,0:T(8,128)(2,1)S(1)}, u32[]{:S(2)}, u32[]{:S(2)}) %collective-permute-start.10) | collective-permute-done | bytes 163872 | tf_op jit(solution)/shard_map/ppermute | solution.py:316
  82.4 7.8 %collective-permute-done.20.refs_1_ = bf16[7,64,256]{2,1,0:T(8,128)(2,1)S(1)} collective-permute-done((bf16[7,64,256]{2,1,0:T(8,128)(2,1)S(1)}, bf16[7,64,256]{2,1,0:T(8,128)(2,1)S(1)}, u32[]{:S(2)}, u32[]{:S(2)}) %collective-permute-start.20) | collective-permute-done | bytes 229408 | tf_op jit(solution)/shard_map/ppermute | solution.py:316
  101.0 14.2 %collective-permute-done.15.refs_7_.refs_3_ = bf16[5,64,256]{2,1,0:T(8,128)(2,1)S(1)} collective-permute-done((bf16[5,64,256]{2,1,0:T(8,128)(2,1)S(1)}, bf16[5,64,256]{2,1,0:T(8,128)(2,1)S(1)}, u32[]{:S(2)}, u32[]{:S(2)}) %collective-permute-start.15) | collective-permute-done | bytes 163872 | tf_op jit(solution)/shard_map/ppermute | solution.py:316
  118.7 5.4 %collective-permute-done.30.refs_2_ = bf16[5,64,256]{2,1,0:T(8,128)(2,1)S(1)} collective-permute-done((bf16[5,64,256]{2,1,0:T(8,128)(2,1)S(1)}, bf16[5,64,256]{2,1,0:T(8,128)(2,1)S(1)}, u32[]{:S(2)}, u32[]{:S(2)}) %collective-permute-start.30) | collective-permute-done | bytes 163872 | tf_op jit(solution)/shard_map/ppermute | solution.py:76
  133.5 5.9 %collective-permute-done.34.refs_3_ = bf16[7,64,256]{2,1,0:T(8,128)(2,1)S(1)} collective-permute-done((bf16[7,64,256]{2,1,0:T(8,128)(2,1)S(1)}, bf16[7,64,256]{2,1,0:T(8,128)(2,1)S(1)}, u32[]{:S(2)}, u32[]{:S(2)}) %collective-permute-start.34) | collective-permute-done | bytes 229408 | tf_op jit(solution)/shard_map/ppermute | solution.py:316
  144.1 13.7 %collective-permute-done.32.refs_4_ = bf16[5,128,256]{2,1,0:T(8,128)(2,1)S(1)} collective-permute-done((bf16[5,128,256]{2,1,0:T(8,128)(2,1)S(1)}, bf16[5,128,256]{2,1,0:T(8,128)(2,1)S(1)}, u32[]{:S(2)}, u32[]{:S(2)}) %collective-permute-start.32) | collective-permute-done | bytes 327712 | tf_op jit(solution)/shard_map/ppermute | solution.py:76
  165.9 4.8 shard_map.58.refs_12_
  179.7 19.3 %collective-permute-done.52.refs_2_ = bf16[256,1792]{1,0:T(8,128)(2,1)S(1)} collective-permute-done((bf16[256,1792]{1,0:T(8,128)(2,1)S(1)}, bf16[256,1792]{1,0:T(8,128)(2,1)S(1)}, u32[]{:S(2)}, u32[]{:S(2)}) %collective-permute-start.52) | collective-permute-done | bytes 917536 | tf_op jit(solution)/shard_map/ppermute | solution.py:76
  199.0 19.1 %collective-permute-done.46.refs_1_ = bf16[256,1792]{1,0:T(8,128)(2,1)S(1)} collective-permute-done((bf16[256,1792]{1,0:T(8,128)(2,1)S(1)}, bf16[256,1792]{1,0:T(8,128)(2,1)S(1)}, u32[]{:S(2)}, u32[]{:S(2)}) %collective-permute-start.46) | collective-permute-done | bytes 917536 | tf_op jit(solution)/shard_map/ppermute | solution.py:76
  220.3 20.2 %collective-permute-done.47.refs_2_ = bf16[256,1792]{1,0:T(8,128)(2,1)S(1)} collective-permute-done((bf16[256,1792]{1,0:T(8,128)(2,1)S(1)}, bf16[256,1792]{1,0:T(8,128)(2,1)S(1)}, u32[]{:S(2)}, u32[]{:S(2)}) %collective-permute-start.47) | collective-permute-done | bytes 917536 | tf_op jit(solution)/shard_map/ppermute | solution.py:76
  259.0 17.8 %collective-permute-done.68.x_bottom.refs_2_ = bf16[256,1792]{1,0:T(8,128)(2,1)S(1)} collective-permute-done((bf16[256,1792]{1,0:T(8,128)(2,1)S(1)}, bf16[256,1792]{1,0:T(8,128)(2,1)S(1)}, u32[]{:S(2)}, u32[]{:S(2)}) %collective-permute-start.68) | collective-permute-done | bytes 917536 | tf_op jit(solution)/shard_map/ppermute | solution.py:76
  280.7 14.9 %collective-permute-done.76.x_top.refs_4_ = bf16[256,1792]{1,0:T(8,128)(2,1)S(1)} collective-permute-done((bf16[256,1792]{1,0:T(8,128)(2,1)S(1)}, bf16[256,1792]{1,0:T(8,128)(2,1)S(1)}, u32[]{:S(2)}, u32[]{:S(2)}) %collective-permute-start.76) | collective-permute-done | bytes 917536 | tf_op jit(solution)/shard_map/ppermute | solution.py:76
  303.3 10.1 %collective-permute-done.79.refs_0_ = bf16[7,64,256]{2,1,0:T(8,128)(2,1)S(1)} collective-permute-done((bf16[7,64,256]{2,1,0:T(8,128)(2,1)S(1)}, bf16[7,64,256]{2,1,0:T(8,128)(2,1)S(1)}, u32[]{:S(2)}, u32[]{:S(2)}) %collective-permute-start.79) | collective-permute-done | bytes 229408 | tf_op jit(solution)/shard_map/ppermute | solution.py:316
  313.5 7.1 %collective-permute-done.70.refs_0_ = bf16[5,64,256]{2,1,0:T(8,128)(2,1)S(1)} collective-permute-done((bf16[5,64,256]{2,1,0:T(8,128)(2,1)S(1)}, bf16[5,64,256]{2,1,0:T(8,128)(2,1)S(1)}, u32[]{:S(2)}, u32[]{:S(2)}) %collective-permute-start.70) | collective-permute-done | bytes 163872 | tf_op jit(solution)/shard_map/ppermute | solution.py:316
  325.2 8.2 %collective-permute-done.80.refs_1_ = bf16[7,64,256]{2,1,0:T(8,128)(2,1)S(1)} collective-permute-done((bf16[7,64,256]{2,1,0:T(8,128)(2,1)S(1)}, bf16[7,64,256]{2,1,0:T(8,128)(2,1)S(1)}, u32[]{:S(2)}, u32[]{:S(2)}) %collective-permute-start.80) | collective-permute-done | bytes 229408 | tf_op jit(solution)/shard_map/ppermute | solution.py:316
  345.1 13.4 %collective-permute-done.75.refs_7_.refs_3_ = bf16[5,64,256]{2,1,0:T(8,128)(2,1)S(1)} collective-permute-done((bf16[5,64,256]{2,1,0:T(8,128)(2,1)S(1)}, bf16[5,64,256]{2,1,0:T(8,128)(2,1)S(1)}, u32[]{:S(2)}, u32[]{:S(2)}) %collective-permute-start.75) | collective-permute-done | bytes 163872 | tf_op jit(solution)/shard_map/ppermute | solution.py:316
  376.5 5.3 %collective-permute-done.94.refs_3_ = bf16[7,64,256]{2,1,0:T(8,128)(2,1)S(1)} collective-permute-done((bf16[7,64,256]{2,1,0:T(8,128)(2,1)S(1)}, bf16[7,64,256]{2,1,0:T(8,128)(2,1)S(1)}, u32[]{:S(2)}, u32[]{:S(2)}) %collective-permute-start.94) | collective-permute-done | bytes 229408 | tf_op jit(solution)/shard_map/ppermute | solution.py:316
  386.7 13.5 %collective-permute-done.92.refs_4_ = bf16[5,128,256]{2,1,0:T(8,128)(2,1)S(1)} collective-permute-done((bf16[5,128,256]{2,1,0:T(8,128)(2,1)S(1)}, bf16[5,128,256]{2,1,0:T(8,128)(2,1)S(1)}, u32[]{:S(2)}, u32[]{:S(2)}) %collective-permute-start.92) | collective-permute-done | bytes 327712 | tf_op jit(solution)/shard_map/ppermute | solution.py:76
  419.1 19.3 %collective-permute-done.112.refs_2_ = bf16[256,1792]{1,0:T(8,128)(2,1)S(1)} collective-permute-done((bf16[256,1792]{1,0:T(8,128)(2,1)S(1)}, bf16[256,1792]{1,0:T(8,128)(2,1)S(1)}, u32[]{:S(2)}, u32[]{:S(2)}) %collective-permute-start.112) | collective-permute-done | bytes 917536 | tf_op jit(solution)/shard_map/ppermute | solution.py:76
  438.4 19.1 %collective-permute-done.106.refs_1_ = bf16[256,1792]{1,0:T(8,128)(2,1)S(1)} collective-permute-done((bf16[256,1792]{1,0:T(8,128)(2,1)S(1)}, bf16[256,1792]{1,0:T(8,128)(2,1)S(1)}, u32[]{:S(2)}, u32[]{:S(2)}) %collective-permute-start.106) | collective-permute-done | bytes 917536 | tf_op jit(solution)/shard_map/ppermute | solution.py:76
  459.8 20.2 %collective-permute-done.107.refs_2_ = bf16[256,1792]{1,0:T(8,128)(2,1)S(1)} collective-permute-done((bf16[256,1792]{1,0:T(8,128)(2,1)S(1)}, bf16[256,1792]{1,0:T(8,128)(2,1)S(1)}, u32[]{:S(2)}, u32[]{:S(2)}) %collective-permute-start.107) | collective-permute-done | bytes 917536 | tf_op jit(solution)/shard_map/ppermute | solution.py:76
  (293 shorter events, 194.9 us)
Async XLA Ops:
  8.6 39.1 %collective-permute-start.16 = (bf16[256,1792]{1,0:T(8,128)(2,1)S(1)}, bf16[256,1792]{1,0:T(8,128)(2,1)}, u32[]{:S(2)}, u32[]{:S(2)}) collective-permute-start(bf16[256,1792]{1,0:T(8,128)(2,1)S(1)} %get-tuple-element.99.top.refs_2_.refs_13_.refs_5_), channel_id=1, source_target_pairs={{8,0},{12,4},{4,8},{0,12},{24,16},{28,20},{20,24},{16,28},{9,1},{1... | collective-permute-start | bytes 2752520 | tf_op jit(solution)/shard_map/ppermute | solution.py:76
  9.6 40.0 %collective-permute-start.17 = (bf16[256,1792]{1,0:T(8,128)(2,1)S(1)}, bf16[256,1792]{1,0:T(8,128)(2,1)}, u32[]{:S(2)}, u32[]{:S(2)}) collective-permute-start(bf16[256,1792]{1,0:T(8,128)(2,1)S(1)} %get-tuple-element.98.bottom.refs_3_.refs_14_.refs_6_), channel_id=1, source_target_pairs={{16,0},{20,4},{28,8},{24,12},{4,16},{0,20},{8,24},{12,28},{17,1},{... | collective-permute-start | bytes 2752520 | tf_op jit(solution)/shard_map/ppermute | solution.py:76
  28.7 28.2 %collective-permute-start.2 = (bf16[5,64,256]{2,1,0:T(8,128)(2,1)S(1)}, bf16[5,64,256]{2,1,0:T(8,128)(2,1)S(1)}, u32[]{:S(2)}, u32[]{:S(2)}) collective-permute-start(bf16[5,64,256]{2,1,0:T(8,128)(2,1)S(1)} %get-tuple-element.53), channel_id=1, source_target_pairs={{0,1},{1,0},{2,3},{3,2},{4,5},{5,4},{6,7},{7,6},{8,9},{9,8},{10,11... | collective-permute-start | bytes 491528 | tf_op jit(solution)/shard_map/ppermute | solution.py:316
  54.9 25.5 %collective-permute-start.18 = (bf16[7,64,256]{2,1,0:T(8,128)(2,1)S(1)}, bf16[7,64,256]{2,1,0:T(8,128)(2,1)S(1)}, u32[]{:S(2)}, u32[]{:S(2)}) collective-permute-start(bf16[7,64,256]{2,1,0:T(8,128)(2,1)S(1)} %get-tuple-element.61), channel_id=1, source_target_pairs={{0,1},{1,0},{2,3},{3,2},{4,5},{5,4},{6,7},{7,6},{8,9},{9,8},{10,11... | collective-permute-start | bytes 688136 | tf_op jit(solution)/shard_map/ppermute | solution.py:316
  96.9 43.3 %collective-permute-start.42 = (bf16[256,1792]{1,0:T(8,128)(2,1)}, bf16[256,1792]{1,0:T(8,128)(2,1)S(1)}, u32[]{:S(2)}, u32[]{:S(2)}) collective-permute-start(bf16[256,1792]{1,0:T(8,128)(2,1)} %collective-permute-done.8.x_bottom.refs_2_), channel_id=1, source_target_pairs={{0,16},{4,20},{8,28},{12,24},{16,4},{20,0},{24,8},{28,12},{1,17},{... | collective-permute-start | bytes 2752520 | tf_op jit(solution)/shard_map/ppermute | solution.py:76
  98.8 41.9 %collective-permute-start.41 = (bf16[256,1792]{1,0:T(8,128)(2,1)S(1)}, bf16[256,1792]{1,0:T(8,128)(2,1)S(1)}, u32[]{:S(2)}, u32[]{:S(2)}) collective-permute-start(bf16[256,1792]{1,0:T(8,128)(2,1)S(1)} %collective-permute-done.9.y_top.refs_3_), channel_id=1, source_target_pairs={{0,8},{4,12},{8,4},{12,0},{16,24},{20,28},{24,20},{28,16},{1,9},{5... | collective-permute-start | bytes 2752520 | tf_op jit(solution)/shard_map/ppermute | solution.py:76
  175.8 42.3 %collective-permute-start.46 = (bf16[256,1792]{1,0:T(8,128)(2,1)S(1)}, bf16[256,1792]{1,0:T(8,128)(2,1)S(1)}, u32[]{:S(2)}, u32[]{:S(2)}) collective-permute-start(bf16[256,1792]{1,0:T(8,128)(2,1)S(1)} %get-tuple-element.72.refs_3_), channel_id=1, source_target_pairs={{8,0},{12,4},{4,8},{0,12},{24,16},{28,20},{20,24},{16,28},{9,1},{1... | collective-permute-start | bytes 2752520 | tf_op jit(solution)/shard_map/ppermute | solution.py:76
  177.5 41.0 %collective-permute-start.49 = (bf16[256,1792]{1,0:T(8,128)(2,1)S(1)}, bf16[256,1792]{1,0:T(8,128)(2,1)S(1)}, u32[]{:S(2)}, u32[]{:S(2)}) collective-permute-start(bf16[256,1792]{1,0:T(8,128)(2,1)S(1)} %get-tuple-element.73.refs_2_), channel_id=1, source_target_pairs={{16,0},{20,4},{28,8},{24,12},{4,16},{0,20},{8,24},{12,28},{17,1},{... | collective-permute-start | bytes 2752520 | tf_op jit(solution)/shard_map/ppermute | solution.py:76
  177.9 40.6 %collective-permute-start.59 = (bf16[256,1792]{1,0:T(8,128)(2,1)S(1)}, bf16[256,1792]{1,0:T(8,128)(2,1)S(1)}, u32[]{:S(2)}, u32[]{:S(2)}) collective-permute-start(bf16[256,1792]{1,0:T(8,128)(2,1)S(1)} %get-tuple-element.72.refs_3_), channel_id=1, source_target_pairs={{0,4},{4,0},{8,12},{12,8},{16,20},{20,16},{24,28},{28,24},{1,5},{5... | collective-permute-start | bytes 2752520 | tf_op jit(solution)/shard_map/ppermute | solution.py:76
  178.2 41.7 %collective-permute-start.53 = (bf16[256,1792]{1,0:T(8,128)(2,1)S(1)}, bf16[256,1792]{1,0:T(8,128)(2,1)S(1)}, u32[]{:S(2)}, u32[]{:S(2)}) collective-permute-start(bf16[256,1792]{1,0:T(8,128)(2,1)S(1)} %get-tuple-element.72.refs_3_), channel_id=1, source_target_pairs={{16,0},{20,4},{28,8},{24,12},{4,16},{0,20},{8,24},{12,28},{17,1},{... | collective-permute-start | bytes 2752520 | tf_op jit(solution)/shard_map/ppermute | solution.py:76
  218.5 27.7 %collective-permute-start.55 = (bf16[256,1792]{1,0:T(8,128)(2,1)S(1)}, bf16[256,1792]{1,0:T(8,128)(2,1)S(1)}, u32[]{:S(2)}, u32[]{:S(2)}) collective-permute-start(bf16[256,1792]{1,0:T(8,128)(2,1)S(1)} %collective-permute-done.46.refs_1_), channel_id=1, source_target_pairs={{0,4},{4,0},{8,12},{12,8},{16,20},{20,16},{24,28},{28,24},{1,5},{5... | collective-permute-start | bytes 2752520 | tf_op jit(solution)/shard_map/ppermute | solution.py:76
  219.8 26.5 %collective-permute-start.56 = (bf16[256,1792]{1,0:T(8,128)(2,1)S(1)}, bf16[256,1792]{1,0:T(8,128)(2,1)S(1)}, u32[]{:S(2)}, u32[]{:S(2)}) collective-permute-start(bf16[256,1792]{1,0:T(8,128)(2,1)S(1)} %collective-permute-done.49.refs_2_), channel_id=1, source_target_pairs={{0,4},{4,0},{8,12},{12,8},{16,20},{20,16},{24,28},{28,24},{1,5},{5... | collective-permute-start | bytes 2752520 | tf_op jit(solution)/shard_map/ppermute | solution.py:76
  219.8 26.5 %collective-permute-start.57 = (bf16[256,1792]{1,0:T(8,128)(2,1)S(1)}, bf16[256,1792]{1,0:T(8,128)(2,1)S(1)}, u32[]{:S(2)}, u32[]{:S(2)}) collective-permute-start(bf16[256,1792]{1,0:T(8,128)(2,1)S(1)} %collective-permute-done.53.refs_3_), channel_id=1, source_target_pairs={{0,4},{4,0},{8,12},{12,8},{16,20},{20,16},{24,28},{28,24},{1,5},{5... | collective-permute-start | bytes 2752520 | tf_op jit(solution)/shard_map/ppermute | solution.py:76
  255.1 40.5 %collective-permute-start.76 = (bf16[256,1792]{1,0:T(8,128)(2,1)S(1)}, bf16[256,1792]{1,0:T(8,128)(2,1)S(1)}, u32[]{:S(2)}, u32[]{:S(2)}) collective-permute-start(bf16[256,1792]{1,0:T(8,128)(2,1)S(1)} %get-tuple-element.74.top.refs_2_.refs_13_.refs_5_), channel_id=1, source_target_pairs={{8,0},{12,4},{4,8},{0,12},{24,16},{28,20},{20,24},{16,28},{9,1},{1... | collective-permute-start | bytes 2752520 | tf_op jit(solution)/shard_map/ppermute | solution.py:76
  255.5 40.3 %collective-permute-start.77 = (bf16[256,1792]{1,0:T(8,128)(2,1)S(1)}, bf16[256,1792]{1,0:T(8,128)(2,1)S(1)}, u32[]{:S(2)}, u32[]{:S(2)}) collective-permute-start(bf16[256,1792]{1,0:T(8,128)(2,1)S(1)} %get-tuple-element.75.bottom.refs_3_.refs_14_.refs_6_), channel_id=1, source_target_pairs={{16,0},{20,4},{28,8},{24,12},{4,16},{0,20},{8,24},{12,28},{17,1},{... | collective-permute-start | bytes 2752520 | tf_op jit(solution)/shard_map/ppermute | solution.py:76
  339.2 43.6 %collective-permute-start.102 = (bf16[256,1792]{1,0:T(8,128)(2,1)S(1)}, bf16[256,1792]{1,0:T(8,128)(2,1)S(1)}, u32[]{:S(2)}, u32[]{:S(2)}) collective-permute-start(bf16[256,1792]{1,0:T(8,128)(2,1)S(1)} %collective-permute-done.68.x_bottom.refs_2_), channel_id=1, source_target_pairs={{0,16},{4,20},{8,28},{12,24},{16,4},{20,0},{24,8},{28,12},{1,17},{... | collective-permute-start | bytes 2752520 | tf_op jit(solution)/shard_map/ppermute | solution.py:76
  341.6 41.7 %collective-permute-start.101 = (bf16[256,1792]{1,0:T(8,128)(2,1)S(1)}, bf16[256,1792]{1,0:T(8,128)(2,1)S(1)}, u32[]{:S(2)}, u32[]{:S(2)}) collective-permute-start(bf16[256,1792]{1,0:T(8,128)(2,1)S(1)} %collective-permute-done.69.y_top.refs_3_), channel_id=1, source_target_pairs={{0,8},{4,12},{8,4},{12,0},{16,24},{20,28},{24,20},{28,16},{1,9},{5... | collective-permute-start | bytes 2752520 | tf_op jit(solution)/shard_map/ppermute | solution.py:76
  415.2 42.3 %collective-permute-start.106 = (bf16[256,1792]{1,0:T(8,128)(2,1)S(1)}, bf16[256,1792]{1,0:T(8,128)(2,1)S(1)}, u32[]{:S(2)}, u32[]{:S(2)}) collective-permute-start(bf16[256,1792]{1,0:T(8,128)(2,1)S(1)} %get-tuple-element.96.refs_3_), channel_id=1, source_target_pairs={{8,0},{12,4},{4,8},{0,12},{24,16},{28,20},{20,24},{16,28},{9,1},{1... | collective-permute-start | bytes 2752520 | tf_op jit(solution)/shard_map/ppermute | solution.py:76
  417.0 41.0 %collective-permute-start.109 = (bf16[256,1792]{1,0:T(8,128)(2,1)S(1)}, bf16[256,1792]{1,0:T(8,128)(2,1)S(1)}, u32[]{:S(2)}, u32[]{:S(2)}) collective-permute-start(bf16[256,1792]{1,0:T(8,128)(2,1)S(1)} %get-tuple-element.97.refs_2_), channel_id=1, source_target_pairs={{16,0},{20,4},{28,8},{24,12},{4,16},{0,20},{8,24},{12,28},{17,1},{... | collective-permute-start | bytes 2752520 | tf_op jit(solution)/shard_map/ppermute | solution.py:76
  417.4 40.6 %collective-permute-start.119 = (bf16[256,1792]{1,0:T(8,128)(2,1)S(1)}, bf16[256,1792]{1,0:T(8,128)(2,1)S(1)}, u32[]{:S(2)}, u32[]{:S(2)}) collective-permute-start(bf16[256,1792]{1,0:T(8,128)(2,1)S(1)} %get-tuple-element.96.refs_3_), channel_id=1, source_target_pairs={{0,4},{4,0},{8,12},{12,8},{16,20},{20,16},{24,28},{28,24},{1,5},{5... | collective-permute-start | bytes 2752520 | tf_op jit(solution)/shard_map/ppermute | solution.py:76
  417.6 41.7 %collective-permute-start.113 = (bf16[256,1792]{1,0:T(8,128)(2,1)S(1)}, bf16[256,1792]{1,0:T(8,128)(2,1)S(1)}, u32[]{:S(2)}, u32[]{:S(2)}) collective-permute-start(bf16[256,1792]{1,0:T(8,128)(2,1)S(1)} %get-tuple-element.96.refs_3_), channel_id=1, source_target_pairs={{16,0},{20,4},{28,8},{24,12},{4,16},{0,20},{8,24},{12,28},{17,1},{... | collective-permute-start | bytes 2752520 | tf_op jit(solution)/shard_map/ppermute | solution.py:76
  458.0 30.0 %collective-permute-start.115 = (bf16[256,1792]{1,0:T(8,128)(2,1)S(1)}, bf16[256,1792]{1,0:T(8,128)(2,1)S(1)}, u32[]{:S(2)}, u32[]{:S(2)}) collective-permute-start(bf16[256,1792]{1,0:T(8,128)(2,1)S(1)} %collective-permute-done.106.refs_1_), channel_id=1, source_target_pairs={{0,4},{4,0},{8,12},{12,8},{16,20},{20,16},{24,28},{28,24},{1,5},{5... | collective-permute-start | bytes 2752520 | tf_op jit(solution)/shard_map/ppermute | solution.py:76
  459.2 28.8 %collective-permute-start.116 = (bf16[256,1792]{1,0:T(8,128)(2,1)S(1)}, bf16[256,1792]{1,0:T(8,128)(2,1)S(1)}, u32[]{:S(2)}, u32[]{:S(2)}) collective-permute-start(bf16[256,1792]{1,0:T(8,128)(2,1)S(1)} %collective-permute-done.109.refs_2_), channel_id=1, source_target_pairs={{0,4},{4,0},{8,12},{12,8},{16,20},{20,16},{24,28},{28,24},{1,5},{5... | collective-permute-start | bytes 2752520 | tf_op jit(solution)/shard_map/ppermute | solution.py:76
  459.3 28.8 %collective-permute-start.117 = (bf16[256,1792]{1,0:T(8,128)(2,1)S(1)}, bf16[256,1792]{1,0:T(8,128)(2,1)S(1)}, u32[]{:S(2)}, u32[]{:S(2)}) collective-permute-start(bf16[256,1792]{1,0:T(8,128)(2,1)S(1)} %collective-permute-done.113.refs_3_), channel_id=1, source_target_pairs={{0,4},{4,0},{8,12},{12,8},{16,20},{20,16},{24,28},{28,24},{1,5},{5... | collective-permute-start | bytes 2752520 | tf_op jit(solution)/shard_map/ppermute | solution.py:76
  (101 other events, 1620.1 us)

commit v9 on v8

--- a/solution.py
+++ b/solution.py
@@ -213,6 +213,19 @@
     if with_wholes:
         outs += [jax.ShapeDtypeStruct((count - 2, half, half), bf16)] * 2
     return call(near_assemble_kernel, outs, parts, [z])
+
+
+def pack_kernel(*refs):
+    parts, (x_pack, y_pack) = refs[:-2], refs[-2:]
+    rows = parts[0].shape[1]
+    for k, part in enumerate(parts):
+        x_pack[:, k * rows : (k + 1) * rows] = part[:-2]
+        y_pack[:, k * rows : (k + 1) * rows] = part[2:]
+
+
+def pack(parts):
+    count, rows, half = parts[0].shape
+    return call(pack_kernel, [jax.ShapeDtypeStruct((count - 2, len(parts) * rows, half), bf16)] * 2, parts)
 
 
 def mirror_assemble_kernel(z_ref, *refs):
@@ -401,8 +414,7 @@
     for shifts in ((0,), (1, 2), (3,)):
         x_part, y_part = late_parts[shifts[0]][:-2], late_parts[shifts[0]][2:]
         if len(shifts) > 1:
-            x_part = jnp.concatenate([late_parts[k][:-2] for k in shifts], axis=1)
-            y_part = jnp.concatenate([late_parts[k][2:] for k in shifts], axis=1)
+            x_part, y_part = pack([late_parts[k] for k in shifts])
         late += [over_dp(x_part, GIVE_X), over_dp(y_part, GIVE_Y)]
     own, beside = own_assemble(z, own_parts)
     beside = beside_of(side_index, beside, over_dp(beside, CORE))

time: 497 us -> 515 us (1.036)
  starting transfers between devices: 85.7 us -> 95.1 us
  waiting for transfers between devices: 334 us -> 343 us
    ppermute x82, starting transfers between devices: 43.5 us -> 53.8 us  [over_dp(): return lax.ppermute(value, 'dp', pairs)]
    ppermute x82, waiting for transfers between devices: 238 us -> 248 us  [over_dp(): return lax.ppermute(value, 'dp', pairs)]
    pallas_call x48 -> x50, Pallas kernels: 66.9 us -> 66.8 us  [call(): pl.pallas_call(kernel, out_shape=outs, in_specs=[pl.BlockSpec(memory_spac...]
  transfers between devices with their start and end apart: 120 -> 120, of which waited for: 48 -> 57; matrix products, arithmetic and copies ran while one was open for 1% -> 0% of each run, Pallas kernels for 11% -> 11%
where the time goes in v9:
time: 515 us; the launch traced here: 514 us
  waiting for transfers between devices  343 us (67%)
  starting transfers between devices  95.1 us (18%)
  Pallas kernels  66.8 us (13%)
  other arithmetic  5.55 us (1%)
    ppermute x82, waiting for transfers between devices, over_dp(): return lax.ppermute(value, 'dp', pairs)  248 us
    ppermute x38, waiting for transfers between devices, exchanged(): lax.ppermute(value, 'shard', [(z, z ^ distance) for z in range(COLUMN_DEV...  95 us
    pallas_call x50, Pallas kernels, call(): pl.pallas_call(kernel, out_shape=outs, in_specs=[pl.BlockSpec(memory_spac...  66.8 us
    ppermute x82, starting transfers between devices, over_dp(): return lax.ppermute(value, 'dp', pairs)  53.8 us
    ppermute x38, starting transfers between devices, exchanged(): lax.ppermute(value, 'shard', [(z, z ^ distance) for z in range(COLUMN_DEV...  41.3 us
  transfers between devices with their start and end apart: 120, of which 57 were waited for; matrix products, arithmetic and copies ran while one was open for 0% of the time, Pallas kernels for 11%

profile of v9, /device:TPU:0, one launch (start us, length us, event | category | flops | bytes accessed | tf_op | source)
XLA Modules:
  0.0 514.2 jit_solution(2116101670175801841)
XLA Ops:
  15.8 12.9 %collective-permute-done.8.x_bottom.refs_2_ = bf16[256,1792]{1,0:T(8,128)(2,1)} collective-permute-done((bf16[256,1792]{1,0:T(8,128)(2,1)S(1)}, bf16[256,1792]{1,0:T(8,128)(2,1)}, u32[]{:S(2)}, u32[]{:S(2)}) %collective-permute-start.8) | collective-permute-done | bytes 917536 | tf_op jit(solution)/shard_map/ppermute | solution.py:76
  34.6 13.1 %collective-permute-done.16.x_top.refs_4_ = bf16[256,1792]{1,0:T(8,128)(2,1)} collective-permute-done((bf16[256,1792]{1,0:T(8,128)(2,1)S(1)}, bf16[256,1792]{1,0:T(8,128)(2,1)}, u32[]{:S(2)}, u32[]{:S(2)}) %collective-permute-start.16) | collective-permute-done | bytes 917536 | tf_op jit(solution)/shard_map/ppermute | solution.py:76
  60.0 8.8 %collective-permute-done.19.refs_0_ = bf16[7,64,256]{2,1,0:T(8,128)(2,1)S(1)} collective-permute-done((bf16[7,64,256]{2,1,0:T(8,128)(2,1)S(1)}, bf16[7,64,256]{2,1,0:T(8,128)(2,1)S(1)}, u32[]{:S(2)}, u32[]{:S(2)}) %collective-permute-start.19) | collective-permute-done | bytes 229408 | tf_op jit(solution)/shard_map/ppermute | solution.py:329
  86.3 7.3 %collective-permute-done.20.refs_1_ = bf16[7,64,256]{2,1,0:T(8,128)(2,1)S(1)} collective-permute-done((bf16[7,64,256]{2,1,0:T(8,128)(2,1)S(1)}, bf16[7,64,256]{2,1,0:T(8,128)(2,1)S(1)}, u32[]{:S(2)}, u32[]{:S(2)}) %collective-permute-start.20) | collective-permute-done | bytes 229408 | tf_op jit(solution)/shard_map/ppermute | solution.py:329
  107.9 9.1 %collective-permute-done.22.refs_10_.refs_1_.refs_2_ = bf16[7,64,256]{2,1,0:T(8,128)(2,1)S(1)} collective-permute-done((bf16[7,64,256]{2,1,0:T(8,128)(2,1)S(1)}, bf16[7,64,256]{2,1,0:T(8,128)(2,1)S(1)}, u32[]{:S(2)}, u32[]{:S(2)}) %collective-permute-start.22) | collective-permute-done | bytes 229408 | tf_op jit(solution)/shard_map/ppermute | solution.py:329
  121.8 6.5 %collective-permute-done.30.refs_2_ = bf16[5,64,256]{2,1,0:T(8,128)(2,1)S(1)} collective-permute-done((bf16[5,64,256]{2,1,0:T(8,128)(2,1)S(1)}, bf16[5,64,256]{2,1,0:T(8,128)(2,1)S(1)}, u32[]{:S(2)}, u32[]{:S(2)}) %collective-permute-start.30) | collective-permute-done | bytes 163872 | tf_op jit(solution)/shard_map/ppermute | solution.py:76
  153.6 13.4 %collective-permute-done.33.refs_5_ = bf16[5,128,256]{2,1,0:T(8,128)(2,1)S(1)} collective-permute-done((bf16[5,128,256]{2,1,0:T(8,128)(2,1)S(1)}, bf16[5,128,256]{2,1,0:T(8,128)(2,1)S(1)}, u32[]{:S(2)}, u32[]{:S(2)}) %collective-permute-start.33) | collective-permute-done | bytes 327712 | tf_op jit(solution)/shard_map/ppermute | solution.py:76
  170.0 4.3 shard_map.58.refs_6_
  174.3 4.8 shard_map.59.refs_12_
  188.1 19.7 %collective-permute-done.52.refs_2_ = bf16[256,1792]{1,0:T(8,128)(2,1)S(1)} collective-permute-done((bf16[256,1792]{1,0:T(8,128)(2,1)S(1)}, bf16[256,1792]{1,0:T(8,128)(2,1)S(1)}, u32[]{:S(2)}, u32[]{:S(2)}) %collective-permute-start.52) | collective-permute-done | bytes 917536 | tf_op jit(solution)/shard_map/ppermute | solution.py:76
  207.7 18.8 %collective-permute-done.46.refs_1_ = bf16[256,1792]{1,0:T(8,128)(2,1)S(1)} collective-permute-done((bf16[256,1792]{1,0:T(8,128)(2,1)S(1)}, bf16[256,1792]{1,0:T(8,128)(2,1)S(1)}, u32[]{:S(2)}, u32[]{:S(2)}) %collective-permute-start.46) | collective-permute-done | bytes 917536 | tf_op jit(solution)/shard_map/ppermute | solution.py:76
  229.1 19.4 %collective-permute-done.47.refs_2_ = bf16[256,1792]{1,0:T(8,128)(2,1)S(1)} collective-permute-done((bf16[256,1792]{1,0:T(8,128)(2,1)S(1)}, bf16[256,1792]{1,0:T(8,128)(2,1)S(1)}, u32[]{:S(2)}, u32[]{:S(2)}) %collective-permute-start.47) | collective-permute-done | bytes 917536 | tf_op jit(solution)/shard_map/ppermute | solution.py:76
  268.5 16.4 %collective-permute-done.68.x_bottom.refs_2_ = bf16[256,1792]{1,0:T(8,128)(2,1)S(1)} collective-permute-done((bf16[256,1792]{1,0:T(8,128)(2,1)S(1)}, bf16[256,1792]{1,0:T(8,128)(2,1)S(1)}, u32[]{:S(2)}, u32[]{:S(2)}) %collective-permute-start.68) | collective-permute-done | bytes 917536 | tf_op jit(solution)/shard_map/ppermute | solution.py:76
  288.7 15.2 %collective-permute-done.76.x_top.refs_4_ = bf16[256,1792]{1,0:T(8,128)(2,1)S(1)} collective-permute-done((bf16[256,1792]{1,0:T(8,128)(2,1)S(1)}, bf16[256,1792]{1,0:T(8,128)(2,1)S(1)}, u32[]{:S(2)}, u32[]{:S(2)}) %collective-permute-start.76) | collective-permute-done | bytes 917536 | tf_op jit(solution)/shard_map/ppermute | solution.py:76
  313.5 9.6 %collective-permute-done.79.refs_0_ = bf16[7,64,256]{2,1,0:T(8,128)(2,1)S(1)} collective-permute-done((bf16[7,64,256]{2,1,0:T(8,128)(2,1)S(1)}, bf16[7,64,256]{2,1,0:T(8,128)(2,1)S(1)}, u32[]{:S(2)}, u32[]{:S(2)}) %collective-permute-start.79) | collective-permute-done | bytes 229408 | tf_op jit(solution)/shard_map/ppermute | solution.py:329
  329.6 5.2 %collective-permute-done.70.refs_0_ = bf16[5,64,256]{2,1,0:T(8,128)(2,1)S(1)} collective-permute-done((bf16[5,64,256]{2,1,0:T(8,128)(2,1)S(1)}, bf16[5,64,256]{2,1,0:T(8,128)(2,1)S(1)}, u32[]{:S(2)}, u32[]{:S(2)}) %collective-permute-start.70) | collective-permute-done | bytes 163872 | tf_op jit(solution)/shard_map/ppermute | solution.py:329
  335.0 4.9 collective-permute-done.78.refs_0_
  339.9 8.0 %collective-permute-done.80.refs_1_ = bf16[7,64,256]{2,1,0:T(8,128)(2,1)S(1)} collective-permute-done((bf16[7,64,256]{2,1,0:T(8,128)(2,1)S(1)}, bf16[7,64,256]{2,1,0:T(8,128)(2,1)S(1)}, u32[]{:S(2)}, u32[]{:S(2)}) %collective-permute-start.80) | collective-permute-done | bytes 229408 | tf_op jit(solution)/shard_map/ppermute | solution.py:329
  361.0 8.3 %collective-permute-done.82.refs_10_.refs_1_.refs_2_ = bf16[7,64,256]{2,1,0:T(8,128)(2,1)S(1)} collective-permute-done((bf16[7,64,256]{2,1,0:T(8,128)(2,1)S(1)}, bf16[7,64,256]{2,1,0:T(8,128)(2,1)S(1)}, u32[]{:S(2)}, u32[]{:S(2)}) %collective-permute-start.82) | collective-permute-done | bytes 229408 | tf_op jit(solution)/shard_map/ppermute | solution.py:329
  372.3 7.4 %collective-permute-done.90.refs_2_ = bf16[5,64,256]{2,1,0:T(8,128)(2,1)S(1)} collective-permute-done((bf16[5,64,256]{2,1,0:T(8,128)(2,1)S(1)}, bf16[5,64,256]{2,1,0:T(8,128)(2,1)S(1)}, u32[]{:S(2)}, u32[]{:S(2)}) %collective-permute-start.90) | collective-permute-done | bytes 163872 | tf_op jit(solution)/shard_map/ppermute | solution.py:76
  405.9 13.0 %collective-permute-done.93.refs_5_ = bf16[5,128,256]{2,1,0:T(8,128)(2,1)S(1)} collective-permute-done((bf16[5,128,256]{2,1,0:T(8,128)(2,1)S(1)}, bf16[5,128,256]{2,1,0:T(8,128)(2,1)S(1)}, u32[]{:S(2)}, u32[]{:S(2)}) %collective-permute-start.93) | collective-permute-done | bytes 327712 | tf_op jit(solution)/shard_map/ppermute | solution.py:76
  437.2 19.7 %collective-permute-done.112.refs_2_ = bf16[256,1792]{1,0:T(8,128)(2,1)S(1)} collective-permute-done((bf16[256,1792]{1,0:T(8,128)(2,1)S(1)}, bf16[256,1792]{1,0:T(8,128)(2,1)S(1)}, u32[]{:S(2)}, u32[]{:S(2)}) %collective-permute-start.112) | collective-permute-done | bytes 917536 | tf_op jit(solution)/shard_map/ppermute | solution.py:76
  456.9 18.8 %collective-permute-done.106.refs_1_ = bf16[256,1792]{1,0:T(8,128)(2,1)S(1)} collective-permute-done((bf16[256,1792]{1,0:T(8,128)(2,1)S(1)}, bf16[256,1792]{1,0:T(8,128)(2,1)S(1)}, u32[]{:S(2)}, u32[]{:S(2)}) %collective-permute-start.106) | collective-permute-done | bytes 917536 | tf_op jit(solution)/shard_map/ppermute | solution.py:76
  478.2 19.4 %collective-permute-done.107.refs_2_ = bf16[256,1792]{1,0:T(8,128)(2,1)S(1)} collective-permute-done((bf16[256,1792]{1,0:T(8,128)(2,1)S(1)}, bf16[256,1792]{1,0:T(8,128)(2,1)S(1)}, u32[]{:S(2)}, u32[]{:S(2)}) %collective-permute-start.107) | collective-permute-done | bytes 917536 | tf_op jit(solution)/shard_map/ppermute | solution.py:76
  (287 shorter events, 228.8 us)
Async XLA Ops:
  8.6 39.1 %collective-permute-start.16 = (bf16[256,1792]{1,0:T(8,128)(2,1)S(1)}, bf16[256,1792]{1,0:T(8,128)(2,1)}, u32[]{:S(2)}, u32[]{:S(2)}) collective-permute-start(bf16[256,1792]{1,0:T(8,128)(2,1)S(1)} %get-tuple-element.107.top.refs_2_.refs_13_.refs_5_), channel_id=1, source_target_pairs={{8,0},{12,4},{4,8},{0,12},{24,16},{28,20},{20,24},{16,28},{9,1},{1... | collective-permute-start | bytes 2752520 | tf_op jit(solution)/shard_map/ppermute | solution.py:76
  9.6 40.0 %collective-permute-start.17 = (bf16[256,1792]{1,0:T(8,128)(2,1)S(1)}, bf16[256,1792]{1,0:T(8,128)(2,1)}, u32[]{:S(2)}, u32[]{:S(2)}) collective-permute-start(bf16[256,1792]{1,0:T(8,128)(2,1)S(1)} %get-tuple-element.106.bottom.refs_3_.refs_14_.refs_6_), channel_id=1, source_target_pairs={{16,0},{20,4},{28,8},{24,12},{4,16},{0,20},{8,24},{12,28},{17,1},{... | collective-permute-start | bytes 2752520 | tf_op jit(solution)/shard_map/ppermute | solution.py:76
  14.1 41.2 %collective-permute-start.3 = (bf16[5,64,256]{2,1,0:T(8,128)(2,1)S(1)}, bf16[5,64,256]{2,1,0:T(8,128)(2,1)S(1)}, u32[]{:S(2)}, u32[]{:S(2)}) collective-permute-start(bf16[5,64,256]{2,1,0:T(8,128)(2,1)S(1)} %get-tuple-element.59), channel_id=1, source_target_pairs={{0,1},{1,0},{2,3},{3,2},{4,5},{5,4},{6,7},{7,6},{8,9},{9,8},{10,11... | collective-permute-start | bytes 491528 | tf_op jit(solution)/shard_map/ppermute | solution.py:329
  33.0 26.6 %collective-permute-start.11 = (bf16[5,64,256]{2,1,0:T(8,128)(2,1)S(1)}, bf16[5,64,256]{2,1,0:T(8,128)(2,1)S(1)}, u32[]{:S(2)}, u32[]{:S(2)}) collective-permute-start(bf16[5,64,256]{2,1,0:T(8,128)(2,1)S(1)} %get-tuple-element.63), channel_id=1, source_target_pairs={{0,1},{1,0},{2,3},{3,2},{4,5},{5,4},{6,7},{7,6},{8,9},{9,8},{10,11... | collective-permute-start | bytes 491528 | tf_op jit(solution)/shard_map/ppermute | solution.py:329
  101.9 46.7 %collective-permute-start.42 = (bf16[256,1792]{1,0:T(8,128)(2,1)}, bf16[256,1792]{1,0:T(8,128)(2,1)S(1)}, u32[]{:S(2)}, u32[]{:S(2)}) collective-permute-start(bf16[256,1792]{1,0:T(8,128)(2,1)} %collective-permute-done.8.x_bottom.refs_2_), channel_id=1, source_target_pairs={{0,16},{4,20},{8,28},{12,24},{16,4},{20,0},{24,8},{28,12},{1,17},{... | collective-permute-start | bytes 2752520 | tf_op jit(solution)/shard_map/ppermute | solution.py:76
  102.8 46.4 %collective-permute-start.41 = (bf16[256,1792]{1,0:T(8,128)(2,1)S(1)}, bf16[256,1792]{1,0:T(8,128)(2,1)S(1)}, u32[]{:S(2)}, u32[]{:S(2)}) collective-permute-start(bf16[256,1792]{1,0:T(8,128)(2,1)S(1)} %collective-permute-done.9.y_top.refs_3_), channel_id=1, source_target_pairs={{0,8},{4,12},{8,4},{12,0},{16,24},{20,28},{24,20},{28,16},{1,9},{5... | collective-permute-start | bytes 2752520 | tf_op jit(solution)/shard_map/ppermute | solution.py:76
  102.8 46.5 %collective-permute-start.38 = (bf16[256,1792]{1,0:T(8,128)(2,1)}, bf16[256,1792]{1,0:T(8,128)(2,1)S(1)}, u32[]{:S(2)}, u32[]{:S(2)}) collective-permute-start(bf16[256,1792]{1,0:T(8,128)(2,1)} %collective-permute-done.8.x_bottom.refs_2_), channel_id=1, source_target_pairs={{0,4},{4,0},{8,12},{12,8},{16,20},{20,16},{24,28},{28,24},{1,5},{5... | collective-permute-start | bytes 2752520 | tf_op jit(solution)/shard_map/ppermute | solution.py:76
  185.6 40.9 %collective-permute-start.46 = (bf16[256,1792]{1,0:T(8,128)(2,1)S(1)}, bf16[256,1792]{1,0:T(8,128)(2,1)S(1)}, u32[]{:S(2)}, u32[]{:S(2)}) collective-permute-start(bf16[256,1792]{1,0:T(8,128)(2,1)S(1)} %get-tuple-element.78.refs_3_), channel_id=1, source_target_pairs={{8,0},{12,4},{4,8},{0,12},{24,16},{28,20},{20,24},{16,28},{9,1},{1... | collective-permute-start | bytes 2752520 | tf_op jit(solution)/shard_map/ppermute | solution.py:76
  185.9 40.6 %collective-permute-start.49 = (bf16[256,1792]{1,0:T(8,128)(2,1)S(1)}, bf16[256,1792]{1,0:T(8,128)(2,1)S(1)}, u32[]{:S(2)}, u32[]{:S(2)}) collective-permute-start(bf16[256,1792]{1,0:T(8,128)(2,1)S(1)} %get-tuple-element.79.refs_2_), channel_id=1, source_target_pairs={{16,0},{20,4},{28,8},{24,12},{4,16},{0,20},{8,24},{12,28},{17,1},{... | collective-permute-start | bytes 2752520 | tf_op jit(solution)/shard_map/ppermute | solution.py:76
  185.9 42.0 %collective-permute-start.59 = (bf16[256,1792]{1,0:T(8,128)(2,1)S(1)}, bf16[256,1792]{1,0:T(8,128)(2,1)S(1)}, u32[]{:S(2)}, u32[]{:S(2)}) collective-permute-start(bf16[256,1792]{1,0:T(8,128)(2,1)S(1)} %get-tuple-element.78.refs_3_), channel_id=1, source_target_pairs={{0,4},{4,0},{8,12},{12,8},{16,20},{20,16},{24,28},{28,24},{1,5},{5... | collective-permute-start | bytes 2752520 | tf_op jit(solution)/shard_map/ppermute | solution.py:76
  186.7 41.9 %collective-permute-start.53 = (bf16[256,1792]{1,0:T(8,128)(2,1)S(1)}, bf16[256,1792]{1,0:T(8,128)(2,1)S(1)}, u32[]{:S(2)}, u32[]{:S(2)}) collective-permute-start(bf16[256,1792]{1,0:T(8,128)(2,1)S(1)} %get-tuple-element.78.refs_3_), channel_id=1, source_target_pairs={{16,0},{20,4},{28,8},{24,12},{4,16},{0,20},{8,24},{12,28},{17,1},{... | collective-permute-start | bytes 2752520 | tf_op jit(solution)/shard_map/ppermute | solution.py:76
  264.5 39.4 %collective-permute-start.76 = (bf16[256,1792]{1,0:T(8,128)(2,1)S(1)}, bf16[256,1792]{1,0:T(8,128)(2,1)S(1)}, u32[]{:S(2)}, u32[]{:S(2)}) collective-permute-start(bf16[256,1792]{1,0:T(8,128)(2,1)S(1)} %get-tuple-element.80.top.refs_2_.refs_13_.refs_5_), channel_id=1, source_target_pairs={{8,0},{12,4},{4,8},{0,12},{24,16},{28,20},{20,24},{16,28},{9,1},{1... | collective-permute-start | bytes 2752520 | tf_op jit(solution)/shard_map/ppermute | solution.py:76
  264.6 40.9 %collective-permute-start.77 = (bf16[256,1792]{1,0:T(8,128)(2,1)S(1)}, bf16[256,1792]{1,0:T(8,128)(2,1)S(1)}, u32[]{:S(2)}, u32[]{:S(2)}) collective-permute-start(bf16[256,1792]{1,0:T(8,128)(2,1)S(1)} %get-tuple-element.81.bottom.refs_3_.refs_14_.refs_6_), channel_id=1, source_target_pairs={{16,0},{20,4},{28,8},{24,12},{4,16},{0,20},{8,24},{12,28},{17,1},{... | collective-permute-start | bytes 2752520 | tf_op jit(solution)/shard_map/ppermute | solution.py:76
  267.0 42.6 %collective-permute-start.63 = (bf16[5,64,256]{2,1,0:T(8,128)(2,1)S(1)}, bf16[5,64,256]{2,1,0:T(8,128)(2,1)S(1)}, u32[]{:S(2)}, u32[]{:S(2)}) collective-permute-start(bf16[5,64,256]{2,1,0:T(8,128)(2,1)S(1)} %get-tuple-element.85), channel_id=1, source_target_pairs={{0,1},{1,0},{2,3},{3,2},{4,5},{5,4},{6,7},{7,6},{8,9},{9,8},{10,11... | collective-permute-start | bytes 491528 | tf_op jit(solution)/shard_map/ppermute | solution.py:329
  354.1 46.3 %collective-permute-start.102 = (bf16[256,1792]{1,0:T(8,128)(2,1)S(1)}, bf16[256,1792]{1,0:T(8,128)(2,1)S(1)}, u32[]{:S(2)}, u32[]{:S(2)}) collective-permute-start(bf16[256,1792]{1,0:T(8,128)(2,1)S(1)} %collective-permute-done.68.x_bottom.refs_2_), channel_id=1, source_target_pairs={{0,16},{4,20},{8,28},{12,24},{16,4},{20,0},{24,8},{28,12},{1,17},{... | collective-permute-start | bytes 2752520 | tf_op jit(solution)/shard_map/ppermute | solution.py:76
  355.2 46.2 %collective-permute-start.101 = (bf16[256,1792]{1,0:T(8,128)(2,1)S(1)}, bf16[256,1792]{1,0:T(8,128)(2,1)S(1)}, u32[]{:S(2)}, u32[]{:S(2)}) collective-permute-start(bf16[256,1792]{1,0:T(8,128)(2,1)S(1)} %collective-permute-done.69.y_top.refs_3_), channel_id=1, source_target_pairs={{0,8},{4,12},{8,4},{12,0},{16,24},{20,28},{24,20},{28,16},{1,9},{5... | collective-permute-start | bytes 2752520 | tf_op jit(solution)/shard_map/ppermute | solution.py:76
  355.2 46.2 %collective-permute-start.100 = (bf16[256,1792]{1,0:T(8,128)(2,1)S(1)}, bf16[256,1792]{1,0:T(8,128)(2,1)S(1)}, u32[]{:S(2)}, u32[]{:S(2)}) collective-permute-start(bf16[256,1792]{1,0:T(8,128)(2,1)S(1)} %collective-permute-done.77.y_bottom.refs_5_), channel_id=1, source_target_pairs={{0,4},{4,0},{8,12},{12,8},{16,20},{20,16},{24,28},{28,24},{1,5},{5... | collective-permute-start | bytes 2752520 | tf_op jit(solution)/shard_map/ppermute | solution.py:76
  434.0 41.7 %collective-permute-start.106 = (bf16[256,1792]{1,0:T(8,128)(2,1)S(1)}, bf16[256,1792]{1,0:T(8,128)(2,1)S(1)}, u32[]{:S(2)}, u32[]{:S(2)}) collective-permute-start(bf16[256,1792]{1,0:T(8,128)(2,1)S(1)} %get-tuple-element.104.refs_3_), channel_id=1, source_target_pairs={{8,0},{12,4},{4,8},{0,12},{24,16},{28,20},{20,24},{16,28},{9,1},{1... | collective-permute-start | bytes 2752520 | tf_op jit(solution)/shard_map/ppermute | solution.py:76
  435.1 40.6 %collective-permute-start.109 = (bf16[256,1792]{1,0:T(8,128)(2,1)S(1)}, bf16[256,1792]{1,0:T(8,128)(2,1)S(1)}, u32[]{:S(2)}, u32[]{:S(2)}) collective-permute-start(bf16[256,1792]{1,0:T(8,128)(2,1)S(1)} %get-tuple-element.105.refs_2_), channel_id=1, source_target_pairs={{16,0},{20,4},{28,8},{24,12},{4,16},{0,20},{8,24},{12,28},{17,1},{... | collective-permute-start | bytes 2752520 | tf_op jit(solution)/shard_map/ppermute | solution.py:76
  435.1 41.4 %collective-permute-start.119 = (bf16[256,1792]{1,0:T(8,128)(2,1)S(1)}, bf16[256,1792]{1,0:T(8,128)(2,1)S(1)}, u32[]{:S(2)}, u32[]{:S(2)}) collective-permute-start(bf16[256,1792]{1,0:T(8,128)(2,1)S(1)} %get-tuple-element.104.refs_3_), channel_id=1, source_target_pairs={{0,4},{4,0},{8,12},{12,8},{16,20},{20,16},{24,28},{28,24},{1,5},{5... | collective-permute-start | bytes 2752520 | tf_op jit(solution)/shard_map/ppermute | solution.py:76
  435.8 41.9 %collective-permute-start.113 = (bf16[256,1792]{1,0:T(8,128)(2,1)S(1)}, bf16[256,1792]{1,0:T(8,128)(2,1)S(1)}, u32[]{:S(2)}, u32[]{:S(2)}) collective-permute-start(bf16[256,1792]{1,0:T(8,128)(2,1)S(1)} %get-tuple-element.104.refs_3_), channel_id=1, source_target_pairs={{16,0},{20,4},{28,8},{24,12},{4,16},{0,20},{8,24},{12,28},{17,1},{... | collective-permute-start | bytes 2752520 | tf_op jit(solution)/shard_map/ppermute | solution.py:76
  476.5 29.2 %collective-permute-start.115 = (bf16[256,1792]{1,0:T(8,128)(2,1)S(1)}, bf16[256,1792]{1,0:T(8,128)(2,1)S(1)}, u32[]{:S(2)}, u32[]{:S(2)}) collective-permute-start(bf16[256,1792]{1,0:T(8,128)(2,1)S(1)} %collective-permute-done.106.refs_1_), channel_id=1, source_target_pairs={{0,4},{4,0},{8,12},{12,8},{16,20},{20,16},{24,28},{28,24},{1,5},{5... | collective-permute-start | bytes 2752520 | tf_op jit(solution)/shard_map/ppermute | solution.py:76
  477.7 28.0 %collective-permute-start.116 = (bf16[256,1792]{1,0:T(8,128)(2,1)S(1)}, bf16[256,1792]{1,0:T(8,128)(2,1)S(1)}, u32[]{:S(2)}, u32[]{:S(2)}) collective-permute-start(bf16[256,1792]{1,0:T(8,128)(2,1)S(1)} %collective-permute-done.109.refs_2_), channel_id=1, source_target_pairs={{0,4},{4,0},{8,12},{12,8},{16,20},{20,16},{24,28},{28,24},{1,5},{5... | collective-permute-start | bytes 2752520 | tf_op jit(solution)/shard_map/ppermute | solution.py:76
  477.7 28.0 %collective-permute-start.117 = (bf16[256,1792]{1,0:T(8,128)(2,1)S(1)}, bf16[256,1792]{1,0:T(8,128)(2,1)S(1)}, u32[]{:S(2)}, u32[]{:S(2)}) collective-permute-start(bf16[256,1792]{1,0:T(8,128)(2,1)S(1)} %collective-permute-done.113.refs_3_), channel_id=1, source_target_pairs={{0,4},{4,0},{8,12},{12,8},{16,20},{20,16},{24,28},{28,24},{1,5},{5... | collective-permute-start | bytes 2752520 | tf_op jit(solution)/shard_map/ppermute | solution.py:76
  (101 other events, 1592.2 us)
